TPU v7x, 32 devices: a whole 2x2x4 slice. The times are simulated.
32 devices in a mesh: rows: 8 (over z, x), feat: 4 (over y, core).
Axes of the slice: x: 2, y: 2, z: 4, core: 2. Of those that a mesh axis runs over, the one named last changes fastest.
Arguments:
- pixels: bfloat16 [12288, 1024], P(('rows', 'feat')), may hold values from -6 to 6
- qkv_weight: bfloat16 [3, 1024, 1024], P(None, None, 'feat'), may hold values from -0.1875 to 0.1875
- out_weight: bfloat16 [1024, 1024], P('feat'), may hold values from -1.5 to 1.5
- up_weight: bfloat16 [1024, 4096], P(None, 'feat'), as said below
- down_weight: bfloat16 [4096, 1024], P('feat'), may hold values from -0.09375 to 0.09375
- norm1_gain: float32 [1024], replicated, may hold values from 0.5 to 1.5
- norm1_bias: float32 [1024], replicated, may hold values from -3 to 3
- norm2_gain: float32 [1024], replicated, may hold values from 0.5 to 1.5
- norm2_bias: float32 [1024], replicated, may hold values from -3 to 3
- crop_lengths: int32 [32], replicated, may hold values from 0 to 3072, as said below
- crop_offsets: int32 [32], replicated, may hold values from 0 to 12288, as said below
- pixel_mask: int32 [12288], P('rows'), may hold values 0 or 1
- out_grad: bfloat16 [12288, 1024], P(('rows', 'feat')), may hold values from -6 to 6
Outputs:
- output: bfloat16 [12288, 1024], P(('rows', 'feat'))
- pixels_grad: bfloat16 [12288, 1024], P(('rows', 'feat'))
- qkv_weight_grad: float32 [3, 1024, 1024], P(None, None, 'feat')
- out_weight_grad: float32 [1024, 1024], P('feat')
- up_weight_grad: float32 [1024, 4096], P(None, 'feat')
- down_weight_grad: float32 [4096, 1024], P('feat')
- norm1_gain_grad: float32 [1024], replicated
- norm1_bias_grad: float32 [1024], replicated
- norm2_gain_grad: float32 [1024], replicated
- norm2_bias_grad: float32 [1024], replicated
- crop_rms: float32 [3, 32], replicated
Inputs may be any that keep to these rules, and one draw needn't show every extreme that they name: Crops lie in order and do not intersection: crop c covers pixels crop_offsets[c] to crop_offsets[c] + crop_lengths[c] - 1. Crop 0 starts at pixel 0 and has exactly 3072 pixels. Crops that would pass the end are cut short; those starting at or past the end have length 0. `crop_offsets`: Non-decreasing; a crop of length 0 at the end has offset 12288. `up_weight`: entries of order 1024 ** -0.5.
All inputs are finite; a program needn't handle non-finite values. No bound on the sum of `pixel_mask` on one device may be relied on, other than what follows from the above.
Results may differ from a plain program's by a relative error of at most 0.02.
Values may be sent and summed in bfloat16 or wider, within the bound.
No kernel may reach another device: no remote copies, remote signals or barrier semaphores. Data moves between devices by JAX's collectives and lax.ppermute only.
A program may use at most 192 MiB of HBM per device.

v0:
```python
import jax
import jax.numpy as jnp
from jax import lax
from jax.sharding import PartitionSpec as P

D = 1024
HEAD = 64
BLOCK = 512


precise = lax.Precision.HIGHEST


def prefix(shard, axis, combine, identity, reverse):
    peers, here = (lax.axis_size(axis), lax.axis_index(axis))
    everything = jax.tree.map(
        lambda part, kind: lax.all_gather(part.astype(kind), axis),
        shard,
        (jnp.bfloat16, jnp.bfloat16, jnp.bfloat16),
    )
    start = jax.tree.map(
        lambda part, zero: jnp.broadcast_to(jnp.asarray(zero, part.dtype), part.shape),
        shard,
        identity,
    )

    def hop(k, before):
        at = peers - 1 - k if reverse else k
        reached = at > here if reverse else at < here
        new = combine(
            before, jax.tree.map(lambda part, own: part[at].astype(own.dtype), everything, shard)
        )
        return jax.tree.map(lambda a, b: jnp.where(reached, a, b), new, before)

    return lax.fori_loop(0, peers, hop, start)


def layer_norm(values, norm_gain, norm_bias):
    centre = jnp.mean(values, axis=-1, keepdims=True)
    shifted = values - centre
    spread = jnp.mean(shifted * shifted, axis=-1, keepdims=True)
    return shifted * lax.rsqrt(spread + 1e-05) * norm_gain + norm_bias


def feature(values):
    return jax.nn.elu(values) + 1.0


def feature_slope(values):
    return jnp.where(values > 0, 1.0, jnp.exp(jnp.minimum(values, 0.0)))


def gelu_tanh(values):
    return jax.nn.gelu(values, approximate=True)


def to_blocks(array, block_count):
    return array.reshape((block_count, BLOCK) + array.shape[1:])


def chain_join(earlier, later):
    state_early, sum_early, flag_early = earlier
    state_late, sum_late, flag_late = later
    carry_on = 1.0 - flag_late
    return (
        state_late + carry_on * state_early,
        sum_late + carry_on * sum_early,
        jnp.maximum(flag_early, flag_late),
    )


def causal_mask():
    return jnp.arange(BLOCK)[:, None] >= jnp.arange(BLOCK)[None, :]


def advance(running, inputs):
    carry_state, carry_sum, last_crop = running
    block_q, block_k, block_v, block_seg = inputs
    same_crop = causal_mask() & (block_seg[:, None] == block_seg[None, :])
    scores = jnp.einsum("ihd,jhd->hij", block_q, block_k, preferred_element_type=jnp.float32)
    scores_low = jnp.where(same_crop[None], scores, 0.0).astype(jnp.bfloat16)
    carried = (block_seg == last_crop).astype(jnp.float32)
    query_wide = block_q.astype(jnp.float32)
    numerator = jnp.einsum("hij,jhe->ihe", scores_low, block_v, preferred_element_type=jnp.float32)
    numerator = numerator + carried[:, None, None] * jnp.einsum(
        "ihd,hde->ihe", query_wide, carry_state, precision=precise
    )
    denominator = jnp.sum(scores_low.astype(jnp.float32), axis=2).T
    denominator = denominator + carried[:, None] * jnp.einsum(
        "ihd,hd->ih", query_wide, carry_sum, precision=precise
    )
    tail_crop = block_seg[-1]
    tail_rows = block_seg == tail_crop
    continues = (tail_crop == last_crop).astype(jnp.float32)
    kept_keys = jnp.where(tail_rows[:, None, None], block_k, jnp.zeros_like(block_k))
    new_state = continues * carry_state + jnp.einsum(
        "jhd,jhe->hde", kept_keys, block_v, preferred_element_type=jnp.float32
    )
    new_sum = continues * carry_sum + jnp.sum(kept_keys.astype(jnp.float32), axis=0)
    return (
        (new_state, new_sum, tail_crop),
        (numerator, denominator, carry_state, carry_sum, last_crop),
    )


def retreat(running, inputs):
    state_grad, sum_grad = running
    (
        block_q,
        block_k,
        block_v,
        block_seg,
        carry_state,
        carry_sum,
        last_crop,
        block_ngrad,
        block_dgrad,
    ) = inputs
    same_crop = causal_mask() & (block_seg[:, None] == block_seg[None, :])
    scores = jnp.einsum("ihd,jhd->hij", block_q, block_k, preferred_element_type=jnp.float32)
    scores_low = jnp.where(same_crop[None], scores, 0.0).astype(jnp.bfloat16)
    carried = (block_seg == last_crop).astype(jnp.float32)
    score_grad = (
        jnp.einsum("ihe,jhe->hij", block_ngrad, block_v, preferred_element_type=jnp.float32)
        + block_dgrad.T[:, :, None]
    )
    score_grad = jnp.where(
        same_crop[None], score_grad.astype(jnp.bfloat16), jnp.zeros_like(scores_low)
    )
    query_part = jnp.einsum("hij,jhd->ihd", score_grad, block_k, preferred_element_type=jnp.float32)
    key_part = jnp.einsum("hij,ihd->jhd", score_grad, block_q, preferred_element_type=jnp.float32)
    value_part = jnp.einsum(
        "hij,ihe->jhe", scores_low, block_ngrad, preferred_element_type=jnp.float32
    )
    ngrad_wide = block_ngrad.astype(jnp.float32)
    query_wide = block_q.astype(jnp.float32)
    query_part = query_part + carried[:, None, None] * (
        jnp.einsum("ihe,hde->ihd", ngrad_wide, carry_state, precision=precise)
        + block_dgrad[:, :, None] * carry_sum[None]
    )
    tail_crop = block_seg[-1]
    tail_rows = (block_seg == tail_crop).astype(jnp.float32)
    continues = (tail_crop == last_crop).astype(jnp.float32)
    key_part = key_part + tail_rows[:, None, None] * (
        jnp.einsum("jhe,hde->jhd", block_v.astype(jnp.float32), state_grad, precision=precise)
        + sum_grad[None]
    )
    value_part = value_part + tail_rows[:, None, None] * jnp.einsum(
        "jhd,hde->jhe", block_k.astype(jnp.float32), state_grad, precision=precise
    )
    opened_q = jnp.where(carried[:, None, None] > 0, block_q, jnp.zeros_like(block_q))
    state_grad_in = continues * state_grad + jnp.einsum(
        "ihd,ihe->hde", opened_q, block_ngrad, preferred_element_type=jnp.float32
    )
    sum_grad_in = continues * sum_grad + jnp.einsum(
        "ih,ihd->hd", carried[:, None] * block_dgrad, query_wide, precision=precise
    )
    return ((state_grad_in, sum_grad_in), (query_part, key_part, value_part))


def on_device(
    pixels,
    qkv_weight,
    out_weight,
    up_weight,
    down_weight,
    norm1_gain,
    norm1_bias,
    norm2_gain,
    norm2_bias,
    crop_lengths,
    crop_offsets,
    pixel_mask,
    out_grad,
):
    local_rows = pixels.shape[0]
    group_rows = pixel_mask.shape[0]
    width_local = qkv_weight.shape[2]
    head_count = width_local // HEAD
    block_count = group_rows // BLOCK
    crop_count = crop_offsets.shape[0]
    group_start = lax.axis_index("rows") * group_rows
    local_start = lax.axis_index("feat") * local_rows
    places = group_start + jnp.arange(group_rows, dtype=jnp.int32)
    started = crop_offsets[None, :] <= places[:, None]
    crop_ends = crop_offsets + crop_lengths
    segment = jnp.sum(started.astype(jnp.int32), axis=1) - 1
    inside = jnp.sum((started & (places[:, None] < crop_ends[None, :])).astype(jnp.int32), axis=1)
    pixel_valid = (pixel_mask * inside).astype(jnp.float32)
    first_crop = jnp.sum((crop_offsets <= group_start - 1).astype(jnp.int32)) - 1
    local_valid = lax.dynamic_slice_in_dim(pixel_valid, local_start, local_rows)
    local_segment = lax.dynamic_slice_in_dim(segment, local_start, local_rows)
    inputs = pixels.astype(jnp.float32)
    normed, norm1_back = jax.vjp(layer_norm, inputs, norm1_gain, norm1_bias)
    normed_all = lax.all_gather(normed.astype(jnp.bfloat16), "feat", axis=0, tiled=True)
    mixed = jnp.einsum("td,cde->tce", normed_all, qkv_weight, preferred_element_type=jnp.float32)
    head_shape = (group_rows, head_count, HEAD)
    queries = feature(mixed[:, 0]).astype(jnp.bfloat16).reshape(head_shape)
    key_rows = (
        (feature(mixed[:, 1]) * pixel_valid[:, None]).astype(jnp.bfloat16).reshape(head_shape)
    )
    value_rows = mixed[:, 2].astype(jnp.bfloat16).reshape(head_shape)
    zero_state = jnp.zeros((head_count, HEAD, HEAD), jnp.float32)
    zero_sum = jnp.zeros((head_count, HEAD), jnp.float32)
    block_inputs = (
        to_blocks(queries, block_count),
        to_blocks(key_rows, block_count),
        to_blocks(value_rows, block_count),
        to_blocks(segment, block_count),
    )
    (tail_state, tail_sum, tail_crop), kept = lax.scan(
        advance, (zero_state, zero_sum, first_crop), block_inputs
    )
    numer_local, denom_local, block_states, block_sums, block_last = kept
    numer_local = numer_local.reshape(head_shape)
    denom_local = denom_local.reshape(group_rows, head_count)
    reset_flag = (tail_crop != first_crop).astype(jnp.float32)
    identity = (zero_state, zero_sum, jnp.zeros((), jnp.float32))
    carry_state, carry_sum, _ = prefix(
        (tail_state, tail_sum, reset_flag), "rows", chain_join, identity, False
    )
    opening = (segment == first_crop).astype(jnp.float32)
    query_wide = queries.astype(jnp.float32)
    numerator = numer_local + opening[:, None, None] * jnp.einsum(
        "ihd,hde->ihe", query_wide, carry_state, precision=precise
    )
    denominator = denom_local + opening[:, None] * jnp.einsum(
        "ihd,hd->ih", query_wide, carry_sum, precision=precise
    )
    spread = denominator + 1e-06 + 1.0 - pixel_valid[:, None]
    heads_wide = pixel_valid[:, None, None] * numerator / spread[:, :, None]
    heads_out = heads_wide.astype(jnp.bfloat16).reshape(group_rows, width_local)
    row_piece = heads_out
    attended = lax.psum_scatter(
        jnp.dot(row_piece, out_weight, preferred_element_type=jnp.float32).astype(jnp.bfloat16),
        "feat",
        scatter_dimension=0,
        tiled=True,
    ).astype(jnp.float32)
    middle = inputs + attended
    normed_two, norm2_back = jax.vjp(layer_norm, middle, norm2_gain, norm2_bias)
    normed_low = normed_two.astype(jnp.bfloat16)
    normed_two_all, grad_all = (
        lax.all_gather(normed_low, "feat", axis=0, tiled=True),
        lax.all_gather(out_grad, "feat", axis=0, tiled=True),
    )
    hidden = jnp.dot(normed_two_all, up_weight, preferred_element_type=jnp.float32)
    activated, gelu_back = jax.vjp(gelu_tanh, hidden)
    activated_low = activated.astype(jnp.bfloat16)
    row_piece = activated_low
    branch = lax.psum_scatter(
        jnp.dot(row_piece, down_weight, preferred_element_type=jnp.float32).astype(jnp.bfloat16),
        "feat",
        scatter_dimension=0,
        tiled=True,
    ).astype(jnp.float32)
    active_grad = jnp.einsum("td,fd->tf", grad_all, down_weight, preferred_element_type=jnp.float32)
    hidden_grad = gelu_back(active_grad)[0].astype(jnp.bfloat16)
    up_grad = jnp.einsum(
        "td,tf->df", normed_two_all, hidden_grad, preferred_element_type=jnp.float32
    )
    down_grad = jnp.einsum("tf,td->fd", activated_low, grad_all, preferred_element_type=jnp.float32)
    row_piece = hidden_grad
    normed_two_grad = lax.psum_scatter(
        jnp.einsum("tf,df->td", row_piece, up_weight, preferred_element_type=jnp.float32).astype(
            jnp.bfloat16
        ),
        "feat",
        scatter_dimension=0,
        tiled=True,
    ).astype(jnp.float32)
    result = middle + branch
    middle_part, gain2_grad, bias2_grad = norm2_back(normed_two_grad)
    middle_grad = out_grad.astype(jnp.float32) + middle_part
    middle_all = lax.all_gather(middle_grad.astype(jnp.bfloat16), "feat", axis=0, tiled=True)
    heads_grad = jnp.einsum("td,ed->te", middle_all, out_weight, preferred_element_type=jnp.float32)
    out_grad_weight = jnp.einsum(
        "te,td->ed", heads_out, middle_all, preferred_element_type=jnp.float32
    )
    heads_grad = heads_grad.reshape(head_shape)
    numer_grad = (pixel_valid[:, None, None] * heads_grad / spread[:, :, None]).astype(jnp.bfloat16)
    denom_grad = -jnp.sum(heads_grad * heads_wide, axis=2) / spread
    opened_q = jnp.where(opening[:, None, None] > 0, queries, jnp.zeros_like(queries))
    carry_state_grad = jnp.einsum(
        "ihd,ihe->hde", opened_q, numer_grad, preferred_element_type=jnp.float32
    )
    carry_sum_grad = jnp.einsum(
        "ih,ihd->hd", opening[:, None] * denom_grad, query_wide, precision=precise
    )
    cross_query = opening[:, None, None] * (
        jnp.einsum("ihe,hde->ihd", numer_grad.astype(jnp.float32), carry_state, precision=precise)
        + denom_grad[:, :, None] * carry_sum[None]
    )
    tail_state_grad, tail_sum_grad, _ = prefix(
        (carry_state_grad, carry_sum_grad, reset_flag), "rows", chain_join, identity, True
    )
    back_inputs = block_inputs + (
        block_states,
        block_sums,
        block_last,
        to_blocks(numer_grad, block_count),
        to_blocks(denom_grad, block_count),
    )
    _, (query_grads, key_grads, value_grads) = lax.scan(
        retreat, (tail_state_grad, tail_sum_grad), back_inputs, reverse=True
    )
    query_total = query_grads.reshape(head_shape) + cross_query
    query_grad = query_total.reshape(group_rows, width_local) * feature_slope(mixed[:, 0])
    key_grad = (
        pixel_valid[:, None]
        * key_grads.reshape(group_rows, width_local)
        * feature_slope(mixed[:, 1])
    )
    value_grad = value_grads.reshape(group_rows, width_local)
    mixed_grad = jnp.stack([query_grad, key_grad, value_grad], axis=1).astype(jnp.bfloat16)
    qkv_grad = jnp.einsum("td,tce->cde", normed_all, mixed_grad, preferred_element_type=jnp.float32)
    row_piece = mixed_grad
    normed_grad = lax.psum_scatter(
        jnp.einsum("tce,cde->td", row_piece, qkv_weight, preferred_element_type=jnp.float32).astype(
            jnp.bfloat16
        ),
        "feat",
        scatter_dimension=0,
        tiled=True,
    ).astype(jnp.float32)
    input_part, gain1_grad, bias1_grad = norm1_back(normed_grad)
    pixels_grad = (middle_grad + input_part).astype(jnp.bfloat16)
    crop_onehot = (
        local_segment[:, None] == jnp.arange(crop_count, dtype=jnp.int32)[None, :]
    ).astype(jnp.float32)
    squares = (
        jnp.stack(
            [
                jnp.sum(result * result, axis=1),
                jnp.sum(attended * attended, axis=1),
                jnp.sum(branch * branch, axis=1),
            ]
        )
        * local_valid[None, :]
    )
    crop_sums = jnp.dot(squares, crop_onehot, precision=precise)
    crop_counts = jnp.dot(local_valid, crop_onehot, precision=precise)
    crop_sums, crop_counts, gain1_grad, bias1_grad, gain2_grad, bias2_grad = lax.psum(
        (crop_sums, crop_counts, gain1_grad, bias1_grad, gain2_grad, bias2_grad), ("rows", "feat")
    )
    qkv_grad, out_grad_weight, up_grad, down_grad = (
        lax.psum(qkv_grad.astype(jnp.bfloat16), "rows").astype(jnp.float32),
        lax.psum(out_grad_weight.astype(jnp.bfloat16), "rows").astype(jnp.float32),
        lax.psum(up_grad.astype(jnp.bfloat16), "rows").astype(jnp.float32),
        lax.psum(down_grad.astype(jnp.bfloat16), "rows").astype(jnp.float32),
    )
    crop_rms = jnp.sqrt(crop_sums / (D * jnp.maximum(crop_counts, 1.0))[None, :])
    return (
        result.astype(jnp.bfloat16),
        pixels_grad,
        qkv_grad,
        out_grad_weight,
        up_grad,
        down_grad,
        gain1_grad,
        bias1_grad,
        gain2_grad,
        bias2_grad,
        crop_rms,
    )


def solution(mesh):
    in_specs = (
        P(("rows", "feat"), None),
        P(None, None, "feat"),
        P("feat", None),
        P(None, "feat"),
        P("feat", None),
        P(),
        P(),
        P(),
        P(),
        P(),
        P(),
        P("rows"),
        P(("rows", "feat"), None),
    )
    out_specs = (
        P(("rows", "feat"), None),
        P(("rows", "feat"), None),
        P(None, None, "feat"),
        P("feat", None),
        P(None, "feat"),
        P("feat", None),
        P(),
        P(),
        P(),
        P(),
        P(),
    )
    return jax.shard_map(
        on_device, mesh=mesh, in_specs=in_specs, out_specs=out_specs, check_vma=False
    )
```

profile of v0, /device:TPU:0, one launch (start us, length us, event | category | flops | bytes accessed | tf_op | source)
XLA Modules:
  0.0 1004.1 jit_solution(1949254464942625301)
XLA Ops:
  16.8 27.9 %all-gather.11.cloned.1.call-done = bf16[1536,1024]{1,0:T(8,128)(2,1)} async-done(((bf16[384,1024]{1,0:T(8,128)(2,1)}), bf16[1536,1024]{1,0:T(8,128)(2,1)}) %all-gather.11.cloned.1.call-update) | async-done | bytes 3145744 | tf_op jit(solution)/shard_map/all_gather | solution.py:195
  44.8 5.0 fusion.114
  54.1 3.8 convert_element_type.318
  58.0 2.3 copy.97
  60.3 3.9 squeeze.147
  64.2 3.5 fusion.133
  68.7 3.9 squeeze.148
  72.6 3.4 fusion.132
  78.7 80.0 %while.82 = (s32[]{:T(128)}, f32[4,64,64]{2,1,0:T(8,128)S(1)}, f32[4,64]{1,0:T(4,128)}, s32[]{:T(128)}, f32[3,512,4,64]{1,0,3,2:T(4,128)}, /*index=5*/f32[3,512,...) while((s32[]{:T(128)}, f32[4,64,64]{2,1,0:T(8,128)S(1)}, ...), condition=%wide.region_8.9_spmd.clone, body=%wide.region_5.8_spmd.clone.sunk | while | flops 393302016 | bytes 10949395 | solution.py:211
  93.3 11.1 %dynamic_update_slice.70 = f32[3,512,4,64]{1,0,3,2:T(4,128)} dynamic-update-slice(f32[3,512,4,64]{1,0,3,2:T(4,128)} %get-tuple-element.1379, f32[1,512,4,64]{1,0,3,2:T(1,128)S(1)} %copy.165, s32[]{:T(128)S(6)} %copy.183, s32[]{:T(128)} %constant.227.clone.1..sunk.1, s32[]{:T(128)} %constant.227.clone.1..sunk.1, s32[]{:T(128)} %constant.227.clone.1..sunk.1) | dynamic-update-slice | bytes 1048580 | tf_op jit(solution)/shard_map/while/body/jit(dynamic_update_index_in_dim)/dynamic_update_slice | solution.py:211
  120.2 11.1 %dynamic_update_slice.70 = f32[3,512,4,64]{1,0,3,2:T(4,128)} dynamic-update-slice(f32[3,512,4,64]{1,0,3,2:T(4,128)} %get-tuple-element.1379, f32[1,512,4,64]{1,0,3,2:T(1,128)S(1)} %copy.165, s32[]{:T(128)S(6)} %copy.183, s32[]{:T(128)} %constant.227.clone.1..sunk.1, s32[]{:T(128)} %constant.227.clone.1..sunk.1, s32[]{:T(128)} %constant.227.clone.1..sunk.1) | dynamic-update-slice | bytes 1048580 | tf_op jit(solution)/shard_map/while/body/jit(dynamic_update_index_in_dim)/dynamic_update_slice | solution.py:211
  147.0 11.1 %dynamic_update_slice.70 = f32[3,512,4,64]{1,0,3,2:T(4,128)} dynamic-update-slice(f32[3,512,4,64]{1,0,3,2:T(4,128)} %get-tuple-element.1379, f32[1,512,4,64]{1,0,3,2:T(1,128)S(1)} %copy.165, s32[]{:T(128)S(6)} %copy.183, s32[]{:T(128)} %constant.227.clone.1..sunk.1, s32[]{:T(128)} %constant.227.clone.1..sunk.1, s32[]{:T(128)} %constant.227.clone.1..sunk.1) | dynamic-update-slice | bytes 1048580 | tf_op jit(solution)/shard_map/while/body/jit(dynamic_update_index_in_dim)/dynamic_update_slice | solution.py:211
  159.5 2.9 fusion.153
  162.4 21.3 %all-reduce = bf16[8]{0:T(256)(128)(2,1)S(1)} all-reduce(bf16[8]{0:T(256)(128)(2,1)S(1)} %dynamic-update-slice), channel_id=1, replica_groups=mesh['rows'=8,'feat'=4] {'rows'}, use_global_device_ids=true, to_apply=%add | all-reduce | flops 8 | bytes 32
  184.5 16.3 %all-gather.4 = bf16[8,4,64]{2,1,0:T(4,128)(2,1)S(1)} all-gather(bf16[1,4,64]{2,1,0:T(4,128)(2,1)S(1)} %convert_bitcast_fusion.1), channel_id=3, replica_groups=mesh['rows'=8,'feat'=4] {'rows'}, dimensions={0}, use_global_device_ids=true | all-gather | bytes 4608 | tf_op jit(solution)/shard_map/all_gather | solution.py:17
  200.7 33.3 %all-gather = bf16[32,64,64]{2,1,0:T(8,128)(2,1)} all-gather(bf16[4,64,64]{2,1,0:T(8,128)(2,1)S(1)} %convert_element_type.321), channel_id=2, replica_groups=mesh['rows'=8,'feat'=4] {'rows'}, dimensions={0}, use_global_device_ids=true | all-gather | bytes 294912 | tf_op jit(solution)/shard_map/all_gather | solution.py:17
  234.0 18.1 %while.83 = (s32[]{:T(128)}, f32[4,64,64]{2,1,0:T(8,128)S(1)}, f32[4,64]{1,0:T(4,128)S(1)}, s32[]{:T(128)}, bf16[8,4,64,64]{3,2,1,0:T(8,128)(2,1)}, /*index=5*/b...) while((s32[]{:T(128)}, f32[4,64,64]{2,1,0:T(8,128)S(1)}, ...), condition=%wide.region_10.11_spmd.clone, body=%wide.region_9.10_spmd.clone.sunk | while | flops 83205 | bytes 166565 | solution.py:35
  252.2 3.9 reshape.357
  258.4 3.9 fusion.189
  263.3 2.7 convolution_convert_fusion
  266.8 35.2 %reduce-scatter.5.cloned.1.call-done = bf16[384,1024]{1,0:T(8,128)(2,1)} async-done(((bf16[1536,1024]{1,0:T(8,128)(2,1)}), bf16[384,1024]{1,0:T(8,128)(2,1)}) %reduce-scatter.5.cloned.1.call-update) | async-done | bytes 786448 | tf_op jit(solution)/shard_map/reduce_scatter | solution.py:234
  305.3 26.9 %all-gather.15.cloned.1.call-done = bf16[1536,1024]{1,0:T(8,128)(2,1)} async-done(((bf16[384,1024]{1,0:T(8,128)(2,1)}), bf16[1536,1024]{1,0:T(8,128)(2,1)}) %all-gather.15.cloned.1.call-update) | async-done | bytes 3145744 | tf_op jit(solution)/shard_map/all_gather | solution.py:245
  332.2 8.7 fusion.191
  340.9 22.0 %all-gather.13.cloned.1.call-done = bf16[1536,1024]{1,0:T(8,128)(2,1)} async-done(((bf16[384,1024]{1,0:T(8,128)(2,1)}), bf16[1536,1024]{1,0:T(8,128)(2,1)}) %all-gather.13.cloned.1.call-update) | async-done | bytes 3145744 | tf_op jit(solution)/shard_map/all_gather | solution.py:244
  362.9 12.0 %fusion.111 = (bf16[1536,1024]{1,0:T(8,128)(2,1)S(1)}, f32[1536,1024]{1,0:T(8,128)}) fusion(f32[1536,1024]{1,0:T(8,128)} %fusion.191, bf16[1536,1024]{1,0:T(8,128)(2,1)} %all-gather.13.cloned.1.call-done, bf16[1024,1024]{1,0:T(8,128)(2,1)S(1)} %copy-done), kind=kOutput, calls=%fused_computation.151 | convolution fusion | flops 3252682752 | bytes 20971520 | tf_op jit(solution)/shard_map/dot_general | solution.py:247
  376.5 4.9 convolution_convert_fusion.1
  383.0 8.5 convolution_convert_fusion.2
  391.7 27.9 %reduce-scatter.9.cloned.1.call-done = bf16[384,1024]{1,0:T(8,128)(2,1)} async-done(((bf16[1536,1024]{1,0:T(8,128)(2,1)}), bf16[384,1024]{1,0:T(8,128)(2,1)}) %reduce-scatter.9.cloned.1.call-update) | async-done | bytes 786448 | tf_op jit(solution)/shard_map/reduce_scatter | solution.py:264
  419.6 41.0 %reduce-scatter.7.cloned.1.call-done = bf16[384,1024]{1,0:T(8,128)(2,1)} async-done(((bf16[1536,1024]{1,0:T(8,128)(2,1)}), bf16[384,1024]{1,0:T(8,128)(2,1)}) %reduce-scatter.7.cloned.1.call-update) | async-done | bytes 786448 | tf_op jit(solution)/shard_map/reduce_scatter | solution.py:251
  460.5 3.3 fusion.149
  467.1 28.6 %all-gather.17.cloned.1.call-done = bf16[1536,1024]{1,0:T(8,128)(2,1)} async-done(((bf16[384,1024]{1,0:T(8,128)(2,1)}), bf16[1536,1024]{1,0:T(8,128)(2,1)}) %all-gather.17.cloned.1.call-update) | async-done | bytes 3145744 | tf_op jit(solution)/shard_map/all_gather | solution.py:275
  495.7 3.6 multiply_reduce_fusion.1
  500.1 20.5 %all-gather.5 = bf16[8,4,64]{2,1,0:T(4,128)(2,1)S(1)} all-gather(bf16[1,4,64]{2,1,0:T(4,128)(2,1)S(1)} %convert_bitcast_fusion), channel_id=5, replica_groups=mesh['rows'=8,'feat'=4] {'rows'}, dimensions={0}, use_global_device_ids=true | all-gather | bytes 4608 | tf_op jit(solution)/shard_map/all_gather | solution.py:17
  520.6 2.1 reshape.361
  524.2 31.3 %all-gather.2 = bf16[32,64,64]{2,1,0:T(8,128)(2,1)S(1)} all-gather(bf16[4,64,64]{2,1,0:T(8,128)(2,1)S(1)} %convolution_convert_fusion.6), channel_id=4, replica_groups=mesh['rows'=8,'feat'=4] {'rows'}, dimensions={0}, use_global_device_ids=true | all-gather | bytes 294912 | tf_op jit(solution)/shard_map/all_gather | solution.py:17
  555.5 11.0 %while.84 = (s32[]{:T(128)}, f32[4,64,64]{2,1,0:T(8,128)S(1)}, f32[4,64]{1,0:T(4,128)S(1)}, s32[]{:T(128)}, bf16[8,4,64,64]{3,2,1,0:T(8,128)(2,1)S(1)}, /*index=...) while((s32[]{:T(128)}, f32[4,64,64]{2,1,0:T(8,128)S(1)}, ...), condition=%wide.region_20.21_spmd.clone, body=%wide.region_19.20_spmd.clone.sunk | while | flops 83209 | bytes 166627 | solution.py:35
  566.5 2.1 fusion.134
  574.0 130.2 %while.81 = (s32[]{:T(128)}, f32[4,64,64]{2,1,0:T(8,128)S(1)}, f32[4,64]{1,0:T(4,128)S(1)}, f32[3,512,4,64]{1,0,3,2:T(4,128)}, f32[3,512,4,64]{1,0,3,2:T(4,128)}...) while((s32[]{:T(128)}, f32[4,64,64]{2,1,0:T(8,128)S(1)}, ...), condition=%wide.region_22.23_spmd, body=%wide.region_21.22_spmd.sunk | while | flops 999855104 | bytes 20155172 | solution.py:304
  582.1 3.0 fusion.285
  595.3 11.1 %dynamic_update_slice.65 = f32[3,512,4,64]{1,0,3,2:T(4,128)} dynamic-update-slice(f32[3,512,4,64]{1,0,3,2:T(4,128)} %get-tuple-element.1495, f32[1,512,4,64]{1,0,3,2:T(1,128)S(1)} %copy.162, s32[]{:T(128)S(6)} %sub.159, s32[]{:T(128)} %constant.227.clone.1..sunk, s32[]{:T(128)} %constant.227.clone.1..sunk, s32[]{:T(128)} %constant.227.clone.1..sunk) | dynamic-update-slice | bytes 1048580 | tf_op jit(solution)/shard_map/while/body/jit(dynamic_update_index_in_dim)/dynamic_update_slice | solution.py:211
  606.4 11.1 %dynamic_update_slice.66 = f32[3,512,4,64]{1,0,3,2:T(4,128)} dynamic-update-slice(f32[3,512,4,64]{1,0,3,2:T(4,128)} %get-tuple-element.1496, f32[1,512,4,64]{1,0,3,2:T(1,128)S(1)} %copy.163, s32[]{:T(128)S(6)} %sub.159, s32[]{:T(128)} %constant.227.clone.1..sunk, s32[]{:T(128)} %constant.227.clone.1..sunk, s32[]{:T(128)} %constant.227.clone.1..sunk) | dynamic-update-slice | bytes 1048580 | tf_op jit(solution)/shard_map/while/body/jit(dynamic_update_index_in_dim)/dynamic_update_slice | solution.py:211
  625.5 3.0 fusion.285
  638.7 11.1 %dynamic_update_slice.65 = f32[3,512,4,64]{1,0,3,2:T(4,128)} dynamic-update-slice(f32[3,512,4,64]{1,0,3,2:T(4,128)} %get-tuple-element.1495, f32[1,512,4,64]{1,0,3,2:T(1,128)S(1)} %copy.162, s32[]{:T(128)S(6)} %sub.159, s32[]{:T(128)} %constant.227.clone.1..sunk, s32[]{:T(128)} %constant.227.clone.1..sunk, s32[]{:T(128)} %constant.227.clone.1..sunk) | dynamic-update-slice | bytes 1048580 | tf_op jit(solution)/shard_map/while/body/jit(dynamic_update_index_in_dim)/dynamic_update_slice | solution.py:211
  649.8 11.1 %dynamic_update_slice.66 = f32[3,512,4,64]{1,0,3,2:T(4,128)} dynamic-update-slice(f32[3,512,4,64]{1,0,3,2:T(4,128)} %get-tuple-element.1496, f32[1,512,4,64]{1,0,3,2:T(1,128)S(1)} %copy.163, s32[]{:T(128)S(6)} %sub.159, s32[]{:T(128)} %constant.227.clone.1..sunk, s32[]{:T(128)} %constant.227.clone.1..sunk, s32[]{:T(128)} %constant.227.clone.1..sunk) | dynamic-update-slice | bytes 1048580 | tf_op jit(solution)/shard_map/while/body/jit(dynamic_update_index_in_dim)/dynamic_update_slice | solution.py:211
  668.9 3.0 fusion.285
  682.1 11.1 %dynamic_update_slice.65 = f32[3,512,4,64]{1,0,3,2:T(4,128)} dynamic-update-slice(f32[3,512,4,64]{1,0,3,2:T(4,128)} %get-tuple-element.1495, f32[1,512,4,64]{1,0,3,2:T(1,128)S(1)} %copy.162, s32[]{:T(128)S(6)} %sub.159, s32[]{:T(128)} %constant.227.clone.1..sunk, s32[]{:T(128)} %constant.227.clone.1..sunk, s32[]{:T(128)} %constant.227.clone.1..sunk) | dynamic-update-slice | bytes 1048580 | tf_op jit(solution)/shard_map/while/body/jit(dynamic_update_index_in_dim)/dynamic_update_slice | solution.py:211
  693.2 11.1 %dynamic_update_slice.66 = f32[3,512,4,64]{1,0,3,2:T(4,128)} dynamic-update-slice(f32[3,512,4,64]{1,0,3,2:T(4,128)} %get-tuple-element.1496, f32[1,512,4,64]{1,0,3,2:T(1,128)S(1)} %copy.163, s32[]{:T(128)S(6)} %sub.159, s32[]{:T(128)} %constant.227.clone.1..sunk, s32[]{:T(128)} %constant.227.clone.1..sunk, s32[]{:T(128)} %constant.227.clone.1..sunk) | dynamic-update-slice | bytes 1048580 | tf_op jit(solution)/shard_map/while/body/jit(dynamic_update_index_in_dim)/dynamic_update_slice | solution.py:211
  704.2 4.0 reshape.363
  708.3 3.5 fusion.122
  711.7 2.9 copy.111
  714.7 3.4 stack_reshape.4
  718.1 2.1 reshape.365
  720.2 3.8 fusion.154
  724.8 4.4 bitcast_convert_fusion
  729.3 8.3 convolution_convert_fusion.4
  737.7 8.5 convolution_convert_fusion.3
  748.7 3.9 fusion.155
  754.0 9.8 reduce-scatter.11.cloned.1.call-done
  766.4 43.2 %all-reduce.1 = (f32[1024]{0:T(1024)}, f32[1024]{0:T(1024)}, f32[1024]{0:T(1024)}, f32[1024]{0:T(1024)}, f32[3,32]{1,0:T(4,128)S(1)}, /*index=5*/f32[32]{0:T(128)S(1)}) all-reduce(f32[1024]{0:T(1024)S(1)} %get-tuple-element.945, f32[1024]{0:T(1024)S(1)} %get-tuple-element.950, ...), channel_id=1, replica_groups=mesh['rows'=8,'feat'=4] {'rows','feat'}, use_global_device_ids=true, to_apply=%region_31.32 | all-reduce | flops 4224 | bytes 33792 | tf_op jit(solution)/shard_map/psum | solution.py:343
  809.6 174.5 %all-reduce.5.cloned.1.call-done = (bf16[3,1024,256]{1,2,0:T(8,128)(2,1)}, bf16[256,1024]{1,0:T(8,128)(2,1)}, bf16[1024,1024]{1,0:T(8,128)(2,1)}, bf16[1024,1024]{1,0:T(8,128)(2,1)}) async-done(((bf16[3,1024,256]{1,2,0:T(8,128)(2,1)}, bf16[256,1024]{1,0:T(8,128)(2,1)}, bf16[1024,1024]{1,0:T(8,128)(2,1)}, bf16[1024,1024]{1,0:T(8,128)(2,1)}), (bf16[3,1024,256]{1,2,0:T(8,128)(2,1)}, ...) | async-done | bytes 6291472 | tf_op jit(solution)/shard_map/psum | solution.py:347
  984.1 2.2 convert_element_type.350
  986.4 2.1 copy.113
  988.4 4.2 convert_element_type.352
  992.7 2.5 convert_element_type.354
  (345 shorter events, 160.7 us)
Async XLA Ops:
  7.2 355.7 %copy-start = (bf16[1024,1024]{1,0:T(8,128)(2,1)S(1)}, bf16[1024,1024]{1,0:T(8,128)(2,1)}, u32[]{:S(2)}) copy-start(bf16[1024,1024]{1,0:T(8,128)(2,1)} %param.24) | copy-start | bytes 6291460
  7.2 8.4 copy-start.51
  7.2 4.2 copy-start.2
  7.2 6.3 copy-start.45
  7.2 6.3 copy-start.46
  7.2 7.7 copy-start.42
  7.2 37.5 %all-gather.11.cloned.1.call-start = ((), (), s32[]{:S(2)}) async-start(), calls=%async_computation.4 | async-start | bytes 3932160 | tf_op jit(solution)/shard_map/all_gather | solution.py:195
  8.8 2.1 copy-start.29
  10.3 0.6 copy-start.40
  10.8 0.6 copy-start.38
  13.4 288.6 %reduce-scatter.5.cloned.1.call-start = ((), (), s32[]{:S(2)}) async-start(), calls=%async_computation.5 | async-start | bytes 3932160 | tf_op jit(solution)/shard_map/reduce_scatter | solution.py:234
  15.0 0.6 copy-start.36
  15.6 48.6 %copy-start.31 = (f32[3,512]{1,0:T(4,128)}, f32[3,512]{1,0:T(4,128)S(1)}, u32[]{:S(2)}) copy-start(f32[3,512]{1,0:T(4,128)S(1)} %mul.552) | copy-start | bytes 18436
  49.8 2.5 copy-start.7
  158.7 75.3 %copy-start.16 = (f32[4,64,64]{2,1,0:T(8,128)S(1)}, f32[4,64,64]{2,1,0:T(8,128)}, u32[]{:S(2)}) copy-start(f32[4,64,64]{2,1,0:T(8,128)} %custom-call.2) | copy-start | bytes 196612
  158.7 75.3 %copy-start.33 = (f32[4,64]{1,0:T(4,128)S(1)}, f32[4,64]{1,0:T(4,128)}, u32[]{:S(2)}) copy-start(f32[4,64]{1,0:T(4,128)} %custom-call.3) | copy-start | bytes 3076
  252.2 5.5 copy-start.34
  258.4 4.8 copy-start.22
  262.3 0.9 copy-start.19
  266.0 38.0 %copy-start.37 = (f32[1024]{0:T(1024)S(1)}, f32[1024]{0:T(1024)}, u32[]{:S(2)}) copy-start(f32[1024]{0:T(1024)} %param.28) | copy-start | bytes 12292
  266.0 38.0 %copy-start.43 = (f32[1024]{0:T(1024)S(1)}, f32[1024]{0:T(1024)}, u32[]{:S(2)}) copy-start(f32[1024]{0:T(1024)} %param.29) | copy-start | bytes 12292
  266.0 66.2 %all-gather.15.cloned.1.call-start = ((), (), s32[]{:S(2)}) async-start(), calls=%async_computation.8 | async-start | bytes 3932160 | tf_op jit(solution)/shard_map/all_gather | solution.py:245
  266.7 96.1 %all-gather.13.cloned.1.call-start = ((), (), s32[]{:S(2)}) async-start(), calls=%async_computation.6 | async-start | bytes 3932160 | tf_op jit(solution)/shard_map/all_gather | solution.py:244
  302.0 1.5 copy-start.3
  305.3 114.3 %reduce-scatter.9.cloned.1.call-start = ((), (), s32[]{:S(2)}) async-start(), calls=%async_computation.9 | async-start | bytes 3932160 | tf_op jit(solution)/shard_map/reduce_scatter | solution.py:264
  374.9 1.7 copy-start.52
  381.4 1.6 copy-start.49
  381.5 79.1 %reduce-scatter.7.cloned.1.call-start = ((), (), s32[]{:S(2)}) async-start(), calls=%async_computation.7 | async-start | bytes 3932160 | tf_op jit(solution)/shard_map/reduce_scatter | solution.py:251
  391.6 69.0 %copy-start.4 = (bf16[384,1024]{1,0:T(8,128)(2,1)S(1)}, bf16[384,1024]{1,0:T(8,128)(2,1)}, u32[]{:S(2)}) copy-start(bf16[384,1024]{1,0:T(8,128)(2,1)} %reduce-scatter.5.cloned.1.call-done) | copy-start | bytes 2359300
  391.6 104.1 %all-gather.17.cloned.1.call-start = ((), (), s32[]{:S(2)}) async-start(), calls=%async_computation.10 | async-start | bytes 3932160 | tf_op jit(solution)/shard_map/all_gather | solution.py:275
  460.5 3.3 copy-start.18
  463.8 2.0 copy-start.11
  464.6 1.2 copy-start.5
  467.0 296.8 %reduce-scatter.11.cloned.1.call-start = ((), (), s32[]{:S(2)}) async-start(), calls=%async_computation.11 | async-start | bytes 3932160 | tf_op jit(solution)/shard_map/reduce_scatter | solution.py:318
  495.7 3.7 copy-start.17
  499.3 23.4 %copy-start.8 = (f32[1536,256]{0,1:T(8,128)}, f32[1536,256]{0,1:T(8,128)S(1)}, u32[]{:S(2)}) copy-start(f32[1536,256]{0,1:T(8,128)S(1)} %get-tuple-element.1078) | copy-start | bytes 4718596
  499.3 23.4 %copy-start.44 = (pred[1536]{0:T(1024)(128)(4,1)S(1)}, pred[1536]{0:T(1024)(128)(4,1)}, u32[]{:S(2)}) copy-start(pred[1536]{0:T(1024)(128)(4,1)} %get-tuple-element.1058) | copy-start | bytes 4612
  524.2 42.3 %copy-start.32 = (f32[3,512]{1,0:T(4,128)S(1)}, f32[3,512]{1,0:T(4,128)}, u32[]{:S(2)}) copy-start(f32[3,512]{1,0:T(4,128)} %copy-done.31) | copy-start | bytes 18436
  704.2 4.0 copy-start.9
  711.7 6.4 copy-start.10
  720.2 4.6 copy-start.24
  720.2 4.6 copy-start.50
  723.9 0.9 copy-start.27
  723.9 5.3 copy-start.25
  729.3 254.9 %all-reduce.5.cloned.1.call-start = ((), (), s32[]{:S(2)}) async-start(), calls=%async_computation.12 | async-start | bytes 12582912 | tf_op jit(solution)/shard_map/psum | solution.py:347
  729.3 8.3 copy-start.48
  737.7 8.5 copy-start.15
  737.7 8.5 copy-start.20
  746.1 1.9 copy-start.26
  746.1 1.9 copy-start.28
  746.1 2.6 copy-start.47
  752.5 11.2 %copy-start.30 = (f32[384]{0:T(512)S(1)}, f32[384]{0:T(512)}, u32[]{:S(2)}) copy-start(f32[384]{0:T(512)} %copy-done.29) | copy-start | bytes 4612
  752.5 11.2 %copy-start.35 = (f32[1024]{0:T(1024)S(1)}, f32[1024]{0:T(1024)}, u32[]{:S(2)}) copy-start(f32[1024]{0:T(1024)} %param.26) | copy-start | bytes 12292
  752.5 12.9 %copy-start.41 = (f32[384]{0:T(512)S(1)}, f32[384]{0:T(512)}, u32[]{:S(2)}) copy-start(f32[384]{0:T(512)} %copy-done.40) | copy-start | bytes 4612
  752.5 12.9 %copy-start.39 = (f32[384]{0:T(512)S(1)}, f32[384]{0:T(512)}, u32[]{:S(2)}) copy-start(f32[384]{0:T(512)} %copy-done.38) | copy-start | bytes 4612
  763.7 1.8 copy-start.13
  984.1 2.2 copy-start.23
  988.4 4.2 copy-start.21
  992.7 3.1 copy-start.6
  992.7 3.1 copy-start.12
  992.7 3.1 copy-start.14
  995.1 2.3 copy-start.1
Sparse Core Ops, SparseCore 0:
  13.5 31.2 all-gather.10
  266.1 35.8 reduce-scatter.4
  303.6 28.5 all-gather.14
  334.3 28.5 all-gather.12
  381.6 37.9 reduce-scatter.8
  422.5 37.9 reduce-scatter.6
  467.1 28.5 all-gather.16
  729.4 34.2 reduce-scatter.10
  768.8 215.3 all-reduce.4
where the time goes:
time: 1010 us; the launch traced here: 1000 us
  waiting for transfers between devices  395 us (39%)
  local copies, waits for them, and re-layouts  187 us (19%)
  blocking collectives  166 us (16%)
  matrix products  149 us (15%)
  other arithmetic  72.6 us (7%)
  loops' own time  19.5 us (2%)
  between operations  15.3 us (2%)
    psum x1, waiting for transfers between devices, on_device(): lax.psum(qkv_grad.astype(jnp.bfloat16), 'rows').astype(jnp.float32)  175 us
    dynamic_update_slice x21, local copies, waits for them, and re-layouts, on_device(): lax.scan(advance, (zero_state, zero_sum, first_crop), block_inputs)  109 us
    all_gather x4, blocking collectives, prefix(): lax.all_gather(part.astype(kind), axis)  101 us
    psum x1, blocking collectives, on_device(): lax.psum((crop_sums, crop_counts, gain1_grad, bias1_grad, gain2_grad, bia...  43.2 us
    reduce_scatter x1, waiting for transfers between devices, on_device(): lax.psum_scatter(jnp.dot(row_piece, down_weight, preferred_element_type=j...  41 us
    reduce_scatter x1, waiting for transfers between devices, on_device(): lax.psum_scatter(jnp.dot(row_piece, out_weight, preferred_element_type=jn...  35.2 us
    all_gather x1, waiting for transfers between devices, on_device(): lax.all_gather(middle_grad.astype(jnp.bfloat16), 'feat', axis=0, tiled=True)  28.6 us
    all_gather x1, waiting for transfers between devices, on_device(): lax.all_gather(normed.astype(jnp.bfloat16), 'feat', axis=0, tiled=True)  27.9 us
  transfers between devices with their start and end apart: 9, of which 9 were waited for; matrix products, arithmetic and copies ran while one was open for 5% of the time, Pallas kernels for 0%

commit v1 on v0

v1 whole, which is shorter than its diff:
```python
import functools

import jax
import jax.numpy as jnp
from jax import lax
from jax.experimental import pallas as pl
from jax.experimental.pallas import tpu as pltpu
from jax.sharding import PartitionSpec as P

D = 1024
HEAD = 64
CHUNK = 256
CROP_MAX = 3072
PACK = HEAD + 16

BF = jnp.bfloat16
F32 = jnp.float32
precise = lax.Precision.HIGHEST


def nn(a, b):
    return lax.dot_general(a, b, (((1,), (0,)), ((), ())), preferred_element_type=F32)


def nt(a, b):
    return lax.dot_general(a, b, (((1,), (1,)), ((), ())), preferred_element_type=F32)


def tn(a, b):
    return lax.dot_general(a, b, (((0,), (0,)), ((), ())), preferred_element_type=F32)


def same_head(width):
    row = lax.broadcasted_iota(jnp.int32, (width, width), 0) // HEAD
    col = lax.broadcasted_iota(jnp.int32, (width, width), 1) // HEAD
    return row == col


def lane_head(rows, width):
    return lax.broadcasted_iota(jnp.int32, (rows, width), 1) // HEAD


def causal(rows):
    row = lax.broadcasted_iota(jnp.int32, (rows, rows), 0)
    col = lax.broadcasted_iota(jnp.int32, (rows, rows), 1)
    return row >= col


def fold_heads(full, width):
    out = full[0:HEAD]
    for h in range(1, width // HEAD):
        out = out + full[h * HEAD : (h + 1) * HEAD]
    return out


def spread_heads(part, width, block):
    tall = jnp.concatenate([part] * (width // HEAD), axis=0)
    return jnp.where(block, tall, jnp.zeros_like(tall))


def pick(mask, value):
    return jnp.where(mask, value, jnp.zeros_like(value))


def forward_body(last_ref, q_ref, k_ref, v_ref, segc_ref, segr_ref, num_ref, den_ref, st_ref, ks_ref):
    rows, width = q_ref.shape
    size = CHUNK
    block = same_head(width)
    ones_block = block.astype(BF)
    lanes = lane_head(size, width)
    lower = causal(size)
    st_ref[...] = jnp.zeros_like(st_ref)
    ks_ref[...] = jnp.zeros_like(ks_ref)

    def step(c, carry):
        at = pl.ds(pl.multiple_of(c * size, size), size)
        q, k, v = q_ref[at, :], k_ref[at, :], v_ref[at, :]
        seg = segc_ref[at, :]
        keep = lower & (seg == segr_ref[c])
        before, after = last_ref[c], last_ref[c + 1]
        carried = (seg == before).astype(F32)
        num = carried * nn(q, st_ref[...].astype(BF))
        den = carried * nn((q.astype(F32) * ks_ref[0:1, :]).astype(BF), ones_block)
        for h in range(width // HEAD):
            mine = lanes == h
            score = pick(keep, nt(pick(mine, q), k)).astype(BF)
            num = num + nn(score, pick(mine, v))
            den = den + nn(score, mine.astype(BF))
        num_ref[at, :] = num
        den_ref[at, :] = den
        kept = pick(seg == after, k)
        cont = (before == after).astype(F32)
        st_ref[...] = cont * st_ref[...] + pick(block, tn(kept, v))
        ks_ref[...] = cont * ks_ref[...] + jnp.sum(kept.astype(F32), axis=0, keepdims=True)
        return carry

    lax.fori_loop(0, rows // size, step, 0)


def full_spec():
    return pl.BlockSpec(memory_space=pltpu.VMEM)


def smem_spec():
    return pl.BlockSpec(memory_space=pltpu.SMEM)


def attend(last, q, k, v, segc, segr):
    rows, width = q.shape
    return pl.pallas_call(
        forward_body,
        out_shape=(jax.ShapeDtypeStruct((rows, width), F32),) * 2,
        in_specs=[smem_spec()] + [full_spec()] * 5,
        out_specs=(full_spec(),) * 2,
        scratch_shapes=[pltpu.VMEM((width, width), F32), pltpu.VMEM((8, width), F32)],
        name="attend",
    )(last, q, k, v, segc, segr)


def tail_body(last_ref, k_ref, v_ref, segc_ref, out_ref):
    rows, width = k_ref.shape
    tail = last_ref[rows // CHUNK]
    kept = pick(segc_ref[...] == tail, k_ref[...])
    state = fold_heads(pick(same_head(width), tn(kept, v_ref[...])), width)
    sums = jnp.sum(kept.astype(F32), axis=0, keepdims=True)
    out_ref[0:HEAD, :] = state.astype(BF)
    out_ref[HEAD:PACK, :] = jnp.broadcast_to(sums, (PACK - HEAD, width)).astype(BF)


def tail_pack(last, k, v, segc):
    return pl.pallas_call(
        tail_body,
        out_shape=jax.ShapeDtypeStruct((PACK, k.shape[1]), BF),
        in_specs=[smem_spec()] + [full_spec()] * 3,
        out_specs=full_spec(),
        name="tail_pack",
    )(last, k, v, segc)


def project_body(
    first_ref, num_ref, den_ref, q_ref, pack_ref, segc_ref, valid_ref, w_ref,
    heads_ref, wide_ref, rinv_ref, out_ref
):
    rows, width = q_ref.shape
    block = same_head(width)
    state = spread_heads(pack_ref[0:HEAD, :], width, block).astype(BF)
    sums = pack_ref[HEAD : HEAD + 1, :]
    q = q_ref[...]
    opening = (segc_ref[...] == first_ref[0]).astype(F32)
    valid = valid_ref[...]
    num = num_ref[...] + opening * nn(q, state)
    den = den_ref[...] + opening * nn((q.astype(F32) * sums).astype(BF), block.astype(BF))
    rinv = valid / (den + 1e-06 + 1.0 - valid)
    wide = num * rinv
    heads = wide.astype(BF)
    heads_ref[...] = heads
    wide_ref[...] = wide
    rinv_ref[...] = rinv
    out_ref[...] = nn(heads, w_ref[...]).astype(BF)


def project(last, num, den, q, pack, segc, valid, w):
    rows, width = q.shape
    tile = 512
    by_row = lambda cols: pl.BlockSpec((tile, cols), lambda i: (i, 0))
    whole = lambda a: pl.BlockSpec(a.shape, lambda i: (0, 0))
    return pl.pallas_call(
        project_body,
        grid=(rows // tile,),
        out_shape=(
            jax.ShapeDtypeStruct((rows, width), BF),
            jax.ShapeDtypeStruct((rows, width), F32),
            jax.ShapeDtypeStruct((rows, width), F32),
            jax.ShapeDtypeStruct((rows, D), BF),
        ),
        in_specs=[
            smem_spec(), by_row(width), by_row(width), by_row(width), whole(pack),
            by_row(1), by_row(1), whole(w),
        ],
        out_specs=(by_row(width), by_row(width), by_row(width), by_row(D)),
        name="project",
    )(last, num, den, q, pack, segc, valid, w)


def heads_back_body(
    first_ref, grad_ref, w_ref, wide_ref, rinv_ref, q_ref, segc_ref,
    ng_ref, dg_ref, pack_ref, st_ref, ks_ref
):
    width = q_ref.shape[1]
    block = same_head(width)
    ones_block = block.astype(BF)
    hg = nt(grad_ref[...], w_ref[...])
    rinv = rinv_ref[...]
    ng = (hg * rinv).astype(BF)
    prod = hg * wide_ref[...]
    high = prod.astype(BF)
    low = (prod - high.astype(F32)).astype(BF)
    dg = -(nn(high, ones_block) + nn(low, ones_block)) * rinv
    ng_ref[...] = ng
    dg_ref[...] = dg
    opened = pick(segc_ref[...] == first_ref[0], q_ref[...])

    @pl.when(pl.program_id(0) == 0)
    def _():
        st_ref[...] = jnp.zeros_like(st_ref)
        ks_ref[...] = jnp.zeros_like(ks_ref)

    st_ref[...] += tn(opened, ng)
    ks_ref[...] += jnp.sum(opened.astype(F32) * dg, axis=0, keepdims=True)

    @pl.when(pl.program_id(0) == pl.num_programs(0) - 1)
    def _():
        pack_ref[0:HEAD, :] = fold_heads(pick(block, st_ref[...]), width).astype(BF)
        pack_ref[HEAD:PACK, :] = jnp.broadcast_to(ks_ref[0:1, :], (PACK - HEAD, width)).astype(BF)


def heads_back(last, grad, w, wide, rinv, q, segc):
    rows, width = q.shape
    tile = 512
    by_row = lambda cols: pl.BlockSpec((tile, cols), lambda i: (i, 0))
    whole = lambda shape: pl.BlockSpec(shape, lambda i: (0, 0))
    return pl.pallas_call(
        heads_back_body,
        grid=(rows // tile,),
        out_shape=(
            jax.ShapeDtypeStruct((rows, width), BF),
            jax.ShapeDtypeStruct((rows, width), F32),
            jax.ShapeDtypeStruct((PACK, width), BF),
        ),
        in_specs=[
            smem_spec(), by_row(D), whole(w.shape), by_row(width), by_row(width), by_row(width),
            by_row(1),
        ],
        out_specs=(by_row(width), by_row(width), whole((PACK, width))),
        scratch_shapes=[pltpu.VMEM((width, width), F32), pltpu.VMEM((8, width), F32)],
        name="heads_back",
    )(last, grad, w, wide, rinv, q, segc)


def backward_body(
    last_ref, q_ref, k_ref, v_ref, ng_ref, dg_ref, segc_ref, segr_ref, pack_ref,
    dq_ref, dk_ref, dv_ref, all_ref, sums_ref, st_ref, ks_ref
):
    rows, width = q_ref.shape
    size = CHUNK
    count = rows // size
    block = same_head(width)
    lanes = lane_head(size, width)
    lower = causal(size)
    st_ref[...] = spread_heads(pack_ref[0:HEAD, :], width, block)
    ks_ref[...] = jnp.broadcast_to(pack_ref[HEAD : HEAD + 1, :], ks_ref.shape)

    def collect(c, carry):
        at = pl.ds(pl.multiple_of(c * size, size), size)
        all_ref[c] = st_ref[...].astype(BF)
        sums_ref[c] = ks_ref[...]
        before, after = last_ref[c], last_ref[c + 1]
        kept = pick(segc_ref[at, :] == after, k_ref[at, :])
        cont = (before == after).astype(F32)
        st_ref[...] = cont * st_ref[...] + pick(block, tn(kept, v_ref[at, :]))
        ks_ref[...] = cont * ks_ref[...] + jnp.sum(kept.astype(F32), axis=0, keepdims=True)
        return carry

    lax.fori_loop(0, count, collect, 0)
    st_ref[...] = jnp.zeros_like(st_ref)
    ks_ref[...] = jnp.zeros_like(ks_ref)

    def step(i, carry):
        c = count - 1 - i
        at = pl.ds(pl.multiple_of(c * size, size), size)
        q, k, v, ng, dg = q_ref[at, :], k_ref[at, :], v_ref[at, :], ng_ref[at, :], dg_ref[at, :]
        seg = segc_ref[at, :]
        keep = lower & (seg == segr_ref[c])
        before, after = last_ref[c], last_ref[c + 1]
        opened = seg == before
        carried = opened.astype(F32)
        tail = (seg == after).astype(F32)
        grad_state = st_ref[...].astype(BF)
        dq = carried * (nt(ng, all_ref[c]) + dg * sums_ref[c][0:1, :])
        dk = tail * (nt(v, grad_state) + ks_ref[0:1, :])
        dv = tail * nn(k, grad_state)
        for h in range(width // HEAD):
            mine = lanes == h
            qh, kh, nh = pick(mine, q), pick(mine, k), pick(mine, ng)
            score = pick(keep, nt(qh, k)).astype(BF)
            lead = dg[:, h * HEAD : h * HEAD + 1]
            back = pick(keep, nt(nh, v) + lead).astype(BF)
            dq = dq + nn(back, kh)
            dk = dk + tn(back, qh)
            dv = dv + tn(score, nh)
        dq_ref[at, :] = (dq * jnp.minimum(q.astype(F32), 1.0)).astype(BF)
        dk_ref[at, :] = dk
        dv_ref[at, :] = dv
        cont = (before == after).astype(F32)
        st_ref[...] = cont * st_ref[...] + pick(block, tn(pick(opened, q), ng))
        ks_ref[...] = cont * ks_ref[...] + jnp.sum(carried * q.astype(F32) * dg, axis=0, keepdims=True)
        return carry

    lax.fori_loop(0, count, step, 0)


def attend_back(last, q, k, v, ng, dg, segc, segr, pack):
    rows, width = q.shape
    count = rows // CHUNK
    return pl.pallas_call(
        backward_body,
        out_shape=(
            jax.ShapeDtypeStruct((rows, width), BF),
            jax.ShapeDtypeStruct((rows, width), F32),
            jax.ShapeDtypeStruct((rows, width), F32),
        ),
        in_specs=[smem_spec()] + [full_spec()] * 8,
        out_specs=(full_spec(),) * 3,
        scratch_shapes=[
            pltpu.VMEM((count, width, width), BF),
            pltpu.VMEM((count, 8, width), F32),
            pltpu.VMEM((width, width), F32),
            pltpu.VMEM((8, width), F32),
        ],
        name="attend_back",
    )(last, q, k, v, ng, dg, segc, segr, pack)


def mix_body(tail_ref, dq_ref, dk_ref, dv_ref, k_ref, v_ref, segc_ref, valid_ref, pack_ref, out_ref):
    rows, width = k_ref.shape
    block = same_head(width)
    state = spread_heads(pack_ref[0:HEAD, :], width, block).astype(BF)
    sums = pack_ref[HEAD : HEAD + 1, :]
    tail = (segc_ref[...] == tail_ref[0]).astype(F32)
    k = k_ref[...]
    dk = dk_ref[...] + tail * (nt(v_ref[...], state) + sums)
    dv = dv_ref[...] + tail * nn(k, state)
    out_ref[:, 0:width] = dq_ref[...]
    out_ref[:, width : 2 * width] = (valid_ref[...] * dk * jnp.minimum(k.astype(F32), 1.0)).astype(BF)
    out_ref[:, 2 * width : 3 * width] = dv.astype(BF)


def mix(tail, dq, dk, dv, k, v, segc, valid, pack):
    rows, width = k.shape
    tile = 512
    by_row = lambda cols: pl.BlockSpec((tile, cols), lambda i: (i, 0))
    return pl.pallas_call(
        mix_body,
        grid=(rows // tile,),
        out_shape=jax.ShapeDtypeStruct((rows, 3 * width), BF),
        in_specs=[smem_spec()] + [by_row(width)] * 5 + [by_row(1)] * 2
        + [pl.BlockSpec(pack.shape, lambda i: (0, 0))],
        out_specs=by_row(3 * width),
        name="mix",
    )(tail, dq, dk, dv, k, v, segc, valid, pack)


def layer_norm(values, norm_gain, norm_bias):
    centre = jnp.mean(values, axis=-1, keepdims=True)
    shifted = values - centre
    spread = jnp.mean(shifted * shifted, axis=-1, keepdims=True)
    return shifted * lax.rsqrt(spread + 1e-05) * norm_gain + norm_bias


def feature(values):
    return jnp.where(values > 0, values + 1.0, jnp.exp(jnp.minimum(values, 0.0)))


def gelu_tanh(values):
    return jax.nn.gelu(values, approximate=True)


def shifted(pack, hop, groups, reverse):
    if reverse:
        pairs = [(i, i - hop) for i in range(hop, groups)]
    else:
        pairs = [(i, i + hop) for i in range(groups - hop)]
    return lax.ppermute(pack, "rows", pairs)


def gather_carry(pack, crops_at, here, groups, reach, reverse):
    total = jnp.zeros(pack.shape, F32)
    mine = crops_at[here + 1] if reverse else crops_at[here]
    for hop in range(1, reach + 1):
        got = shifted(pack, hop, groups, reverse).astype(F32)
        other = here + hop if reverse else here - hop
        inside = (other < groups) if reverse else (other >= 0)
        at = jnp.clip(other, 0, groups - 1)
        theirs = crops_at[at] if reverse else crops_at[at + 1]
        total = total + jnp.where(inside & (theirs == mine), got, 0.0)
    return total


def on_device(
    pixels,
    qkv_weight,
    out_weight,
    up_weight,
    down_weight,
    norm1_gain,
    norm1_bias,
    norm2_gain,
    norm2_bias,
    crop_lengths,
    crop_offsets,
    pixel_mask,
    out_grad,
):
    local_rows = pixels.shape[0]
    group_rows = pixel_mask.shape[0]
    width_local = qkv_weight.shape[2]
    crop_count = crop_offsets.shape[0]
    groups = lax.axis_size("rows")
    here = lax.axis_index("rows")
    reach = min(groups - 1, -(-(CROP_MAX - 1) // group_rows))
    group_start = here * group_rows
    local_start = lax.axis_index("feat") * local_rows
    places = group_start + jnp.arange(group_rows, dtype=jnp.int32)
    started = crop_offsets[None, :] <= places[:, None]
    crop_ends = crop_offsets + crop_lengths
    segment = jnp.sum(started.astype(jnp.int32), axis=1) - 1
    inside = jnp.sum((started & (places[:, None] < crop_ends[None, :])).astype(jnp.int32), axis=1)
    pixel_valid = (pixel_mask * inside).astype(F32)
    edges = jnp.arange(groups + 1, dtype=jnp.int32) * group_rows - 1
    crops_at = jnp.sum((crop_offsets[None, :] <= edges[:, None]).astype(jnp.int32), axis=1) - 1
    chunk_edges = group_start - 1 + jnp.arange(group_rows // CHUNK + 1, dtype=jnp.int32) * CHUNK
    last = jnp.sum((crop_offsets[None, :] <= chunk_edges[:, None]).astype(jnp.int32), axis=1) - 1
    segc = segment[:, None]
    segr = segment.reshape(group_rows // CHUNK, 1, CHUNK)
    validc = pixel_valid[:, None]
    local_valid = lax.dynamic_slice_in_dim(pixel_valid, local_start, local_rows)
    local_segment = lax.dynamic_slice_in_dim(segment, local_start, local_rows)

    inputs = pixels.astype(F32)
    normed, norm1_back = jax.vjp(layer_norm, inputs, norm1_gain, norm1_bias)
    normed_all = lax.all_gather(normed.astype(BF), "feat", axis=0, tiled=True)
    grad_all = lax.all_gather(out_grad, "feat", axis=0, tiled=True)
    k = (feature(nn(normed_all, qkv_weight[1])) * validc).astype(BF)
    v = nn(normed_all, qkv_weight[2]).astype(BF)
    pack = tail_pack(last, k, v, segc)
    carry = gather_carry(pack, crops_at, here, groups, reach, False)
    q = feature(nn(normed_all, qkv_weight[0])).astype(BF)
    num, den = attend(last, q, k, v, segc, segr)
    heads_out, heads_wide, rinv, part = project(last, num, den, q, carry, segc, validc, out_weight)
    attended = lax.psum_scatter(part, "feat", scatter_dimension=0, tiled=True).astype(F32)
    middle = inputs + attended
    normed_two, norm2_back = jax.vjp(layer_norm, middle, norm2_gain, norm2_bias)
    normed_two_all = lax.all_gather(normed_two.astype(BF), "feat", axis=0, tiled=True)
    hidden = nn(normed_two_all, up_weight)
    activated, gelu_back = jax.vjp(gelu_tanh, hidden)
    activated_low = activated.astype(BF)
    active_grad = nt(grad_all, down_weight)
    hidden_grad = gelu_back(active_grad)[0].astype(BF)
    normed_two_grad = lax.psum_scatter(
        nt(hidden_grad, up_weight).astype(BF), "feat", scatter_dimension=0, tiled=True
    ).astype(F32)
    branch = lax.psum_scatter(
        nn(activated_low, down_weight).astype(BF), "feat", scatter_dimension=0, tiled=True
    ).astype(F32)
    up_grad = tn(normed_two_all, hidden_grad)
    down_grad = tn(activated_low, grad_all)
    result = middle + branch
    middle_part, gain2_grad, bias2_grad = norm2_back(normed_two_grad)
    middle_grad = out_grad.astype(F32) + middle_part
    middle_all = lax.all_gather(middle_grad.astype(BF), "feat", axis=0, tiled=True)
    ng, dg, grad_pack = heads_back(last, middle_all, out_weight, heads_wide, rinv, q, segc)
    grad_carry = gather_carry(grad_pack, crops_at, here, groups, reach, True)
    out_weight_grad = tn(heads_out, middle_all)
    dq, dk, dv = attend_back(last, q, k, v, ng, dg, segc, segr, carry)
    mixed_grad = mix(last[-1:], dq, dk, dv, k, v, segc, validc, grad_carry)
    qkv_flat = jnp.concatenate([qkv_weight[0], qkv_weight[1], qkv_weight[2]], axis=1)
    normed_grad = lax.psum_scatter(
        nt(mixed_grad, qkv_flat).astype(BF), "feat", scatter_dimension=0, tiled=True
    ).astype(F32)
    qkv_grad = jnp.stack(
        [
            tn(normed_all, mixed_grad[:, c * width_local : (c + 1) * width_local])
            for c in range(3)
        ]
    )
    input_part, gain1_grad, bias1_grad = norm1_back(normed_grad)
    pixels_grad = (middle_grad + input_part).astype(BF)
    crop_onehot = (
        local_segment[:, None] == jnp.arange(crop_count, dtype=jnp.int32)[None, :]
    ).astype(F32)
    squares = (
        jnp.stack(
            [
                jnp.sum(result * result, axis=1),
                jnp.sum(attended * attended, axis=1),
                jnp.sum(branch * branch, axis=1),
            ]
        )
        * local_valid[None, :]
    )
    crop_sums = jnp.dot(squares, crop_onehot, precision=precise)
    crop_counts = jnp.dot(local_valid, crop_onehot, precision=precise)
    crop_sums, crop_counts, gain1_grad, bias1_grad, gain2_grad, bias2_grad = lax.psum(
        (crop_sums, crop_counts, gain1_grad, bias1_grad, gain2_grad, bias2_grad), ("rows", "feat")
    )
    qkv_grad, out_weight_grad, up_grad, down_grad = (
        lax.psum(qkv_grad.astype(BF), "rows").astype(F32),
        lax.psum(out_weight_grad.astype(BF), "rows").astype(F32),
        lax.psum(up_grad.astype(BF), "rows").astype(F32),
        lax.psum(down_grad.astype(BF), "rows").astype(F32),
    )
    crop_rms = jnp.sqrt(crop_sums / (D * jnp.maximum(crop_counts, 1.0))[None, :])
    return (
        result.astype(BF),
        pixels_grad,
        qkv_grad,
        out_weight_grad,
        up_grad,
        down_grad,
        gain1_grad,
        bias1_grad,
        gain2_grad,
        bias2_grad,
        crop_rms,
    )


def solution(mesh):
    split = P(("rows", "feat"), None)
    qkv, rows_feat, cols_feat = P(None, None, "feat"), P("feat", None), P(None, "feat")
    in_specs = (
        (split, qkv, rows_feat, cols_feat, rows_feat) + (P(),) * 6 + (P("rows"), split)
    )
    out_specs = (split, split, qkv, rows_feat, cols_feat, rows_feat) + (P(),) * 5
    return jax.shard_map(
        on_device, mesh=mesh, in_specs=in_specs, out_specs=out_specs, check_vma=False
    )
```

time: 1010 us -> 643 us (0.64)
  local copies, waits for them, and re-layouts: 187 us -> 9.98 us
  blocking collectives: 166 us -> 42.9 us
  matrix products: 149 us -> 73 us
  Pallas kernels: 0 us -> 50.7 us
  other arithmetic: 72.6 us -> 31.3 us
  loops' own time: 19.5 us -> 0 us
    dynamic_update_slice x21 -> x0, local copies, waits for them, and re-layouts: 109 us -> none  [on_device(): lax.scan(advance, (zero_state, zero_sum, first_crop), block_inputs)]
    all_gather x4 -> x0, blocking collectives: 101 us -> none  [prefix(): lax.all_gather(part.astype(kind), axis)]
    dot_general x59 -> x14, matrix products: 149 us -> 72.5 us  [the longest x5 31.4 us: nn(): lax.dot_general(a, b, (((1,), (0,)), ((), ())), preferred_element_type=F32)]
    pallas_call x0 -> x6, Pallas kernels: none -> 50.7 us  [the longest x1 16.2 us: attend_back(): pl.pallas_call(backward_body, out_shape=(jax.ShapeDtypeStruct((rows, widt...]
    unnamed x1 -> x0, blocking collectives: 21.3 us -> none
    another operation x4 -> x0, loops' own time: 19.5 us -> none  [the longest x2 11.7 us: prefix(): return lax.fori_loop(0, peers, hop, start)]
    convert_element_type x16 -> x9, other arithmetic: 28.5 us -> 15.2 us  [the longest x1 2.48 us: on_device(): lax.psum(down_grad.astype(BF), 'rows').astype(F32)]
    unnamed x113 -> x64, local copies, waits for them, and re-layouts: 18.1 us -> 4.78 us
  transfers between devices with their start and end apart: 9 -> 13, of which waited for: 9 -> 9; matrix products, arithmetic and copies ran while one was open for 5% -> 9% of each run, Pallas kernels for 0% -> 4%
where the time goes in v1:
time: 643 us; the launch traced here: 636 us
  waiting for transfers between devices  397 us (62%)
  matrix products  73 us (11%)
  Pallas kernels  50.7 us (8%)
  blocking collectives  42.9 us (7%)
  other arithmetic  31.3 us (5%)
  between operations  19.9 us (3%)
  starting transfers between devices  10.4 us (2%)
  local copies, waits for them, and re-layouts  9.98 us (2%)
    psum x1, waiting for transfers between devices, on_device(): lax.psum(qkv_grad.astype(BF), 'rows').astype(F32)  175 us
    psum x1, blocking collectives, on_device(): lax.psum((crop_sums, crop_counts, gain1_grad, bias1_grad, gain2_grad, bia...  42.9 us
    reduce_scatter x1, waiting for transfers between devices, on_device(): lax.psum_scatter(nn(activated_low, down_weight).astype(BF), 'feat', scatt...  41 us
    reduce_scatter x1, waiting for transfers between devices, on_device(): lax.psum_scatter(part, 'feat', scatter_dimension=0, tiled=True).astype(F32)  35.4 us
    dot_general x5, matrix products, nn(): lax.dot_general(a, b, (((1,), (0,)), ((), ())), preferred_element_type=F32)  31.4 us
    all_gather x1, waiting for transfers between devices, on_device(): lax.all_gather(middle_grad.astype(BF), 'feat', axis=0, tiled=True)  28.6 us
    reduce_scatter x1, waiting for transfers between devices, on_device(): lax.psum_scatter(nt(hidden_grad, up_weight).astype(BF), 'feat', scatter_d...  27.9 us
    all_gather x1, waiting for transfers between devices, on_device(): grad_all = lax.all_gather(out_grad, 'feat', axis=0, tiled=True)  26.7 us
  transfers between devices with their start and end apart: 13, of which 9 were waited for; matrix products, arithmetic and copies ran while one was open for 9% of the time, Pallas kernels for 4%

profile of v1, /device:TPU:0, one launch (start us, length us, event | category | flops | bytes accessed | tf_op | source)
XLA Modules:
  0.0 635.7 jit_solution(18385743837449953226)
XLA Ops:
  7.3 1.5 convert_reduce_fusion.2
  8.8 1.5 fusion.20
  10.3 1.9 fusion.16
  12.5 0.6 sub.51.segr_ref
  13.1 1.2 sub.59.segc_ref
  14.5 0.6 fusion.56
  17.7 1.1 broadcast_in_dim.23.valid_ref
  19.0 0.5 broadcast_add_fusion.2.last_ref.first_ref
  19.6 24.0 %all-gather.5.cloned.1.call-done = bf16[1536,1024]{1,0:T(8,128)(2,1)} async-done(((bf16[384,1024]{1,0:T(8,128)(2,1)}), bf16[1536,1024]{1,0:T(8,128)(2,1)}) %all-gather.5.cloned.1.call-update) | async-done | bytes 3145744 | tf_op jit(solution)/shard_map/all_gather | solution.py:431
  43.6 4.1 multiply_convert_fusion.1.k_ref
  47.7 3.0 convolution_convert_fusion.3.v_ref
  50.7 2.9 tail_pack.1
  53.7 3.4 collective-permute-start.1
  57.1 3.4 collective-permute-start
  60.5 3.9 select_convert_fusion.q_ref
  64.4 10.3 %attend.1 = (f32[1536,256]{1,0:T(8,128)}, f32[1536,256]{1,0:T(8,128)}) custom-call(s32[7]{0:T(128)} %broadcast_add_fusion.2.last_ref.first_ref, bf16[1536,256]{1,0:T(8,128)(2,1)} %select_convert_fusion.q_ref, bf16[1536,256]{1,0:T(8,128)(2,1)} %multiply_convert_fusion.1.k_ref, bf16[1536,256]{1,0:T(8,128)(2,1)} %convolution_convert_fusion.3.v_ref, ...), custom_call_target="tpu_custom_call" | custom-call | tf_op jit(solution)/shard_map/attend/pallas_call | solution.py:110
  74.7 0.7 select_add_fusion.1.pack_ref
  75.4 7.2 %project.1 = (bf16[1536,256]{1,0:T(8,128)(2,1)}, f32[1536,256]{1,0:T(8,128)}, f32[1536,256]{1,0:T(8,128)}, bf16[1536,1024]{1,0:T(8,128)(2,1)}) custom-call(s32[7]{0:T(128)} %broadcast_add_fusion.2.last_ref.first_ref, f32[1536,256]{1,0:T(8,128)} %get-tuple-element.23.num_ref, f32[1536,256]{1,0:T(8,128)} %get-tuple-element.24.den_ref, ...), custom_call_target="tpu_custom_call" | custom-call | tf_op jit(solution)/shard_map/project/pallas_call | solution.py:167
  82.7 0.7 all-gather.9.cloned.1.call-update
  83.5 35.4 %reduce-scatter.5.cloned.1.call-done = bf16[384,1024]{1,0:T(8,128)(2,1)} async-done(((bf16[1536,1024]{1,0:T(8,128)(2,1)}), bf16[384,1024]{1,0:T(8,128)(2,1)}) %reduce-scatter.5.cloned.1.call-update) | async-done | bytes 786448 | tf_op jit(solution)/shard_map/reduce_scatter | solution.py:440
  118.9 1.5 fusion.30
  120.8 1.3 add_convert_fusion.1
  122.4 26.7 %all-gather.9.cloned.1.call-done = bf16[1536,1024]{1,0:T(8,128)(2,1)} async-done(((bf16[384,1024]{1,0:T(8,128)(2,1)}), bf16[1536,1024]{1,0:T(8,128)(2,1)}) %all-gather.9.cloned.1.call-update) | async-done | bytes 3145744 | tf_op jit(solution)/shard_map/all_gather | solution.py:432
  149.1 8.7 %fusion.57 = f32[1536,1024]{1,0:T(8,128)} fusion(bf16[1536,1024]{1,0:T(8,128)(2,1)} %all-gather.9.cloned.1.call-done, bf16[1024,1024]{1,0:T(8,128)(2,1)} %param.17), kind=kOutput, calls=%fused_computation.122 | convolution fusion | flops 3221225472 | bytes 11534336 | tf_op jit(solution)/shard_map/dot_general | solution.py:26
  157.8 22.0 %all-gather.7.cloned.1.call-done = bf16[1536,1024]{1,0:T(8,128)(2,1)} async-done(((bf16[384,1024]{1,0:T(8,128)(2,1)}), bf16[1536,1024]{1,0:T(8,128)(2,1)}) %all-gather.7.cloned.1.call-update) | async-done | bytes 3145744 | tf_op jit(solution)/shard_map/all_gather | solution.py:443
  179.7 11.9 %fusion.6 = (bf16[1536,1024]{1,0:T(8,128)(2,1)S(1)}, f32[1536,1024]{1,0:T(8,128)}) fusion(f32[1536,1024]{1,0:T(8,128)} %fusion.57, bf16[1536,1024]{1,0:T(8,128)(2,1)} %all-gather.7.cloned.1.call-done, bf16[1024,1024]{1,0:T(8,128)(2,1)S(1)} %copy-done), kind=kOutput, calls=%fused_computation.8 | convolution fusion | flops 3252682752 | bytes 20971520 | tf_op jit(solution)/shard_map/dot_general | solution.py:22
  191.6 1.7 copy-done.31
  193.2 4.9 convolution_convert_fusion.1
  198.5 1.3 copy-done.28
  199.8 8.5 %convolution_convert_fusion.2 = bf16[1536,1024]{1,0:T(8,128)(2,1)} fusion(bf16[1024,1024]{1,0:T(8,128)(2,1)S(1)} %copy-done.28, f32[1536,1024]{1,0:T(8,128)} %get-tuple-element.70), kind=kOutput, calls=%fused_computation.12 | convolution fusion | flops 3236954112 | bytes 11534336 | tf_op jit(solution)/shard_map/dot_general | solution.py:22
  208.4 27.9 %reduce-scatter.9.cloned.1.call-done = bf16[384,1024]{1,0:T(8,128)(2,1)} async-done(((bf16[1536,1024]{1,0:T(8,128)(2,1)}), bf16[384,1024]{1,0:T(8,128)(2,1)}) %reduce-scatter.9.cloned.1.call-update) | async-done | bytes 786448 | tf_op jit(solution)/shard_map/reduce_scatter | solution.py:449
  236.3 41.0 %reduce-scatter.7.cloned.1.call-done = bf16[384,1024]{1,0:T(8,128)(2,1)} async-done(((bf16[1536,1024]{1,0:T(8,128)(2,1)}), bf16[384,1024]{1,0:T(8,128)(2,1)}) %reduce-scatter.7.cloned.1.call-update) | async-done | bytes 786448 | tf_op jit(solution)/shard_map/reduce_scatter | solution.py:452
  277.3 3.3 fusion.22
  280.6 0.7 fusion.55
  281.3 1.2 copy-done.5
  282.5 1.1 fusion.35
  283.7 28.6 %all-gather.11.cloned.1.call-done.grad_ref = bf16[1536,1024]{1,0:T(8,128)(2,1)} async-done(((bf16[384,1024]{1,0:T(8,128)(2,1)}), bf16[1536,1024]{1,0:T(8,128)(2,1)}) %all-gather.11.cloned.1.call-update) | async-done | bytes 3145744 | tf_op jit(solution)/shard_map/all_gather | solution.py:460
  312.4 7.5 %heads_back.1 = (bf16[1536,256]{1,0:T(8,128)(2,1)}, f32[1536,256]{1,0:T(8,128)}, bf16[80,256]{1,0:T(8,128)(2,1)}) custom-call(s32[7]{0:T(128)} %broadcast_add_fusion.2.last_ref.first_ref, bf16[1536,1024]{1,0:T(8,128)(2,1)} %all-gather.11.cloned.1.call-done.grad_ref, bf16[256,1024]{1,0:T(8,128)(2,1)} %w_ref.3, f32[1536,256]{1,0:T(8,128)} %get-tuple-element.26.wide_ref, ...), custom_call_target="tpu_custom_call" | custom-call | tf_op jit(solution)/shard_map/heads_back/pallas_call | solution.py:222
  319.9 1.3 collective-permute-start.3
  321.2 1.3 collective-permute-start.2
  322.5 0.9 slice_bitcast_fusion.2
  323.4 0.6 slice.27.tail_ref
  326.6 16.2 %attend_back.1 = (bf16[1536,256]{1,0:T(8,128)(2,1)}, f32[1536,256]{1,0:T(8,128)}, f32[1536,256]{1,0:T(8,128)}) custom-call(s32[7]{0:T(128)} %broadcast_add_fusion.2.last_ref.first_ref, bf16[1536,256]{1,0:T(8,128)(2,1)} %select_convert_fusion.q_ref, bf16[1536,256]{1,0:T(8,128)(2,1)} %multiply_convert_fusion.1.k_ref, ...), custom_call_target="tpu_custom_call" | custom-call | tf_op jit(solution)/shard_map/attend_back/pallas_call | solution.py:305
  342.8 0.7 select_add_fusion.pack_ref
  343.5 6.5 %mix.1 = bf16[1536,768]{1,0:T(8,128)(2,1)} custom-call(s32[1]{0:T(128)} %slice.27.tail_ref, bf16[1536,256]{1,0:T(8,128)(2,1)} %get-tuple-element.30.dq_ref, f32[1536,256]{1,0:T(8,128)} %get-tuple-element.31.dk_ref, f32[1536,256]{1,0:T(8,128)} %get-tuple-element.32.dv_ref, bf16[1536,256]{1,0:T(8,128)(2,1)} %multiply_convert_fusion.1.k_ref, ...), custom_call_target="tpu_custom_call" | custom-call | tf_op jit(solution)/shard_map/mix/pallas_call | solution.py:342
  349.9 5.7 convolution_convert_fusion
  356.0 7.8 %convolution_convert_fusion.5 = bf16[1024,1024]{1,0:T(8,128)(2,1)} fusion(bf16[1536,1024]{1,0:T(8,128)(2,1)} %all-gather.7.cloned.1.call-done, bf16[1536,1024]{1,0:T(8,128)(2,1)} %copy-done.31), kind=kOutput, calls=%fused_computation.33 | convolution fusion | flops 3222274048 | bytes 8388608 | tf_op jit(solution)/shard_map/dot_general | solution.py:30
  363.8 9.1 %convolution_convert_fusion.4 = bf16[1024,1024]{1,0:T(8,128)(2,1)} fusion(bf16[1536,1024]{1,0:T(8,128)(2,1)S(1)} %copy-done.27, f32[1536,1024]{1,0:T(8,128)} %get-tuple-element.70), kind=kOutput, calls=%fused_computation.32 | convolution fusion | flops 3236429824 | bytes 11534336 | tf_op jit(solution)/shard_map/dot_general | solution.py:30
  372.9 1.8 convolution_convert_fusion.6
  374.7 1.0 fusion.33
  375.7 1.0 fusion.32
  376.8 1.0 fusion.31
  377.8 1.3 pad_maximum_fusion
  379.9 16.3 %reduce-scatter.11.cloned.1.call-done = bf16[384,1024]{1,0:T(8,128)(2,1)} async-done(((bf16[1536,1024]{1,0:T(8,128)(2,1)}), bf16[384,1024]{1,0:T(8,128)(2,1)}) %reduce-scatter.11.cloned.1.call-update) | async-done | bytes 786448 | tf_op jit(solution)/shard_map/reduce_scatter | solution.py:467
  396.1 1.7 convert_reduce_fusion
  397.9 1.2 fusion.23
  399.1 42.9 %all-reduce = (f32[1024]{0:T(1024)}, f32[1024]{0:T(1024)}, f32[1024]{0:T(1024)}, f32[1024]{0:T(1024)}, f32[3,32]{1,0:T(4,128)S(1)}, /*index=5*/f32[32]{0:T(128)S(1)}) all-reduce(f32[1024]{0:T(1024)S(1)} %get-tuple-element.37, f32[1024]{0:T(1024)S(1)} %get-tuple-element.42, ...), channel_id=1, replica_groups=mesh['rows'=8,'feat'=4] {'rows','feat'}, use_global_device_ids=true, to_apply=%region_21.22 | all-reduce | flops 4224 | bytes 33792 | tf_op jit(solution)/shard_map/psum | solution.py:493
  442.0 174.7 %all-reduce.4.cloned.1.call-done = (bf16[3,1024,256]{2,1,0:T(8,128)(2,1)}, bf16[256,1024]{1,0:T(8,128)(2,1)}, bf16[1024,1024]{1,0:T(8,128)(2,1)}, bf16[1024,1024]{1,0:T(8,128)(2,1)}) async-done(((bf16[3,1024,256]{2,1,0:T(8,128)(2,1)}, bf16[256,1024]{1,0:T(8,128)(2,1)}, bf16[1024,1024]{1,0:T(8,128)(2,1)}, bf16[1024,1024]{1,0:T(8,128)(2,1)}), (bf16[3,1024,256]{2,1,0:T(8,128)(2,1)}, ...) | async-done | bytes 6291472 | tf_op jit(solution)/shard_map/psum | solution.py:497
  616.7 2.2 convert_element_type.137
  619.0 1.9 convert_element_type.135
  621.4 2.5 convert_element_type.139
  623.9 2.5 convert_element_type.141
  626.4 0.6 divide_sqrt_fusion
  627.0 1.6 add_convert_fusion
  (109 shorter events, 3.5 us)
Async XLA Ops:
  7.2 172.6 %copy-start = (bf16[1024,1024]{1,0:T(8,128)(2,1)S(1)}, bf16[1024,1024]{1,0:T(8,128)(2,1)}, u32[]{:S(2)}) copy-start(bf16[1024,1024]{1,0:T(8,128)(2,1)} %param.16) | copy-start | bytes 6291460
  7.2 3.1 copy-start.2
  7.2 5.1 copy-start.24
  7.2 5.1 copy-start.30
  7.2 5.2 copy-start.22
  7.2 36.4 %all-gather.5.cloned.1.call-start = ((), (), s32[]{:S(2)}) async-start(), calls=%async_computation.4 | async-start | bytes 3932160 | tf_op jit(solution)/shard_map/all_gather | solution.py:431
  12.2 106.7 %reduce-scatter.5.cloned.1.call-start = ((), (), s32[]{:S(2)}) async-start(), calls=%async_computation.5 | async-start | bytes 3932160 | tf_op jit(solution)/shard_map/reduce_scatter | solution.py:440
  43.6 4.1 copy-start.25
  53.7 21.1 %collective-permute-start.1 = (bf16[80,256]{1,0:T(8,128)(2,1)}, bf16[80,256]{1,0:T(8,128)(2,1)S(1)}, u32[]{:S(2)}, u32[]{:S(2)}) collective-permute-start(bf16[80,256]{1,0:T(8,128)(2,1)} %tail_pack.1), channel_id=1, source_target_pairs={{0,8},{4,12},{8,16},{12,20},{16,24},{20,28},{1,9},{5,13},{9,17},{1... | collective-permute-start | bytes 122888 | tf_op jit(solution)/shard_map/ppermute | solution.py:373
  57.1 17.7 %collective-permute-start = (bf16[80,256]{1,0:T(8,128)(2,1)}, bf16[80,256]{1,0:T(8,128)(2,1)S(1)}, u32[]{:S(2)}, u32[]{:S(2)}) collective-permute-start(bf16[80,256]{1,0:T(8,128)(2,1)} %tail_pack.1), channel_id=1, source_target_pairs={{0,4},{4,8},{8,12},{12,16},{16,20},{20,24},{24,28},{1,5},{5,9},{9,... | collective-permute-start | bytes 122888 | tf_op jit(solution)/shard_map/ppermute | solution.py:373
  82.7 38.1 %copy-start.20 = (f32[1024]{0:T(1024)S(1)}, f32[1024]{0:T(1024)}, u32[]{:S(2)}) copy-start(f32[1024]{0:T(1024)} %param.20) | copy-start | bytes 12292
  82.7 38.1 %copy-start.23 = (f32[1024]{0:T(1024)S(1)}, f32[1024]{0:T(1024)}, u32[]{:S(2)}) copy-start(f32[1024]{0:T(1024)} %param.21) | copy-start | bytes 12292
  82.7 66.4 %all-gather.9.cloned.1.call-start = ((), (), s32[]{:S(2)}) async-start(), calls=%async_computation.8 | async-start | bytes 3932160 | tf_op jit(solution)/shard_map/all_gather | solution.py:432
  83.4 96.3 %all-gather.7.cloned.1.call-start = ((), (), s32[]{:S(2)}) async-start(), calls=%async_computation.6 | async-start | bytes 3932160 | tf_op jit(solution)/shard_map/all_gather | solution.py:443
  118.9 1.5 copy-start.3
  122.1 114.2 %reduce-scatter.9.cloned.1.call-start = ((), (), s32[]{:S(2)}) async-start(), calls=%async_computation.9 | async-start | bytes 3932160 | tf_op jit(solution)/shard_map/reduce_scatter | solution.py:449
  191.6 1.7 copy-start.31
  198.2 1.6 copy-start.28
  198.2 79.1 %reduce-scatter.7.cloned.1.call-start = ((), (), s32[]{:S(2)}) async-start(), calls=%async_computation.7 | async-start | bytes 3932160 | tf_op jit(solution)/shard_map/reduce_scatter | solution.py:452
  208.3 68.9 %copy-start.4 = (bf16[384,1024]{1,0:T(8,128)(2,1)S(1)}, bf16[384,1024]{1,0:T(8,128)(2,1)}, u32[]{:S(2)}) copy-start(bf16[384,1024]{1,0:T(8,128)(2,1)} %reduce-scatter.5.cloned.1.call-done) | copy-start | bytes 2359300
  208.3 104.0 %all-gather.11.cloned.1.call-start = ((), (), s32[]{:S(2)}) async-start(), calls=%async_computation.10 | async-start | bytes 3932160 | tf_op jit(solution)/shard_map/all_gather | solution.py:460
  277.3 3.3 copy-start.12
  280.6 1.9 copy-start.7
  281.3 1.2 copy-start.5
  283.7 112.5 %reduce-scatter.11.cloned.1.call-start = ((), (), s32[]{:S(2)}) async-start(), calls=%async_computation.11 | async-start | bytes 3932160 | tf_op jit(solution)/shard_map/reduce_scatter | solution.py:467
  312.4 10.2 %copy-start.16 = (bf16[3,1024,256]{2,1,0:T(8,128)(2,1)S(1)}, bf16[3,1024,256]{2,1,0:T(8,128)(2,1)}, u32[]{:S(2)}) copy-start(bf16[3,1024,256]{2,1,0:T(8,128)(2,1)} %param.14) | copy-start | bytes 4718596
  319.9 3.5 copy-start.21
  319.9 22.9 %collective-permute-start.3 = (bf16[80,256]{1,0:T(8,128)(2,1)}, bf16[80,256]{1,0:T(8,128)(2,1)S(1)}, u32[]{:S(2)}, u32[]{:S(2)}) collective-permute-start(bf16[80,256]{1,0:T(8,128)(2,1)} %get-tuple-element.33), channel_id=1, source_target_pairs={{8,0},{12,4},{16,8},{20,12},{24,16},{28,20},{9,1},{13,5},{17,9},{2... | collective-permute-start | bytes 122888 | tf_op jit(solution)/shard_map/ppermute | solution.py:373
  321.2 21.6 %collective-permute-start.2 = (bf16[80,256]{1,0:T(8,128)(2,1)}, bf16[80,256]{1,0:T(8,128)(2,1)S(1)}, u32[]{:S(2)}, u32[]{:S(2)}) collective-permute-start(bf16[80,256]{1,0:T(8,128)(2,1)} %get-tuple-element.33), channel_id=1, source_target_pairs={{4,0},{8,4},{12,8},{16,12},{20,16},{24,20},{28,24},{5,1},{9,5},{13... | collective-permute-start | bytes 122888 | tf_op jit(solution)/shard_map/ppermute | solution.py:373
  343.5 6.5 %copy-start.18 = (bf16[1024,256]{1,0:T(8,128)(2,1)S(1)}, bf16[1024,256]{1,0:T(8,128)(2,1)}, u32[]{:S(2)}) copy-start(bf16[1024,256]{1,0:T(8,128)(2,1)} %get-tuple-element.61) | copy-start | bytes 1572868
  355.7 261.1 %all-reduce.4.cloned.1.call-start = ((), (), s32[]{:S(2)}) async-start(), calls=%async_computation.12 | async-start | bytes 12582912 | tf_op jit(solution)/shard_map/psum | solution.py:497
  356.0 7.8 %copy-start.27 = (bf16[1536,1024]{1,0:T(8,128)(2,1)S(1)}, bf16[1536,1024]{1,0:T(8,128)(2,1)}, u32[]{:S(2)}) copy-start(bf16[1536,1024]{1,0:T(8,128)(2,1)} %all-gather.9.cloned.1.call-done) | copy-start | bytes 9437188
  363.8 9.1 %copy-start.11 = (bf16[1536,1024]{1,0:T(8,128)(2,1)S(1)}, bf16[1536,1024]{1,0:T(8,128)(2,1)}, u32[]{:S(2)}) copy-start(bf16[1536,1024]{1,0:T(8,128)(2,1)} %all-gather.11.cloned.1.call-done.grad_ref) | copy-start | bytes 9437188
  363.8 9.1 %copy-start.29 = (bf16[1536,256]{1,0:T(8,128)(2,1)S(1)}, bf16[1536,256]{1,0:T(8,128)(2,1)}, u32[]{:S(2)}) copy-start(bf16[1536,256]{1,0:T(8,128)(2,1)} %get-tuple-element.34) | copy-start | bytes 2359300
  363.8 10.9 %copy-start.26 = (bf16[1536,1024]{1,0:T(8,128)(2,1)S(1)}, bf16[1536,1024]{1,0:T(8,128)(2,1)}, u32[]{:S(2)}) copy-start(bf16[1536,1024]{1,0:T(8,128)(2,1)} %all-gather.5.cloned.1.call-done) | copy-start | bytes 9437188
  372.9 1.8 copy-start.13
  379.1 17.0 %copy-start.19 = (f32[1024]{0:T(1024)S(1)}, f32[1024]{0:T(1024)}, u32[]{:S(2)}) copy-start(f32[1024]{0:T(1024)} %param.18) | copy-start | bytes 12292
  396.1 1.7 copy-start.9
  616.7 2.2 copy-start.17
  619.0 2.4 copy-start.15
  621.4 2.5 copy-start.14
  623.9 3.1 copy-start.6
  623.9 3.1 copy-start.8
  623.9 3.1 copy-start.10
  626.4 2.3 copy-start.1
Sparse Core Ops, SparseCore 0:
  12.3 31.2 all-gather.4
  82.8 36.0 reduce-scatter.4
  120.5 28.5 all-gather.8
  151.2 28.5 all-gather.6
  198.3 37.9 reduce-scatter.8
  239.3 37.9 reduce-scatter.6
  283.8 28.5 all-gather.10
  355.8 40.2 reduce-scatter.10
  401.2 215.5 all-reduce.3

commit v2 on v1

v2 whole, which is shorter than its diff:
```python
import functools

import jax
import jax.numpy as jnp
from jax import lax
from jax.experimental import pallas as pl
from jax.experimental.pallas import tpu as pltpu
from jax.sharding import PartitionSpec as P

D = 1024
HEAD = 64
CHUNK = 128
CROP_MAX = 3072
UNROLL = 3
PACK = HEAD + 16

BF = jnp.bfloat16
F32 = jnp.float32
precise = lax.Precision.HIGHEST


def nn(a, b):
    return lax.dot_general(a, b, (((1,), (0,)), ((), ())), preferred_element_type=F32)


def nt(a, b):
    return lax.dot_general(a, b, (((1,), (1,)), ((), ())), preferred_element_type=F32)


def tn(a, b):
    return lax.dot_general(a, b, (((0,), (0,)), ((), ())), preferred_element_type=F32)


def same_head(width):
    row = lax.broadcasted_iota(jnp.int32, (width, width), 0) // HEAD
    col = lax.broadcasted_iota(jnp.int32, (width, width), 1) // HEAD
    return row == col


def lane_head(rows, width):
    return lax.broadcasted_iota(jnp.int32, (rows, width), 1) // HEAD


def causal(rows):
    row = lax.broadcasted_iota(jnp.int32, (rows, rows), 0)
    col = lax.broadcasted_iota(jnp.int32, (rows, rows), 1)
    return row >= col


def fold_heads(full, width):
    out = full[0:HEAD]
    for h in range(1, width // HEAD):
        out = out + full[h * HEAD : (h + 1) * HEAD]
    return out


def spread_heads(part, width, block):
    tall = jnp.concatenate([part] * (width // HEAD), axis=0)
    return jnp.where(block, tall, jnp.zeros_like(tall))


def pick(mask, value):
    return jnp.where(mask, value, jnp.zeros_like(value))


def vmem():
    return pl.BlockSpec(memory_space=pltpu.VMEM)


def smem():
    return pl.BlockSpec(memory_space=pltpu.SMEM)


def shape(rows, cols, kind):
    return jax.ShapeDtypeStruct((rows, cols), kind)


def qkv_body(x_ref, w_ref, valid_ref, q_ref, k_ref, v_ref):
    x = x_ref[...]
    q = nn(x, w_ref[0])
    k = nn(x, w_ref[1])
    q_ref[...] = feature(q).astype(BF)
    k_ref[...] = (feature(k) * valid_ref[...]).astype(BF)
    v_ref[...] = nn(x, w_ref[2]).astype(BF)


def project_qkv(x, w, valid):
    rows, width = x.shape[0], w.shape[2]
    return pl.pallas_call(
        qkv_body,
        out_shape=(shape(rows, width, BF),) * 3,
        in_specs=[vmem()] * 3,
        out_specs=(vmem(),) * 3,
        name="project_qkv",
    )(x, w, valid)


def forward_body(
    last_ref, spot_ref, q_ref, k_ref, v_ref, segc_ref, segr_ref, num_ref, den_ref, st_ref, ks_ref
):
    rows, width = q_ref.shape
    size = CHUNK
    block = same_head(width)
    ones_block = block.astype(BF)
    lanes = lane_head(size, width)
    lower = causal(size)
    st_ref[...] = jnp.zeros_like(st_ref)
    ks_ref[...] = jnp.zeros_like(ks_ref)

    def chunk(c):
        spot = spot_ref[c]
        at = pl.ds(pl.multiple_of(spot * size, size), size)
        q, k, v = q_ref[at, :], k_ref[at, :], v_ref[at, :]
        seg = segc_ref[at, :]
        keep = lower & (seg == segr_ref[spot])
        before, after = last_ref[c], last_ref[c + 1]
        carried = (seg == before).astype(F32)
        num = carried * nn(q, st_ref[...].astype(BF))
        den = carried * nn((q.astype(F32) * ks_ref[0:1, :]).astype(BF), ones_block)
        for h in range(width // HEAD):
            mine = lanes == h
            score = pick(keep, nt(pick(mine, q), k)).astype(BF)
            num = num + nn(score, pick(mine, v))
            den = den + nn(score, mine.astype(BF))
        num_ref[at, :] = num
        den_ref[at, :] = den
        kept = pick(seg == after, k)
        cont = (before == after).astype(F32)
        st_ref[...] = cont * st_ref[...] + pick(block, tn(kept, v))
        ks_ref[...] = cont * ks_ref[...] + jnp.sum(kept.astype(F32), axis=0, keepdims=True)

    def step(i, carry):
        for j in range(UNROLL):
            chunk(i * UNROLL + j)
        return carry

    lax.fori_loop(0, rows // size // UNROLL, step, 0)


def attend(last, spot, q, k, v, segc, segr):
    rows, width = q.shape
    return pl.pallas_call(
        forward_body,
        out_shape=(shape(rows, width, F32),) * 2,
        in_specs=[smem()] * 2 + [vmem()] * 5,
        out_specs=(vmem(),) * 2,
        scratch_shapes=[pltpu.VMEM((width, width), F32), pltpu.VMEM((8, width), F32)],
        name="attend",
    )(last, spot, q, k, v, segc, segr)


def tail_body(last_ref, k_ref, v_ref, segc_ref, out_ref):
    rows, width = k_ref.shape
    tail = last_ref[rows // CHUNK]
    kept = pick(segc_ref[...] == tail, k_ref[...])
    state = fold_heads(pick(same_head(width), tn(kept, v_ref[...])), width)
    sums = jnp.sum(kept.astype(F32), axis=0, keepdims=True)
    out_ref[0:HEAD, :] = state.astype(BF)
    out_ref[HEAD:PACK, :] = jnp.broadcast_to(sums, (PACK - HEAD, width)).astype(BF)


def tail_pack(last, k, v, segc):
    return pl.pallas_call(
        tail_body,
        out_shape=shape(PACK, k.shape[1], BF),
        in_specs=[smem()] + [vmem()] * 3,
        out_specs=vmem(),
        name="tail_pack",
    )(last, k, v, segc)


def project_body(
    first_ref, num_ref, den_ref, q_ref, pack_ref, segc_ref, valid_ref, w_ref,
    heads_ref, wide_ref, rinv_ref, out_ref
):
    rows, width = q_ref.shape
    block = same_head(width)
    state = spread_heads(pack_ref[0:HEAD, :], width, block).astype(BF)
    sums = pack_ref[HEAD : HEAD + 1, :]
    q = q_ref[...]
    opening = (segc_ref[...] == first_ref[0]).astype(F32)
    valid = valid_ref[...]
    num = num_ref[...] + opening * nn(q, state)
    den = den_ref[...] + opening * nn((q.astype(F32) * sums).astype(BF), block.astype(BF))
    rinv = valid / (den + 1e-06 + 1.0 - valid)
    wide = num * rinv
    heads = wide.astype(BF)
    heads_ref[...] = heads
    wide_ref[...] = wide
    rinv_ref[...] = rinv
    out_ref[...] = nn(heads, w_ref[...]).astype(BF)


def slot_spec(rows, cols, slot):
    return pl.BlockSpec((rows, cols), lambda i: (slot, 0))


def whole_spec(array):
    rank = array.ndim
    return pl.BlockSpec(array.shape, lambda i: (0,) * rank)


def project(slot, rows, last, num, den, q, pack, segc, valid, w):
    width = q.shape[1]
    at = lambda cols: slot_spec(rows, cols, slot)
    mine = lambda cols: slot_spec(rows, cols, 0)
    return pl.pallas_call(
        project_body,
        grid=(1,),
        out_shape=(shape(rows, width, BF), shape(rows, width, F32), shape(rows, width, F32), shape(rows, D, BF)),
        in_specs=[smem(), at(width), at(width), at(width), whole_spec(pack), at(1), at(1), whole_spec(w)],
        out_specs=(mine(width), mine(width), mine(width), mine(D)),
        name="project",
    )(last, num, den, q, pack, segc, valid, w)


def heads_back_body(
    first_ref, grad_ref, w_ref, wide_ref, rinv_ref, q_ref, segc_ref, ng_ref, dg_ref, pack_ref
):
    width = q_ref.shape[1]
    block = same_head(width)
    ones_block = block.astype(BF)
    hg = nt(grad_ref[...], w_ref[...])
    rinv = rinv_ref[...]
    ng = (hg * rinv).astype(BF)
    prod = hg * wide_ref[...]
    high = prod.astype(BF)
    low = (prod - high.astype(F32)).astype(BF)
    dg = -(nn(high, ones_block) + nn(low, ones_block)) * rinv
    ng_ref[...] = ng
    dg_ref[...] = dg
    opened = pick(segc_ref[...] == first_ref[0], q_ref[...])
    pack_ref[0:HEAD, :] = fold_heads(pick(block, tn(opened, ng)), width)
    sums = jnp.sum(opened.astype(F32) * dg, axis=0, keepdims=True)
    pack_ref[HEAD:PACK, :] = jnp.broadcast_to(sums, (PACK - HEAD, width))


def heads_back(slot, last, grad, w, wide, rinv, q, segc):
    rows, width = grad.shape[0], q.shape[1]
    at = lambda cols: slot_spec(rows, cols, slot)
    mine = lambda cols: slot_spec(rows, cols, 0)
    return pl.pallas_call(
        heads_back_body,
        grid=(1,),
        out_shape=(shape(rows, width, BF), shape(rows, width, F32), shape(PACK, width, F32)),
        in_specs=[smem(), mine(D), whole_spec(w), mine(width), mine(width), at(width), at(1)],
        out_specs=(mine(width), mine(width), slot_spec(PACK, width, 0)),
        name="heads_back",
    )(last, grad, w, wide, rinv, q, segc)


def backward_body(
    last_ref, spot_ref, q_ref, k_ref, v_ref, ng_ref, dg_ref, segc_ref, segr_ref, pack_ref,
    dq_ref, dk_ref, dv_ref, all_ref, sums_ref, st_ref, ks_ref
):
    rows, width = q_ref.shape
    size = CHUNK
    count = rows // size
    block = same_head(width)
    lanes = lane_head(size, width)
    lower = causal(size)
    st_ref[...] = spread_heads(pack_ref[0:HEAD, :], width, block)
    ks_ref[...] = jnp.broadcast_to(pack_ref[HEAD : HEAD + 1, :], ks_ref.shape)

    def collect(c):
        at = pl.ds(pl.multiple_of(spot_ref[c] * size, size), size)
        all_ref[c] = st_ref[...].astype(BF)
        sums_ref[c] = ks_ref[...]
        before, after = last_ref[c], last_ref[c + 1]
        kept = pick(segc_ref[at, :] == after, k_ref[at, :])
        cont = (before == after).astype(F32)
        st_ref[...] = cont * st_ref[...] + pick(block, tn(kept, v_ref[at, :]))
        ks_ref[...] = cont * ks_ref[...] + jnp.sum(kept.astype(F32), axis=0, keepdims=True)

    def collects(i, carry):
        for j in range(UNROLL):
            collect(i * UNROLL + j)
        return carry

    lax.fori_loop(0, count // UNROLL, collects, 0)
    st_ref[...] = jnp.zeros_like(st_ref)
    ks_ref[...] = jnp.zeros_like(ks_ref)

    def chunk(c):
        spot = spot_ref[c]
        at = pl.ds(pl.multiple_of(spot * size, size), size)
        q, k, v, ng, dg = q_ref[at, :], k_ref[at, :], v_ref[at, :], ng_ref[at, :], dg_ref[at, :]
        seg = segc_ref[at, :]
        keep = lower & (seg == segr_ref[spot])
        before, after = last_ref[c], last_ref[c + 1]
        opened = seg == before
        carried = opened.astype(F32)
        tail = (seg == after).astype(F32)
        grad_state = st_ref[...].astype(BF)
        dq = carried * (nt(ng, all_ref[c]) + dg * sums_ref[c][0:1, :])
        dk = tail * (nt(v, grad_state) + ks_ref[0:1, :])
        dv = tail * nn(k, grad_state)
        for h in range(width // HEAD):
            mine = lanes == h
            qh, kh, nh = pick(mine, q), pick(mine, k), pick(mine, ng)
            score = pick(keep, nt(qh, k)).astype(BF)
            lead = dg[:, h * HEAD : h * HEAD + 1]
            back = pick(keep, nt(nh, v) + lead).astype(BF)
            dq = dq + nn(back, kh)
            dk = dk + tn(back, qh)
            dv = dv + tn(score, nh)
        dq_ref[at, :] = (dq * jnp.minimum(q.astype(F32), 1.0)).astype(BF)
        dk_ref[at, :] = dk
        dv_ref[at, :] = dv
        cont = (before == after).astype(F32)
        st_ref[...] = cont * st_ref[...] + pick(block, tn(pick(opened, q), ng))
        ks_ref[...] = cont * ks_ref[...] + jnp.sum(carried * q.astype(F32) * dg, axis=0, keepdims=True)

    def step(i, carry):
        for j in range(UNROLL):
            chunk(count - 1 - i * UNROLL - j)
        return carry

    lax.fori_loop(0, count // UNROLL, step, 0)


def attend_back(last, spot, q, k, v, ng, dg, segc, segr, pack):
    rows, width = q.shape
    count = rows // CHUNK
    return pl.pallas_call(
        backward_body,
        out_shape=(shape(rows, width, BF), shape(rows, width, F32), shape(rows, width, F32)),
        in_specs=[smem()] * 2 + [vmem()] * 8,
        out_specs=(vmem(),) * 3,
        scratch_shapes=[
            pltpu.VMEM((count, width, width), BF),
            pltpu.VMEM((count, 8, width), F32),
            pltpu.VMEM((width, width), F32),
            pltpu.VMEM((8, width), F32),
        ],
        name="attend_back",
    )(last, spot, q, k, v, ng, dg, segc, segr, pack)


def mix_body(
    tail_ref, dq_ref, dk_ref, dv_ref, k_ref, v_ref, segc_ref, valid_ref, pack_ref, w_ref,
    mixed_ref, out_ref
):
    rows, width = k_ref.shape
    block = same_head(width)
    state = spread_heads(pack_ref[0:HEAD, :], width, block).astype(BF)
    sums = pack_ref[HEAD : HEAD + 1, :]
    tail = (segc_ref[...] == tail_ref[0]).astype(F32)
    k = k_ref[...]
    dk = dk_ref[...] + tail * (nt(v_ref[...], state) + sums)
    dv = dv_ref[...] + tail * nn(k, state)
    dq = dq_ref[...]
    dk = (valid_ref[...] * dk * jnp.minimum(k.astype(F32), 1.0)).astype(BF)
    dv = dv.astype(BF)
    mixed_ref[:, 0:width] = dq
    mixed_ref[:, width : 2 * width] = dk
    mixed_ref[:, 2 * width : 3 * width] = dv
    out_ref[...] = (nt(dq, w_ref[0]) + nt(dk, w_ref[1]) + nt(dv, w_ref[2])).astype(BF)


def mix(slot, rows, tail, dq, dk, dv, k, v, segc, valid, pack, w):
    width = k.shape[1]
    at = lambda cols: slot_spec(rows, cols, slot)
    mine = lambda cols: slot_spec(rows, cols, 0)
    return pl.pallas_call(
        mix_body,
        grid=(1,),
        out_shape=(shape(rows, 3 * width, BF), shape(rows, D, BF)),
        in_specs=[smem()] + [at(width)] * 5 + [at(1)] * 2 + [whole_spec(pack), whole_spec(w)],
        out_specs=(mine(3 * width), mine(D)),
        name="mix",
    )(tail, dq, dk, dv, k, v, segc, valid, pack, w)


def layer_norm(values, norm_gain, norm_bias):
    centre = jnp.mean(values, axis=-1, keepdims=True)
    shifted = values - centre
    spread = jnp.mean(shifted * shifted, axis=-1, keepdims=True)
    return shifted * lax.rsqrt(spread + 1e-05) * norm_gain + norm_bias


def feature(values):
    return jnp.where(values > 0, values + 1.0, jnp.exp(jnp.minimum(values, 0.0)))


def gelu_tanh(values):
    return jax.nn.gelu(values, approximate=True)


def bits_of(count):
    return [1 << b for b in range(count.bit_length() - 1)]


def swap(value, axis, bit):
    return lax.ppermute(value, axis, [(i, i ^ bit) for i in range(lax.axis_size(axis))])


def gather_slots(value):
    slots = {0: value}
    for bit in reversed(bits_of(lax.axis_size("feat"))):
        for s in sorted(slots):
            slots[s | bit] = swap(slots[s], "feat", bit)
    return [slots[s] for s in range(len(slots))]


def scatter_slots(parts):
    parts = dict(enumerate(parts))
    for bit in bits_of(lax.axis_size("feat")):
        for s in sorted(parts, reverse=True):
            if s & bit:
                got = swap(parts.pop(s).astype(BF), "feat", bit)
                parts[s ^ bit] = parts[s ^ bit].astype(F32) + got.astype(F32)
    return parts[0]


def sum_everywhere(value):
    for axis in ("feat", "rows"):
        for bit in bits_of(lax.axis_size(axis)):
            value = value + swap(value, axis, bit)
    return value


def sum_rows(value, order):
    here = lax.axis_index("rows")
    for bit in order:
        half = value.shape[0] // 2
        upper = (here & bit) != 0
        low, high = value[:half], value[half:]
        got = swap(jnp.where(upper, low, high), "rows", bit)
        value = (jnp.where(upper, high, low).astype(F32) + got.astype(F32)).astype(BF)
    for bit in reversed(order):
        upper = (here & bit) != 0
        got = swap(value, "rows", bit)
        value = jnp.concatenate([jnp.where(upper, got, value), jnp.where(upper, value, got)], axis=0)
    return value


def shifted(pack, hop, groups, reverse):
    if reverse:
        pairs = [(i, i - hop) for i in range(hop, groups)]
    else:
        pairs = [(i, i + hop) for i in range(groups - hop)]
    return lax.ppermute(pack, "rows", pairs)


def gather_carry(pack, crops_at, here, groups, reach, reverse):
    total = jnp.zeros(pack.shape, F32)
    mine = crops_at[here + 1] if reverse else crops_at[here]
    for hop in range(1, reach + 1):
        got = shifted(pack, hop, groups, reverse).astype(F32)
        other = here + hop if reverse else here - hop
        inside = (other < groups) if reverse else (other >= 0)
        at = jnp.clip(other, 0, groups - 1)
        theirs = crops_at[at] if reverse else crops_at[at + 1]
        total = total + jnp.where(inside & (theirs == mine), got, 0.0)
    return total


def on_device(
    pixels,
    qkv_weight,
    out_weight,
    up_weight,
    down_weight,
    norm1_gain,
    norm1_bias,
    norm2_gain,
    norm2_bias,
    crop_lengths,
    crop_offsets,
    pixel_mask,
    out_grad,
):
    local_rows = pixels.shape[0]
    group_rows = pixel_mask.shape[0]
    width = qkv_weight.shape[2]
    crop_count = crop_offsets.shape[0]
    groups = lax.axis_size("rows")
    members = lax.axis_size("feat")
    here = lax.axis_index("rows")
    member = lax.axis_index("feat")
    reach = min(groups - 1, -(-(CROP_MAX - 1) // group_rows))
    group_start = here * group_rows
    slot_ids = jnp.arange(members, dtype=jnp.int32) ^ member
    in_group = (slot_ids[:, None] * local_rows + jnp.arange(local_rows, dtype=jnp.int32)[None, :]).reshape(-1)
    places = group_start + in_group
    started = crop_offsets[None, :] <= places[:, None]
    crop_ends = crop_offsets + crop_lengths
    segment = jnp.sum(started.astype(jnp.int32), axis=1) - 1
    inside = jnp.sum((started & (places[:, None] < crop_ends[None, :])).astype(jnp.int32), axis=1)
    mask = jnp.concatenate(
        [
            lax.dynamic_slice_in_dim(pixel_mask, (member ^ s) * local_rows, local_rows)
            for s in range(members)
        ]
    )
    pixel_valid = (mask * inside).astype(F32)
    edges = jnp.arange(groups + 1, dtype=jnp.int32) * group_rows - 1
    crops_at = jnp.sum((crop_offsets[None, :] <= edges[:, None]).astype(jnp.int32), axis=1) - 1
    chunks = group_rows // CHUNK
    per = local_rows // CHUNK
    chunk_edges = group_start - 1 + jnp.arange(chunks + 1, dtype=jnp.int32) * CHUNK
    last = jnp.sum((crop_offsets[None, :] <= chunk_edges[:, None]).astype(jnp.int32), axis=1) - 1
    order = jnp.arange(chunks, dtype=jnp.int32)
    spot = ((order // per) ^ member) * per + order % per
    segc = segment[:, None]
    segr = segment.reshape(chunks, 1, CHUNK)
    validc = pixel_valid[:, None]
    local_valid = pixel_valid[:local_rows]
    local_segment = segment[:local_rows]

    inputs = pixels.astype(F32)
    normed, norm1_back = jax.vjp(layer_norm, inputs, norm1_gain, norm1_bias)
    normed_slots = gather_slots(normed.astype(BF))
    late_grad = lax.optimization_barrier((out_grad, normed_slots[members // 2]))[0]
    grad_slots = gather_slots(late_grad)
    made = [
        project_qkv(normed_slots[s], qkv_weight, validc[s * local_rows : (s + 1) * local_rows])
        for s in range(members)
    ]
    q, k, v = (jnp.concatenate([m[i] for m in made], axis=0) for i in range(3))
    pack = tail_pack(last, k, v, segc)
    carry = gather_carry(pack, crops_at, here, groups, reach, False)
    num, den = attend(last, spot, q, k, v, segc, segr)
    sent = {
        s: project(s, local_rows, last, num, den, q, carry, segc, validc, out_weight)
        for s in reversed(range(members))
    }
    heads_slots, wide_slots, rinv_slots, parts = ([sent[s][i] for s in range(members)] for i in range(4))
    attended = scatter_slots(parts)
    middle = inputs + attended
    normed_two, norm2_back = jax.vjp(layer_norm, middle, norm2_gain, norm2_bias)
    two_slots = gather_slots(normed_two.astype(BF))
    active_slots, hidden_slots, two_parts, branch_parts = [], [], [], []
    for s in range(members):
        hidden = nn(two_slots[s], up_weight)
        activated, gelu_back = jax.vjp(gelu_tanh, hidden)
        activated = activated.astype(BF)
        hidden_grad = gelu_back(nt(grad_slots[s], down_weight))[0].astype(BF)
        two_parts.append(nt(hidden_grad, up_weight).astype(BF))
        branch_parts.append(nn(activated, down_weight).astype(BF))
        active_slots.append(activated)
        hidden_slots.append(hidden_grad)
    normed_two_grad = scatter_slots(two_parts)
    branch = scatter_slots(branch_parts)
    grad_all = jnp.concatenate(grad_slots, axis=0)
    down_grad = tn(jnp.concatenate(active_slots, axis=0), grad_all).astype(BF)
    up_grad = tn(jnp.concatenate(two_slots, axis=0), jnp.concatenate(hidden_slots, axis=0)).astype(BF)
    down_grad = lax.psum(down_grad, "rows").astype(F32)
    up_grad = lax.psum(up_grad, "rows").astype(F32)
    result = middle + branch
    middle_part, gain2_grad, bias2_grad = norm2_back(normed_two_grad)
    middle_grad = out_grad.astype(F32) + middle_part
    middle_slots = gather_slots(middle_grad.astype(BF))
    backs = [
        heads_back(s, last, middle_slots[s], out_weight, wide_slots[s], rinv_slots[s], q, segc)
        for s in range(members)
    ]
    ng, dg = (jnp.concatenate([b[i] for b in backs], axis=0) for i in range(2))
    grad_pack = functools.reduce(jnp.add, [b[2] for b in backs]).astype(BF)
    grad_carry = gather_carry(grad_pack, crops_at, here, groups, reach, True)
    out_weight_grad = tn(jnp.concatenate(heads_slots, axis=0), jnp.concatenate(middle_slots, axis=0))
    dq, dk, dv = attend_back(last, spot, q, k, v, ng, dg, segc, segr, carry)
    mixes = {
        s: mix(s, local_rows, last[-1:], dq, dk, dv, k, v, segc, validc, grad_carry, qkv_weight)
        for s in reversed(range(members))
    }
    normed_grad = scatter_slots([mixes[s][1] for s in range(members)])
    mixed_grad = jnp.concatenate([mixes[s][0] for s in range(members)], axis=0)
    qkv_grad = tn(mixed_grad, jnp.concatenate(normed_slots, axis=0)).astype(BF)
    bits = bits_of(groups)
    turned = bits[1:] + bits[:1]
    cut = 3 * width // 2
    qkv_grad = jnp.concatenate([sum_rows(qkv_grad[:cut], bits), sum_rows(qkv_grad[cut:], turned)], axis=0)
    qkv_grad = jnp.swapaxes(qkv_grad.reshape(3, width, D), 1, 2).astype(F32)
    out_weight_grad = sum_rows(out_weight_grad.astype(BF), turned).astype(F32)
    input_part, gain1_grad, bias1_grad = norm1_back(normed_grad)
    pixels_grad = (middle_grad + input_part).astype(BF)
    crop_onehot = (
        local_segment[:, None] == jnp.arange(crop_count, dtype=jnp.int32)[None, :]
    ).astype(F32)
    squares = (
        jnp.stack(
            [
                jnp.sum(result * result, axis=1),
                jnp.sum(attended * attended, axis=1),
                jnp.sum(branch * branch, axis=1),
                jnp.ones((local_rows,), F32),
            ]
        )
        * local_valid[None, :]
    )
    crop_sums = jnp.dot(squares, crop_onehot, precision=precise)
    early = sum_everywhere(jnp.concatenate([gain2_grad, bias2_grad, crop_sums.reshape(-1)]))
    gain2_grad, bias2_grad = early[:D], early[D : 2 * D]
    crop_sums = early[2 * D :].reshape(4, crop_count)
    late = sum_everywhere(jnp.concatenate([gain1_grad, bias1_grad]))
    gain1_grad, bias1_grad = late[:D], late[D:]
    crop_rms = jnp.sqrt(crop_sums[:3] / (D * jnp.maximum(crop_sums[3], 1.0))[None, :])
    return (
        result.astype(BF),
        pixels_grad,
        qkv_grad,
        out_weight_grad,
        up_grad,
        down_grad,
        gain1_grad,
        bias1_grad,
        gain2_grad,
        bias2_grad,
        crop_rms,
    )


def solution(mesh):
    split = P(("rows", "feat"), None)
    qkv, rows_feat, cols_feat = P(None, None, "feat"), P("feat", None), P(None, "feat")
    in_specs = (
        (split, qkv, rows_feat, cols_feat, rows_feat) + (P(),) * 6 + (P("rows"), split)
    )
    out_specs = (split, split, qkv, rows_feat, cols_feat, rows_feat) + (P(),) * 5
    return jax.shard_map(
        on_device, mesh=mesh, in_specs=in_specs, out_specs=out_specs, check_vma=False
    )
```

time: 643 us -> 470 us (0.73)
  waiting for transfers between devices: 397 us -> 176 us
  Pallas kernels: 50.7 us -> 94.1 us
  blocking collectives: 42.9 us -> 0 us
  starting transfers between devices: 10.4 us -> 49.1 us
  matrix products: 73 us -> 46.9 us
  other arithmetic: 31.3 us -> 48.8 us
  local copies, waits for them, and re-layouts: 9.98 us -> 26.7 us
    ppermute x0 -> x52, waiting for transfers between devices: none -> 154 us  [swap(): lax.ppermute(value, axis, [(i, i ^ bit) for i in range(lax.axis_size(axis...]
    psum x1, waiting for transfers between devices: 175 us -> 21.8 us  [on_device(): up_grad = lax.psum(up_grad, 'rows').astype(F32)]
    reduce_scatter x4 -> x0, waiting for transfers between devices: 121 us -> none  [the longest x1 41 us: on_device(): lax.psum_scatter(nn(activated_low, down_weight).astype(BF), 'feat', scatt...]
    all_gather x4 -> x0, waiting for transfers between devices: 101 us -> none  [the longest x1 28.6 us: on_device(): lax.all_gather(middle_grad.astype(BF), 'feat', axis=0, tiled=True)]
    pallas_call x6 -> x19, Pallas kernels: 50.7 us -> 94.1 us  [the longest x1 20.6 us: attend_back(): pl.pallas_call(backward_body, out_shape=(shape(rows, width, BF), shape(ro...]
    psum x1 -> x0, blocking collectives: 42.9 us -> none  [on_device(): lax.psum((crop_sums, crop_counts, gain1_grad, bias1_grad, gain2_grad, bia...]
    ppermute x0 -> x52, starting transfers between devices: none -> 39.6 us  [swap(): lax.ppermute(value, axis, [(i, i ^ bit) for i in range(lax.axis_size(axis...]
    dot_general x5 -> x8, matrix products: 31.4 us -> 12 us  [nn(): lax.dot_general(a, b, (((1,), (0,)), ((), ())), preferred_element_type=F32)]
  transfers between devices with their start and end apart: 13 -> 57, of which waited for: 9 -> 21; matrix products, arithmetic and copies ran while one was open for 9% -> 22% of each run, Pallas kernels for 4% -> 18%
where the time goes in v2:
time: 470 us; the launch traced here: 463 us
  waiting for transfers between devices  176 us (37%)
  Pallas kernels  94.1 us (20%)
  starting transfers between devices  49.1 us (10%)
  other arithmetic  48.8 us (10%)
  matrix products  46.9 us (10%)
  local copies, waits for them, and re-layouts  26.7 us (6%)
  between operations  20.8 us (4%)
    ppermute x52, waiting for transfers between devices, swap(): lax.ppermute(value, axis, [(i, i ^ bit) for i in range(lax.axis_size(axis...  154 us
    ppermute x52, starting transfers between devices, swap(): lax.ppermute(value, axis, [(i, i ^ bit) for i in range(lax.axis_size(axis...  39.6 us
    psum x1, waiting for transfers between devices, on_device(): up_grad = lax.psum(up_grad, 'rows').astype(F32)  21.8 us
    pallas_call x1, Pallas kernels, attend_back(): pl.pallas_call(backward_body, out_shape=(shape(rows, width, BF), shape(ro...  20.6 us
    dot_general x4, matrix products, tn(): lax.dot_general(a, b, (((0,), (0,)), ((), ())), preferred_element_type=F32)  20.2 us
    pallas_call x4, Pallas kernels, mix(): pl.pallas_call(mix_body, grid=(1,), out_shape=(shape(rows, 3 * width, BF)...  18.7 us
    dot_general x8, matrix products, nt(): lax.dot_general(a, b, (((1,), (1,)), ((), ())), preferred_element_type=F32)  14.5 us
    pallas_call x1, Pallas kernels, attend(): pl.pallas_call(forward_body, out_shape=(shape(rows, width, F32),) * 2, in...  13.5 us
  transfers between devices with their start and end apart: 57, of which 21 were waited for; matrix products, arithmetic and copies ran while one was open for 22% of the time, Pallas kernels for 18%

profile of v2, /device:TPU:0, one launch (start us, length us, event | category | flops | bytes accessed | tf_op | source)
XLA Modules:
  0.0 462.7 jit_solution(15692964447421533152)
XLA Ops:
  11.5 3.0 collective-permute-start.1
  16.6 3.2 project_qkv.4
  30.8 2.3 fusion.119.valid_ref
  34.1 3.2 project_qkv.6
  37.3 3.2 project_qkv.5
  45.2 3.2 project_qkv.7
  51.7 2.9 tail_pack.1
  54.6 3.5 collective-permute-start.4
  58.1 3.4 collective-permute-start.3
  62.4 13.5 %attend.1 = (f32[1536,256]{1,0:T(8,128)}, f32[1536,256]{1,0:T(8,128)}) custom-call(s32[13]{0:T(128)} %broadcast_add_fusion.2.last_ref.first_ref, s32[12]{0:T(128)} %fusion.134.spot_ref, bf16[1536,256]{1,0:T(8,128)(2,1)} %copy-done.2, bf16[1536,256]{1,0:T(8,128)(2,1)} %constant_dynamic-update-slice_fusion.4.k_ref, ...), custom_call_target="tpu_custom_call" | custom-call | tf_op jit(solution)/shard_map/attend/pallas_call | solution.py:142
  76.6 3.1 project.7
  80.2 3.1 project.6
  83.3 3.1 project.5
  86.7 2.3 add_convert_fusion.5
  93.9 4.0 fusion.155
  97.9 2.5 collective-permute-done.16
  100.4 3.2 project.4
  103.5 13.3 %collective-permute-done.7 = bf16[384,1024]{1,0:T(8,128)(2,1)} collective-permute-done((bf16[384,1024]{1,0:T(8,128)(2,1)}, bf16[384,1024]{1,0:T(8,128)(2,1)}, u32[]{:S(2)}, u32[]{:S(2)}) %collective-permute-start.7) | collective-permute-done | bytes 786464 | tf_op jit(solution)/shard_map/ppermute | solution.py:395
  116.8 2.2 fusion.149
  121.4 2.1 fusion.157
  123.6 2.1 fusion.156
  125.7 2.1 fusion.158
  127.9 11.5 %collective-permute-done.10 = bf16[384,1024]{1,0:T(8,128)(2,1)S(1)} collective-permute-done((bf16[384,1024]{1,0:T(8,128)(2,1)S(1)}, bf16[384,1024]{1,0:T(8,128)(2,1)S(1)}, u32[]{:S(2)}, u32[]{:S(2)}) %collective-permute-start.10) | collective-permute-done | bytes 786464 | tf_op jit(solution)/shard_map/ppermute | solution.py:395
  144.9 2.3 fusion.104
  161.1 13.1 %collective-permute-done.13 = bf16[384,1024]{1,0:T(8,128)(2,1)S(1)} collective-permute-done((bf16[384,1024]{1,0:T(8,128)(2,1)S(1)}, bf16[384,1024]{1,0:T(8,128)(2,1)S(1)}, u32[]{:S(2)}, u32[]{:S(2)}) %collective-permute-start.13) | collective-permute-done | bytes 786464 | tf_op jit(solution)/shard_map/ppermute | solution.py:395
  174.2 16.4 %collective-permute-done.19 = bf16[384,1024]{1,0:T(8,128)(2,1)S(1)} collective-permute-done((bf16[384,1024]{1,0:T(8,128)(2,1)S(1)}, bf16[384,1024]{1,0:T(8,128)(2,1)S(1)}, u32[]{:S(2)}, u32[]{:S(2)}) %collective-permute-start.19) | collective-permute-done | bytes 786464 | tf_op jit(solution)/shard_map/ppermute | solution.py:395
  190.6 2.1 multiply_reduce_fusion.3
  193.2 3.0 fusion.148
  196.9 3.1 collective-permute-done.52
  201.6 2.4 fusion.111.grad_ref
  206.3 6.9 %fusion.57 = bf16[1024,1024]{1,0:T(8,128)(2,1)} fusion(bf16[384,1024]{1,0:T(8,128)(2,1)} %collective-permute-done.17, bf16[384,1024]{1,0:T(8,128)(2,1)} %collective-permute-done.16, bf16[384,1024]{1,0:T(8,128)(2,1)} %collective-permute-done.14, bf16[384,1024]{1,0:T(8,128)(2,1)} %param.25, bf16[384,1024]{1,0:T(8,128)(2,1)S(1)} %copy-done.63, ...), kind=kOutput, calls=%fused_computation.70 | convolution fusion | flops 3247439872 | bytes 8388608 | tf_op jit(solution)/shard_map/dot_general | solution.py:31
  213.5 9.3 %collective-permute-done.21.grad_ref = bf16[384,1024]{1,0:T(8,128)(2,1)} collective-permute-done((bf16[384,1024]{1,0:T(8,128)(2,1)}, bf16[384,1024]{1,0:T(8,128)(2,1)}, u32[]{:S(2)}, u32[]{:S(2)}) %collective-permute-start.21) | collective-permute-done | bytes 786464 | tf_op jit(solution)/shard_map/ppermute | solution.py:395
  222.9 4.9 %fusion.62 = bf16[1024,1024]{1,0:T(8,128)(2,1)} fusion(bf16[384,1024]{1,0:T(8,128)(2,1)S(1)} %copy-done.59, bf16[384,1024]{1,0:T(8,128)(2,1)S(1)} %copy-done.55, bf16[384,1024]{1,0:T(8,128)(2,1)S(1)} %copy-done.57, bf16[384,1024]{1,0:T(8,128)(2,1)S(1)} %copy-done.65, bf16[384,1024]{1,0:T(8,128)(2,1)S(1)} %copy-done.51, ...), kind=kOutput, calls=%fused_computation.71 | convolution fusion | flops 3247439872 | bytes 8388608 | tf_op jit(solution)/shard_map/dot_general | solution.py:31
  227.8 3.2 heads_back.4
  232.4 3.3 heads_back.6
  236.6 3.2 heads_back.5
  239.9 3.4 heads_back.7
  246.8 3.1 fusion.107
  249.9 3.3 collective-permute-start.40
  255.9 20.6 %attend_back.1 = (bf16[1536,256]{1,0:T(8,128)(2,1)}, f32[1536,256]{1,0:T(8,128)}, f32[1536,256]{1,0:T(8,128)}) custom-call(s32[13]{0:T(128)} %broadcast_add_fusion.2.last_ref.first_ref, s32[12]{0:T(128)} %fusion.134.spot_ref, bf16[1536,256]{1,0:T(8,128)(2,1)} %copy-done.2, bf16[1536,256]{1,0:T(8,128)(2,1)} %constant_dynamic-update-slice_fusion.4.k_ref, ...), custom_call_target="tpu_custom_call" | custom-call | tf_op jit(solution)/shard_map/attend_back/pallas_call | solution.py:325
  277.1 4.6 mix.7
  281.7 4.6 mix.6
  286.3 4.7 %mix.5 = (bf16[384,768]{1,0:T(8,128)(2,1)}, bf16[384,1024]{1,0:T(8,128)(2,1)}) custom-call(s32[1]{0:T(128)} %slice.137.tail_ref, bf16[1536,256]{1,0:T(8,128)(2,1)} %get-tuple-element.100.dq_ref, f32[1536,256]{1,0:T(8,128)} %get-tuple-element.101.dk_ref, f32[1536,256]{1,0:T(8,128)} %get-tuple-element.102.dv_ref, ...), custom_call_target="tpu_custom_call" | custom-call | tf_op jit(solution)/shard_map/mix/pallas_call | solution.py:365
  291.0 4.9 %mix.4 = (bf16[384,768]{1,0:T(8,128)(2,1)}, bf16[384,1024]{1,0:T(8,128)(2,1)}) custom-call(s32[1]{0:T(128)} %slice.137.tail_ref, bf16[1536,256]{1,0:T(8,128)(2,1)} %get-tuple-element.100.dq_ref, f32[1536,256]{1,0:T(8,128)} %get-tuple-element.101.dk_ref, f32[1536,256]{1,0:T(8,128)} %get-tuple-element.102.dv_ref, ...), custom_call_target="tpu_custom_call" | custom-call | tf_op jit(solution)/shard_map/mix/pallas_call | solution.py:365
  295.9 5.2 %fusion.69 = bf16[768,1024]{1,0:T(8,128)(2,1)S(1)} fusion(bf16[384,1024]{1,0:T(8,128)(2,1)} %collective-permute-done.2.x_ref, bf16[384,1024]{1,0:T(8,128)(2,1)} %collective-permute-done.1.x_ref, bf16[384,1024]{1,0:T(8,128)(2,1)} %collective-permute-done.x_ref, bf16[384,1024]{1,0:T(8,128)(2,1)} %fusion.75.x_ref, bf16[384,768]{1,0:T(8,128)(2,1)} %get-tuple-element.114, ...), kind=kOutput, calls=%fused_computation.74 | convolution fusion | flops 2438725632 | bytes 7077888 | tf_op jit(solution)/shard_map/dot_general | solution.py:31
  302.2 3.3 collective-permute-start.41
  307.5 8.8 %collective-permute-done.41 = bf16[64,1024]{1,0:T(8,128)(2,1)S(1)} collective-permute-done((bf16[64,1024]{1,0:T(8,128)(2,1)S(1)}, bf16[64,1024]{1,0:T(8,128)(2,1)S(1)}, u32[]{:S(2)}, u32[]{:S(2)}) %collective-permute-start.41) | collective-permute-done | bytes 131104 | tf_op jit(solution)/shard_map/ppermute | solution.py:395
  317.1 4.5 collective-permute-done.34
  324.9 2.9 collective-permute-done.43
  329.5 14.9 %collective-permute-done.35 = bf16[96,1024]{1,0:T(8,128)(2,1)S(1)} collective-permute-done((bf16[96,1024]{1,0:T(8,128)(2,1)S(1)}, bf16[96,1024]{1,0:T(8,128)(2,1)S(1)}, u32[]{:S(2)}, u32[]{:S(2)}) %collective-permute-start.35) | collective-permute-done | bytes 196640 | tf_op jit(solution)/shard_map/ppermute | solution.py:395
  346.1 6.6 %collective-permute-done.44 = bf16[64,1024]{1,0:T(8,128)(2,1)S(1)} collective-permute-done((bf16[64,1024]{1,0:T(8,128)(2,1)S(1)}, bf16[64,1024]{1,0:T(8,128)(2,1)S(1)}, u32[]{:S(2)}, u32[]{:S(2)}) %collective-permute-start.44) | collective-permute-done | bytes 131104 | tf_op jit(solution)/shard_map/ppermute | solution.py:395
  356.1 2.1 collective-permute-done.37
  359.1 13.3 %collective-permute-done.31 = bf16[48,1024]{1,0:T(8,128)(2,1)S(1)} collective-permute-done((bf16[48,1024]{1,0:T(8,128)(2,1)S(1)}, bf16[48,1024]{1,0:T(8,128)(2,1)S(1)}, u32[]{:S(2)}, u32[]{:S(2)}) %collective-permute-start.31) | collective-permute-done | bytes 98336 | tf_op jit(solution)/shard_map/ppermute | solution.py:395
  375.4 9.5 %collective-permute-done.38 = bf16[96,1024]{1,0:T(8,128)(2,1)S(1)} collective-permute-done((bf16[96,1024]{1,0:T(8,128)(2,1)S(1)}, bf16[96,1024]{1,0:T(8,128)(2,1)S(1)}, u32[]{:S(2)}, u32[]{:S(2)}) %collective-permute-start.38) | collective-permute-done | bytes 196640 | tf_op jit(solution)/shard_map/ppermute | solution.py:395
  385.8 14.9 %collective-permute-done.32 = bf16[96,1024]{1,0:T(8,128)(2,1)S(1)} collective-permute-done((bf16[96,1024]{1,0:T(8,128)(2,1)S(1)}, bf16[96,1024]{1,0:T(8,128)(2,1)S(1)}, u32[]{:S(2)}, u32[]{:S(2)}) %collective-permute-start.32) | collective-permute-done | bytes 196640 | tf_op jit(solution)/shard_map/ppermute | solution.py:395
  403.6 21.8 %all-reduce.3.cloned.1.call-done = (bf16[1024,1024]{1,0:T(8,128)(2,1)}, bf16[1024,1024]{1,0:T(8,128)(2,1)}) async-done(((bf16[1024,1024]{1,0:T(8,128)(2,1)}, bf16[1024,1024]{1,0:T(8,128)(2,1)}), (bf16[1024,1024]{1,0:T(8,128)(2,1)}, bf16[1024,1024]{1,0:T(8,128)(2,1)})) %all-reduce.3.cloned.1.call-update) | async-done | bytes 4194320 | tf_op jit(solution)/shard_map/psum | solution.py:550
  425.4 4.2 convert_element_type.384
  429.6 2.5 convert_element_type.386
  434.6 2.3 fusion.76
  437.1 2.1 copy.93
  440.7 2.2 collective-permute-done.47
  444.3 2.4 fusion.147
  447.3 3.1 collective-permute-done.49
  450.6 2.6 add_convert_fusion
  (361 shorter events, 94.2 us)
Async XLA Ops:
  7.2 132.2 %copy-start = (bf16[1024,1024]{1,0:T(8,128)(2,1)S(1)}, bf16[1024,1024]{1,0:T(8,128)(2,1)}, u32[]{:S(2)}) copy-start(bf16[1024,1024]{1,0:T(8,128)(2,1)} %param.16) | copy-start | bytes 6291460
  7.3 418.1 %all-reduce.3.cloned.1.call-start = ((), (), s32[]{:S(2)}) async-start(), calls=%async_computation | async-start | bytes 8388608 | tf_op jit(solution)/shard_map/psum | solution.py:550
  11.5 21.5 %collective-permute-start.1 = (bf16[384,1024]{1,0:T(8,128)(2,1)}, bf16[384,1024]{1,0:T(8,128)(2,1)}, u32[]{:S(2)}, u32[]{:S(2)}) collective-permute-start(bf16[384,1024]{1,0:T(8,128)(2,1)} %fusion.75.x_ref), channel_id=1, source_target_pairs={{0,2},{1,3},{2,0},{3,1},{4,6},{5,7},{6,4},{7,5},{8,10},{9,11},{10,... | collective-permute-start | bytes 2359304 | tf_op jit(solution)/shard_map/ppermute | solution.py:395
  14.5 22.8 %collective-permute-start = (bf16[384,1024]{1,0:T(8,128)(2,1)}, bf16[384,1024]{1,0:T(8,128)(2,1)}, u32[]{:S(2)}, u32[]{:S(2)}) collective-permute-start(bf16[384,1024]{1,0:T(8,128)(2,1)} %fusion.75.x_ref), channel_id=1, source_target_pairs={{0,1},{1,0},{2,3},{3,2},{4,5},{5,4},{6,7},{7,6},{8,9},{9,8},{10,11... | collective-permute-start | bytes 2359304 | tf_op jit(solution)/shard_map/ppermute | solution.py:395
  15.8 75.4 %copy-start.34 = (s32[1536]{0:T(1024)}, s32[1536]{0:T(1024)S(1)}, u32[]{:S(2)}) copy-start(s32[1536]{0:T(1024)S(1)} %broadcast_add_fusion) | copy-start | bytes 18436
  33.1 12.2 %collective-permute-start.2 = (bf16[384,1024]{1,0:T(8,128)(2,1)}, bf16[384,1024]{1,0:T(8,128)(2,1)}, u32[]{:S(2)}, u32[]{:S(2)}) collective-permute-start(bf16[384,1024]{1,0:T(8,128)(2,1)} %collective-permute-done.1.x_ref), channel_id=1, source_target_pairs={{0,1},{1,0},{2,3},{3,2},{4,5},{5,4},{6,7},{7,6},{8,9},{9,8},{10,11... | collective-permute-start | bytes 2359304 | tf_op jit(solution)/shard_map/ppermute | solution.py:395
  54.6 21.3 %collective-permute-start.4 = (bf16[80,256]{1,0:T(8,128)(2,1)}, bf16[80,256]{1,0:T(8,128)(2,1)S(1)}, u32[]{:S(2)}, u32[]{:S(2)}) collective-permute-start(bf16[80,256]{1,0:T(8,128)(2,1)} %tail_pack.1), channel_id=1, source_target_pairs={{0,8},{4,12},{8,16},{12,20},{16,24},{20,28},{1,9},{5,13},{9,17},{1... | collective-permute-start | bytes 122888 | tf_op jit(solution)/shard_map/ppermute | solution.py:443
  58.1 17.9 %collective-permute-start.3 = (bf16[80,256]{1,0:T(8,128)(2,1)}, bf16[80,256]{1,0:T(8,128)(2,1)S(1)}, u32[]{:S(2)}, u32[]{:S(2)}) collective-permute-start(bf16[80,256]{1,0:T(8,128)(2,1)} %tail_pack.1), channel_id=1, source_target_pairs={{0,4},{4,8},{8,12},{12,16},{16,20},{20,24},{24,28},{1,5},{5,9},{9,... | collective-permute-start | bytes 122888 | tf_op jit(solution)/shard_map/ppermute | solution.py:443
  79.7 7.0 %collective-permute-start.6 = (bf16[384,1024]{1,0:T(8,128)(2,1)}, bf16[384,1024]{1,0:T(8,128)(2,1)S(1)}, u32[]{:S(2)}, u32[]{:S(2)}) collective-permute-start(bf16[384,1024]{1,0:T(8,128)(2,1)} %get-tuple-element.82), channel_id=1, source_target_pairs={{0,1},{1,0},{2,3},{3,2},{4,5},{5,4},{6,7},{7,6},{8,9},{9,8},{10,11... | collective-permute-start | bytes 2359304 | tf_op jit(solution)/shard_map/ppermute | solution.py:395
  79.7 20.7 %collective-permute-start.16 = (bf16[384,1024]{1,0:T(8,128)(2,1)}, bf16[384,1024]{1,0:T(8,128)(2,1)}, u32[]{:S(2)}, u32[]{:S(2)}) collective-permute-start(bf16[384,1024]{1,0:T(8,128)(2,1)} %param.25), channel_id=1, source_target_pairs={{0,2},{1,3},{2,0},{3,1},{4,6},{5,7},{6,4},{7,5},{8,10},{9,11},{10,... | collective-permute-start | bytes 2359304 | tf_op jit(solution)/shard_map/ppermute | solution.py:395
  86.5 17.0 %collective-permute-start.5 = (bf16[384,1024]{1,0:T(8,128)(2,1)}, bf16[384,1024]{1,0:T(8,128)(2,1)}, u32[]{:S(2)}, u32[]{:S(2)}) collective-permute-start(bf16[384,1024]{1,0:T(8,128)(2,1)} %get-tuple-element.80), channel_id=1, source_target_pairs={{0,1},{1,0},{2,3},{3,2},{4,5},{5,4},{6,7},{7,6},{8,9},{9,8},{10,11... | collective-permute-start | bytes 2359304 | tf_op jit(solution)/shard_map/ppermute | solution.py:395
  89.0 27.8 %collective-permute-start.7 = (bf16[384,1024]{1,0:T(8,128)(2,1)}, bf16[384,1024]{1,0:T(8,128)(2,1)}, u32[]{:S(2)}, u32[]{:S(2)}) collective-permute-start(bf16[384,1024]{1,0:T(8,128)(2,1)} %add_convert_fusion.5), channel_id=1, source_target_pairs={{0,2},{1,3},{2,0},{3,1},{4,6},{5,7},{6,4},{7,5},{8,10},{9,11},{10,... | collective-permute-start | bytes 2359304 | tf_op jit(solution)/shard_map/ppermute | solution.py:395
  93.8 29.7 %collective-permute-start.14 = (bf16[384,1024]{1,0:T(8,128)(2,1)}, bf16[384,1024]{1,0:T(8,128)(2,1)}, u32[]{:S(2)}, u32[]{:S(2)}) collective-permute-start(bf16[384,1024]{1,0:T(8,128)(2,1)} %param.25), channel_id=1, source_target_pairs={{0,1},{1,0},{2,3},{3,2},{4,5},{5,4},{6,7},{7,6},{8,9},{9,8},{10,11... | collective-permute-start | bytes 2359304 | tf_op jit(solution)/shard_map/ppermute | solution.py:395
  100.4 25.4 %collective-permute-start.17 = (bf16[384,1024]{1,0:T(8,128)(2,1)}, bf16[384,1024]{1,0:T(8,128)(2,1)}, u32[]{:S(2)}, u32[]{:S(2)}) collective-permute-start(bf16[384,1024]{1,0:T(8,128)(2,1)} %collective-permute-done.16), channel_id=1, source_target_pairs={{0,1},{1,0},{2,3},{3,2},{4,5},{5,4},{6,7},{7,6},{8,9},{9,8},{10,11... | collective-permute-start | bytes 2359304 | tf_op jit(solution)/shard_map/ppermute | solution.py:395
  119.0 71.6 %copy-start.3 = (f32[384,1024]{1,0:T(8,128)}, f32[384,1024]{1,0:T(8,128)S(1)}, u32[]{:S(2)}) copy-start(f32[384,1024]{1,0:T(8,128)S(1)} %get-tuple-element.138) | copy-start | bytes 4718596
  120.1 36.8 %copy-start.14 = (bf16[384,1024]{1,0:T(8,128)(2,1)}, bf16[384,1024]{1,0:T(8,128)(2,1)S(1)}, u32[]{:S(2)}) copy-start(bf16[384,1024]{1,0:T(8,128)(2,1)S(1)} %add_convert_fusion.4) | copy-start | bytes 2359300
  120.1 19.2 %collective-permute-start.10 = (bf16[384,1024]{1,0:T(8,128)(2,1)S(1)}, bf16[384,1024]{1,0:T(8,128)(2,1)S(1)}, u32[]{:S(2)}, u32[]{:S(2)}) collective-permute-start(bf16[384,1024]{1,0:T(8,128)(2,1)S(1)} %add_convert_fusion.4), channel_id=1, source_target_pairs={{0,2},{1,3},{2,0},{3,1},{4,6},{5,7},{6,4},{7,5},{8,10},{9,11},{10,... | collective-permute-start | bytes 2359304 | tf_op jit(solution)/shard_map/ppermute | solution.py:395
  120.8 18.6 %collective-permute-start.8 = (bf16[384,1024]{1,0:T(8,128)(2,1)S(1)}, bf16[384,1024]{1,0:T(8,128)(2,1)S(1)}, u32[]{:S(2)}, u32[]{:S(2)}) collective-permute-start(bf16[384,1024]{1,0:T(8,128)(2,1)S(1)} %add_convert_fusion.4), channel_id=1, source_target_pairs={{0,1},{1,0},{2,3},{3,2},{4,5},{5,4},{6,7},{7,6},{8,9},{9,8},{10,11... | collective-permute-start | bytes 2359304 | tf_op jit(solution)/shard_map/ppermute | solution.py:395
  139.4 5.5 %collective-permute-start.11 = (bf16[384,1024]{1,0:T(8,128)(2,1)S(1)}, bf16[384,1024]{1,0:T(8,128)(2,1)S(1)}, u32[]{:S(2)}, u32[]{:S(2)}) collective-permute-start(bf16[384,1024]{1,0:T(8,128)(2,1)S(1)} %collective-permute-done.10), channel_id=1, source_target_pairs={{0,1},{1,0},{2,3},{3,2},{4,5},{5,4},{6,7},{7,6},{8,9},{9,8},{10,11... | collective-permute-start | bytes 2359304 | tf_op jit(solution)/shard_map/ppermute | solution.py:395
  143.2 17.8 %collective-permute-start.9 = (bf16[384,1024]{1,0:T(8,128)(2,1)S(1)}, bf16[384,1024]{1,0:T(8,128)(2,1)S(1)}, u32[]{:S(2)}, u32[]{:S(2)}) collective-permute-start(bf16[384,1024]{1,0:T(8,128)(2,1)S(1)} %convolution_convert_fusion.6), channel_id=1, source_target_pairs={{0,1},{1,0},{2,3},{3,2},{4,5},{5,4},{6,7},{7,6},{8,9},{9,8},{10,11... | collective-permute-start | bytes 2359304 | tf_op jit(solution)/shard_map/ppermute | solution.py:395
  144.8 16.2 %collective-permute-start.15 = (bf16[384,1024]{1,0:T(8,128)(2,1)S(1)}, bf16[384,1024]{1,0:T(8,128)(2,1)S(1)}, u32[]{:S(2)}, u32[]{:S(2)}) collective-permute-start(bf16[384,1024]{1,0:T(8,128)(2,1)S(1)} %convolution_convert_fusion.2), channel_id=1, source_target_pairs={{0,1},{1,0},{2,3},{3,2},{4,5},{5,4},{6,7},{7,6},{8,9},{9,8},{10,11... | collective-permute-start | bytes 2359304 | tf_op jit(solution)/shard_map/ppermute | solution.py:395
  149.1 3.6 collective-permute-start.12
  150.7 3.7 collective-permute-start.18
  153.8 20.4 %collective-permute-start.13 = (bf16[384,1024]{1,0:T(8,128)(2,1)S(1)}, bf16[384,1024]{1,0:T(8,128)(2,1)S(1)}, u32[]{:S(2)}, u32[]{:S(2)}) collective-permute-start(bf16[384,1024]{1,0:T(8,128)(2,1)S(1)} %add_convert_fusion.3), channel_id=1, source_target_pairs={{0,2},{1,3},{2,0},{3,1},{4,6},{5,7},{6,4},{7,5},{8,10},{9,11},{10,... | collective-permute-start | bytes 2359304 | tf_op jit(solution)/shard_map/ppermute | solution.py:395
  155.4 35.2 %collective-permute-start.19 = (bf16[384,1024]{1,0:T(8,128)(2,1)S(1)}, bf16[384,1024]{1,0:T(8,128)(2,1)S(1)}, u32[]{:S(2)}, u32[]{:S(2)}) collective-permute-start(bf16[384,1024]{1,0:T(8,128)(2,1)S(1)} %add_convert_fusion.2), channel_id=1, source_target_pairs={{0,2},{1,3},{2,0},{3,1},{4,6},{5,7},{6,4},{7,5},{8,10},{9,11},{10,... | collective-permute-start | bytes 2359304 | tf_op jit(solution)/shard_map/ppermute | solution.py:395
  159.9 30.7 %copy-start.10 = (bf16[384,1024]{1,0:T(8,128)(2,1)}, bf16[384,1024]{1,0:T(8,128)(2,1)S(1)}, u32[]{:S(2)}) copy-start(bf16[384,1024]{1,0:T(8,128)(2,1)S(1)} %convolution_convert_fusion.3) | copy-start | bytes 2359300
  161.0 31.8 %slice-start = ((s32[1536]{0:T(1024)}), s32[384]{0:T(512)S(1)}, s32[]{:S(2)}) async-start(s32[1536]{0:T(1024)} %copy-done.34), calls=%async_computation.1 | async-start | bytes 4096 | tf_op jit(solution)/shard_map/slice | solution.py:510
  161.0 31.7 %copy-start.8 = (bf16[384,1024]{1,0:T(8,128)(2,1)}, bf16[384,1024]{1,0:T(8,128)(2,1)S(1)}, u32[]{:S(2)}) copy-start(bf16[384,1024]{1,0:T(8,128)(2,1)S(1)} %collective-permute-done.15) | copy-start | bytes 2359300
  193.2 3.1 collective-permute-start.51
  196.2 3.8 collective-permute-start.52
  200.0 4.5 collective-permute-start.53
  204.0 18.8 %collective-permute-start.21 = (bf16[384,1024]{1,0:T(8,128)(2,1)}, bf16[384,1024]{1,0:T(8,128)(2,1)}, u32[]{:S(2)}, u32[]{:S(2)}) collective-permute-start(bf16[384,1024]{1,0:T(8,128)(2,1)} %fusion.111.grad_ref), channel_id=1, source_target_pairs={{0,2},{1,3},{2,0},{3,1},{4,6},{5,7},{6,4},{7,5},{8,10},{9,11},{10,... | collective-permute-start | bytes 2359304 | tf_op jit(solution)/shard_map/ppermute | solution.py:395
  204.6 8.6 %collective-permute-start.54 = (f32[2176]{0:T(1024)S(1)}, f32[2176]{0:T(1024)S(1)}, u32[]{:S(2)}, u32[]{:S(2)}) collective-permute-start(f32[2176]{0:T(1024)S(1)} %add.389), channel_id=1, source_target_pairs={{0,8},{4,12},{8,0},{12,4},{16,24},{20,28},{24,16},{28,20},{1,9},{5... | collective-permute-start | bytes 26120 | tf_op jit(solution)/shard_map/ppermute | solution.py:395
  213.2 22.6 %collective-permute-start.20 = (bf16[384,1024]{1,0:T(8,128)(2,1)}, bf16[384,1024]{1,0:T(8,128)(2,1)S(1)}, u32[]{:S(2)}, u32[]{:S(2)}) collective-permute-start(bf16[384,1024]{1,0:T(8,128)(2,1)} %fusion.111.grad_ref), channel_id=1, source_target_pairs={{0,1},{1,0},{2,3},{3,2},{4,5},{5,4},{6,7},{7,6},{8,9},{9,8},{10,11... | collective-permute-start | bytes 2359304 | tf_op jit(solution)/shard_map/ppermute | solution.py:395
  213.2 17.9 %collective-permute-start.55 = (f32[2176]{0:T(1024)S(1)}, f32[2176]{0:T(1024)S(1)}, u32[]{:S(2)}, u32[]{:S(2)}) collective-permute-start(f32[2176]{0:T(1024)S(1)} %add.390), channel_id=1, source_target_pairs={{0,16},{4,20},{8,24},{12,28},{16,0},{20,4},{24,8},{28,12},{1,17},{... | collective-permute-start | bytes 26120 | tf_op jit(solution)/shard_map/ppermute | solution.py:395
  222.8 17.0 %collective-permute-start.22 = (bf16[384,1024]{1,0:T(8,128)(2,1)}, bf16[384,1024]{1,0:T(8,128)(2,1)}, u32[]{:S(2)}, u32[]{:S(2)}) collective-permute-start(bf16[384,1024]{1,0:T(8,128)(2,1)} %collective-permute-done.21.grad_ref), channel_id=1, source_target_pairs={{0,1},{1,0},{2,3},{3,2},{4,5},{5,4},{6,7},{7,6},{8,9},{9,8},{10,11... | collective-permute-start | bytes 2359304 | tf_op jit(solution)/shard_map/ppermute | solution.py:395
  244.1 32.3 %collective-permute-start.24 = (bf16[80,256]{1,0:T(8,128)(2,1)S(1)}, bf16[80,256]{1,0:T(8,128)(2,1)S(1)}, u32[]{:S(2)}, u32[]{:S(2)}) collective-permute-start(bf16[80,256]{1,0:T(8,128)(2,1)S(1)} %add_convert_fusion.15), channel_id=1, source_target_pairs={{8,0},{12,4},{16,8},{20,12},{24,16},{28,20},{9,1},{13,5},{17,9},{2... | collective-permute-start | bytes 122888 | tf_op jit(solution)/shard_map/ppermute | solution.py:443
  245.4 31.0 %collective-permute-start.23 = (bf16[80,256]{1,0:T(8,128)(2,1)S(1)}, bf16[80,256]{1,0:T(8,128)(2,1)S(1)}, u32[]{:S(2)}, u32[]{:S(2)}) collective-permute-start(bf16[80,256]{1,0:T(8,128)(2,1)S(1)} %add_convert_fusion.15), channel_id=1, source_target_pairs={{4,0},{8,4},{12,8},{16,12},{20,16},{24,20},{28,24},{5,1},{9,5},{13... | collective-permute-start | bytes 122888 | tf_op jit(solution)/shard_map/ppermute | solution.py:443
  249.9 51.2 %collective-permute-start.40 = (bf16[128,1024]{1,0:T(8,128)(2,1)S(1)}, bf16[128,1024]{1,0:T(8,128)(2,1)}, u32[]{:S(2)}, u32[]{:S(2)}) collective-permute-start(bf16[128,1024]{1,0:T(8,128)(2,1)S(1)} %broadcast_select_fusion.8), channel_id=1, source_target_pairs={{0,8},{4,12},{8,0},{12,4},{16,24},{20,28},{24,16},{28,20},{1,9},{5... | collective-permute-start | bytes 786440 | tf_op jit(solution)/shard_map/ppermute | solution.py:395
  295.9 76.6 %collective-permute-start.26 = (bf16[384,1024]{1,0:T(8,128)(2,1)}, bf16[384,1024]{1,0:T(8,128)(2,1)S(1)}, u32[]{:S(2)}, u32[]{:S(2)}) collective-permute-start(bf16[384,1024]{1,0:T(8,128)(2,1)} %get-tuple-element.110), channel_id=1, source_target_pairs={{0,1},{1,0},{2,3},{3,2},{4,5},{5,4},{6,7},{7,6},{8,9},{9,8},{10,11... | collective-permute-start | bytes 2359304 | tf_op jit(solution)/shard_map/ppermute | solution.py:395
  302.2 14.1 %collective-permute-start.41 = (bf16[64,1024]{1,0:T(8,128)(2,1)S(1)}, bf16[64,1024]{1,0:T(8,128)(2,1)S(1)}, u32[]{:S(2)}, u32[]{:S(2)}) collective-permute-start(bf16[64,1024]{1,0:T(8,128)(2,1)S(1)} %broadcast_select_fusion.17), channel_id=1, source_target_pairs={{0,16},{4,20},{8,24},{12,28},{16,0},{20,4},{24,8},{28,12},{1,17},{... | collective-permute-start | bytes 393224 | tf_op jit(solution)/shard_map/ppermute | solution.py:395
  305.6 11.5 %collective-permute-start.28 = (bf16[192,1024]{1,0:T(8,128)(2,1)S(1)}, bf16[192,1024]{1,0:T(8,128)(2,1)S(1)}, u32[]{:S(2)}, u32[]{:S(2)}) collective-permute-start(bf16[192,1024]{1,0:T(8,128)(2,1)S(1)} %get-tuple-element.143), channel_id=1, source_target_pairs={{0,4},{4,0},{8,12},{12,8},{16,20},{20,16},{24,28},{28,24},{1,5},{5... | collective-permute-start | bytes 1179656 | tf_op jit(solution)/shard_map/ppermute | solution.py:395
  306.4 15.1 %collective-permute-start.34 = (bf16[192,1024]{1,0:T(8,128)(2,1)S(1)}, bf16[192,1024]{1,0:T(8,128)(2,1)S(1)}, u32[]{:S(2)}, u32[]{:S(2)}) collective-permute-start(bf16[192,1024]{1,0:T(8,128)(2,1)S(1)} %get-tuple-element.144), channel_id=1, source_target_pairs={{0,8},{4,12},{8,0},{12,4},{16,24},{20,28},{24,16},{28,20},{1,9},{5... | collective-permute-start | bytes 1179656 | tf_op jit(solution)/shard_map/ppermute | solution.py:395
  307.5 127.1 %collective-permute-start.25 = (bf16[384,1024]{1,0:T(8,128)(2,1)}, bf16[384,1024]{1,0:T(8,128)(2,1)}, u32[]{:S(2)}, u32[]{:S(2)}) collective-permute-start(bf16[384,1024]{1,0:T(8,128)(2,1)} %get-tuple-element.108), channel_id=1, source_target_pairs={{0,1},{1,0},{2,3},{3,2},{4,5},{5,4},{6,7},{7,6},{8,9},{9,8},{10,11... | collective-permute-start | bytes 2359304 | tf_op jit(solution)/shard_map/ppermute | solution.py:395
  316.4 5.6 %collective-permute-start.42 = (bf16[32,1024]{1,0:T(8,128)(2,1)S(1)}, bf16[32,1024]{1,0:T(8,128)(2,1)S(1)}, u32[]{:S(2)}, u32[]{:S(2)}) collective-permute-start(bf16[32,1024]{1,0:T(8,128)(2,1)S(1)} %broadcast_select_fusion.26), channel_id=1, source_target_pairs={{0,4},{4,0},{8,12},{12,8},{16,20},{20,16},{24,28},{28,24},{1,5},{5... | collective-permute-start | bytes 196616 | tf_op jit(solution)/shard_map/ppermute | solution.py:395
  322.1 5.7 %collective-permute-start.43 = (bf16[32,1024]{1,0:T(8,128)(2,1)S(1)}, bf16[32,1024]{1,0:T(8,128)(2,1)S(1)}, u32[]{:S(2)}, u32[]{:S(2)}) collective-permute-start(bf16[32,1024]{1,0:T(8,128)(2,1)S(1)} %add_convert_fusion.14), channel_id=1, source_target_pairs={{0,4},{4,0},{8,12},{12,8},{16,20},{20,16},{24,28},{28,24},{1,5},{5... | collective-permute-start | bytes 196616 | tf_op jit(solution)/shard_map/ppermute | solution.py:395
  323.2 21.2 %collective-permute-start.35 = (bf16[96,1024]{1,0:T(8,128)(2,1)S(1)}, bf16[96,1024]{1,0:T(8,128)(2,1)S(1)}, u32[]{:S(2)}, u32[]{:S(2)}) collective-permute-start(bf16[96,1024]{1,0:T(8,128)(2,1)S(1)} %broadcast_select_fusion.11), channel_id=1, source_target_pairs={{0,16},{4,20},{8,24},{12,28},{16,0},{20,4},{24,8},{28,12},{1,17},{... | collective-permute-start | bytes 589832 | tf_op jit(solution)/shard_map/ppermute | solution.py:395
  324.3 21.6 %collective-permute-start.29 = (bf16[96,1024]{1,0:T(8,128)(2,1)S(1)}, bf16[96,1024]{1,0:T(8,128)(2,1)S(1)}, u32[]{:S(2)}, u32[]{:S(2)}) collective-permute-start(bf16[96,1024]{1,0:T(8,128)(2,1)S(1)} %broadcast_select_fusion.14), channel_id=1, source_target_pairs={{0,8},{4,12},{8,0},{12,4},{16,24},{20,28},{24,16},{28,20},{1,9},{5... | collective-permute-start | bytes 589832 | tf_op jit(solution)/shard_map/ppermute | solution.py:395
  327.8 24.8 %collective-permute-start.44 = (bf16[64,1024]{1,0:T(8,128)(2,1)S(1)}, bf16[64,1024]{1,0:T(8,128)(2,1)S(1)}, u32[]{:S(2)}, u32[]{:S(2)}) collective-permute-start(bf16[64,1024]{1,0:T(8,128)(2,1)S(1)} %pad_maximum_fusion.8), channel_id=1, source_target_pairs={{0,16},{4,20},{8,24},{12,28},{16,0},{20,4},{24,8},{28,12},{1,17},{... | collective-permute-start | bytes 393224 | tf_op jit(solution)/shard_map/ppermute | solution.py:395
  344.5 8.4 %collective-permute-start.36 = (bf16[48,1024]{1,0:T(8,128)(2,1)S(1)}, bf16[48,1024]{1,0:T(8,128)(2,1)S(1)}, u32[]{:S(2)}, u32[]{:S(2)}) collective-permute-start(bf16[48,1024]{1,0:T(8,128)(2,1)S(1)} %broadcast_select_fusion.20), channel_id=1, source_target_pairs={{0,4},{4,0},{8,12},{12,8},{16,20},{20,16},{24,28},{28,24},{1,5},{5... | collective-permute-start | bytes 294920 | tf_op jit(solution)/shard_map/ppermute | solution.py:395
  346.0 8.6 %collective-permute-start.30 = (bf16[48,1024]{1,0:T(8,128)(2,1)S(1)}, bf16[48,1024]{1,0:T(8,128)(2,1)S(1)}, u32[]{:S(2)}, u32[]{:S(2)}) collective-permute-start(bf16[48,1024]{1,0:T(8,128)(2,1)S(1)} %broadcast_select_fusion.23), channel_id=1, source_target_pairs={{0,16},{4,20},{8,24},{12,28},{16,0},{20,4},{24,8},{28,12},{1,17},{... | collective-permute-start | bytes 294920 | tf_op jit(solution)/shard_map/ppermute | solution.py:395
  352.7 49.7 %collective-permute-start.45 = (bf16[128,1024]{1,0:T(8,128)(2,1)S(1)}, bf16[128,1024]{1,0:T(8,128)(2,1)S(1)}, u32[]{:S(2)}, u32[]{:S(2)}) collective-permute-start(bf16[128,1024]{1,0:T(8,128)(2,1)S(1)} %pad_maximum_fusion.5), channel_id=1, source_target_pairs={{0,8},{4,12},{8,0},{12,4},{16,24},{20,28},{24,16},{28,20},{1,9},{5... | collective-permute-start | bytes 786440 | tf_op jit(solution)/shard_map/ppermute | solution.py:395
  352.9 5.3 %collective-permute-start.37 = (bf16[48,1024]{1,0:T(8,128)(2,1)S(1)}, bf16[48,1024]{1,0:T(8,128)(2,1)S(1)}, u32[]{:S(2)}, u32[]{:S(2)}) collective-permute-start(bf16[48,1024]{1,0:T(8,128)(2,1)S(1)} %add_convert_fusion.12), channel_id=1, source_target_pairs={{0,4},{4,0},{8,12},{12,8},{16,20},{20,16},{24,28},{28,24},{1,5},{5... | collective-permute-start | bytes 294920 | tf_op jit(solution)/shard_map/ppermute | solution.py:395
  354.7 17.7 %collective-permute-start.31 = (bf16[48,1024]{1,0:T(8,128)(2,1)S(1)}, bf16[48,1024]{1,0:T(8,128)(2,1)S(1)}, u32[]{:S(2)}, u32[]{:S(2)}) collective-permute-start(bf16[48,1024]{1,0:T(8,128)(2,1)S(1)} %add_convert_fusion.13), channel_id=1, source_target_pairs={{0,16},{4,20},{8,24},{12,28},{16,0},{20,4},{24,8},{28,12},{1,17},{... | collective-permute-start | bytes 294920 | tf_op jit(solution)/shard_map/ppermute | solution.py:395
  358.3 26.6 %collective-permute-start.38 = (bf16[96,1024]{1,0:T(8,128)(2,1)S(1)}, bf16[96,1024]{1,0:T(8,128)(2,1)S(1)}, u32[]{:S(2)}, u32[]{:S(2)}) collective-permute-start(bf16[96,1024]{1,0:T(8,128)(2,1)S(1)} %pad_maximum_fusion.7), channel_id=1, source_target_pairs={{0,16},{4,20},{8,24},{12,28},{16,0},{20,4},{24,8},{28,12},{1,17},{... | collective-permute-start | bytes 589832 | tf_op jit(solution)/shard_map/ppermute | solution.py:395
  372.4 28.2 %collective-permute-start.32 = (bf16[96,1024]{1,0:T(8,128)(2,1)S(1)}, bf16[96,1024]{1,0:T(8,128)(2,1)S(1)}, u32[]{:S(2)}, u32[]{:S(2)}) collective-permute-start(bf16[96,1024]{1,0:T(8,128)(2,1)S(1)} %pad_maximum_fusion.6), channel_id=1, source_target_pairs={{0,8},{4,12},{8,0},{12,4},{16,24},{20,28},{24,16},{28,20},{1,9},{5... | collective-permute-start | bytes 589832 | tf_op jit(solution)/shard_map/ppermute | solution.py:395
  373.7 60.8 %collective-permute-start.27 = (bf16[384,1024]{1,0:T(8,128)(2,1)}, bf16[384,1024]{1,0:T(8,128)(2,1)S(1)}, u32[]{:S(2)}, u32[]{:S(2)}) collective-permute-start(bf16[384,1024]{1,0:T(8,128)(2,1)} %add_convert_fusion.1), channel_id=1, source_target_pairs={{0,2},{1,3},{2,0},{3,1},{4,6},{5,7},{6,4},{7,5},{8,10},{9,11},{10,... | collective-permute-start | bytes 2359304 | tf_op jit(solution)/shard_map/ppermute | solution.py:395
  385.8 46.4 %collective-permute-start.39 = (bf16[192,1024]{1,0:T(8,128)(2,1)}, bf16[192,1024]{1,0:T(8,128)(2,1)}, u32[]{:S(2)}, u32[]{:S(2)}) collective-permute-start(bf16[192,1024]{1,0:T(8,128)(2,1)} %pad_maximum_fusion.4), channel_id=1, source_target_pairs={{0,8},{4,12},{8,0},{12,4},{16,24},{20,28},{24,16},{28,20},{1,9},{5... | collective-permute-start | bytes 1179656 | tf_op jit(solution)/shard_map/ppermute | solution.py:395
  401.5 31.9 %collective-permute-start.33 = (bf16[192,1024]{1,0:T(8,128)(2,1)}, bf16[192,1024]{1,0:T(8,128)(2,1)}, u32[]{:S(2)}, u32[]{:S(2)}) collective-permute-start(bf16[192,1024]{1,0:T(8,128)(2,1)} %pad_maximum_fusion.3), channel_id=1, source_target_pairs={{0,4},{4,0},{8,12},{12,8},{16,20},{20,16},{24,28},{28,24},{1,5},{5... | collective-permute-start | bytes 1179656 | tf_op jit(solution)/shard_map/ppermute | solution.py:395
  436.9 2.3 collective-permute-start.46
  439.2 3.7 collective-permute-start.47
  442.9 3.7 collective-permute-start.48
  446.7 3.7 collective-permute-start.49
  450.4 4.6 collective-permute-start.50
  (64 other events, 408.3 us)
Sparse Core Ops, SparseCore 0:
  228.0 197.3 all-reduce.2

commit v3 on v2

--- a/solution.py
+++ b/solution.py
@@ -71,28 +71,234 @@
     return pl.BlockSpec(memory_space=pltpu.SMEM)
 
 
+def anywhere():
+    return pl.BlockSpec(memory_space=pl.ANY)
+
+
 def shape(rows, cols, kind):
     return jax.ShapeDtypeStruct((rows, cols), kind)
 
 
-def qkv_body(x_ref, w_ref, valid_ref, q_ref, k_ref, v_ref):
-    x = x_ref[...]
-    q = nn(x, w_ref[0])
-    k = nn(x, w_ref[1])
-    q_ref[...] = feature(q).astype(BF)
-    k_ref[...] = (feature(k) * valid_ref[...]).astype(BF)
-    v_ref[...] = nn(x, w_ref[2]).astype(BF)
-
-
-def project_qkv(x, w, valid):
-    rows, width = x.shape[0], w.shape[2]
+def whole_spec(array):
+    rank = len(array.shape)
+    return pl.BlockSpec(array.shape, lambda i: (0,) * rank)
+
+
+def row_spec(tile, cols, start=0):
+    return pl.BlockSpec((tile, cols), lambda i: (start + i, 0))
+
+
+def first_spec(tile, cols, half):
+    return pl.BlockSpec((tile, cols), lambda i: (jnp.minimum(i, half - 1), 0))
+
+
+def second_spec(tile, cols, half):
+    return pl.BlockSpec((tile, cols), lambda i: (jnp.maximum(i - half, 0), 0))
+
+
+def either(first_ref, second_ref):
+    half = pl.num_programs(0) // 2
+    return jnp.where(pl.program_id(0) < half, first_ref[...], second_ref[...])
+
+
+def put_either(first_ref, second_ref, value):
+    half = pl.num_programs(0) // 2
+
+    @pl.when(pl.program_id(0) < half)
+    def _():
+        first_ref[...] = value
+
+    @pl.when(pl.program_id(0) >= half)
+    def _():
+        second_ref[...] = value
+
+
+ROW_TILE = 192
+
+
+def normal(values):
+    centre = jnp.mean(values, axis=-1, keepdims=True)
+    moved = values - centre
+    scale = lax.rsqrt(jnp.mean(moved * moved, axis=-1, keepdims=True) + 1e-05)
+    return moved * scale, scale
+
+
+def normal_back(grad, gain, xhat, scale):
+    g = grad * gain
+    return scale * (
+        g - jnp.mean(g, axis=-1, keepdims=True) - xhat * jnp.mean(g * xhat, axis=-1, keepdims=True)
+    )
+
+
+def total(refs):
+    value = refs[0][...].astype(F32)
+    for ref in refs[1:]:
+        value = value + ref[...].astype(F32)
+    return value
+
+
+def gain_sums(grad, xhat, gain_ref, bias_ref):
+    @pl.when(pl.program_id(0) == 0)
+    def _():
+        gain_ref[...] = jnp.zeros_like(gain_ref)
+        bias_ref[...] = jnp.zeros_like(bias_ref)
+
+    gain_ref[...] += jnp.sum(grad * xhat, axis=0, keepdims=True)
+    bias_ref[...] += jnp.sum(grad, axis=0, keepdims=True)
+
+
+def norm_body(x_ref, gain_ref, bias_ref, out_ref):
+    xhat, _ = normal(x_ref[...].astype(F32))
+    out_ref[...] = (xhat * gain_ref[...] + bias_ref[...]).astype(BF)
+
+
+def norm_one(x, gain, bias):
+    rows = x.shape[0]
+    return pl.pallas_call(
+        norm_body,
+        grid=(rows // ROW_TILE,),
+        out_shape=shape(rows, D, BF),
+        in_specs=[row_spec(ROW_TILE, D), whole_spec(gain), whole_spec(bias)],
+        out_specs=row_spec(ROW_TILE, D),
+        name="norm_one",
+    )(x, gain, bias)
+
+
+def middle_body(*refs):
+    x_ref, gain_ref, bias_ref = refs[:3]
+    parts = refs[3:-3]
+    middle_ref, out_ref, square_ref = refs[-3:]
+    attended = total(parts)
+    middle = x_ref[...].astype(F32) + attended
+    middle_ref[...] = middle
+    xhat, _ = normal(middle)
+    out_ref[...] = (xhat * gain_ref[...] + bias_ref[...]).astype(BF)
+    square_ref[...] = jnp.sum(attended * attended, axis=-1, keepdims=True)
+
+
+def norm_two(x, gain, bias, parts):
+    rows = x.shape[0]
+    return pl.pallas_call(
+        middle_body,
+        grid=(rows // ROW_TILE,),
+        out_shape=(shape(rows, D, F32), shape(rows, D, BF), shape(rows, 1, F32)),
+        in_specs=[row_spec(ROW_TILE, D), whole_spec(gain), whole_spec(bias)]
+        + [row_spec(ROW_TILE, D)] * len(parts),
+        out_specs=(row_spec(ROW_TILE, D), row_spec(ROW_TILE, D), row_spec(ROW_TILE, 1)),
+        name="norm_two",
+    )(x, gain, bias, *parts)
+
+
+def middle_back_body(*refs):
+    grad_ref, middle_ref, gain_ref = refs[:3]
+    parts = refs[3:-4]
+    wide_ref, low_ref, gain_grad_ref, bias_grad_ref = refs[-4:]
+    grad = total(parts)
+    xhat, scale = normal(middle_ref[...])
+    gain_sums(grad, xhat, gain_grad_ref, bias_grad_ref)
+    out = grad_ref[...].astype(F32) + normal_back(grad, gain_ref[...], xhat, scale)
+    wide_ref[...] = out
+    low_ref[...] = out.astype(BF)
+
+
+def norm_two_back(grad, middle, gain, parts):
+    rows = grad.shape[0]
+    return pl.pallas_call(
+        middle_back_body,
+        grid=(rows // ROW_TILE,),
+        out_shape=(shape(rows, D, F32), shape(rows, D, BF), shape(1, D, F32), shape(1, D, F32)),
+        in_specs=[row_spec(ROW_TILE, D), row_spec(ROW_TILE, D), whole_spec(gain)]
+        + [row_spec(ROW_TILE, D)] * len(parts),
+        out_specs=(row_spec(ROW_TILE, D), row_spec(ROW_TILE, D), whole_spec(gain), whole_spec(gain)),
+        name="norm_two_back",
+    )(grad, middle, gain, *parts)
+
+
+def pixels_back_body(*refs):
+    x_ref, wide_ref, gain_ref = refs[:3]
+    parts = refs[3:-3]
+    out_ref, gain_grad_ref, bias_grad_ref = refs[-3:]
+    grad = total(parts)
+    xhat, scale = normal(x_ref[...].astype(F32))
+    gain_sums(grad, xhat, gain_grad_ref, bias_grad_ref)
+    out_ref[...] = (wide_ref[...] + normal_back(grad, gain_ref[...], xhat, scale)).astype(BF)
+
+
+def norm_one_back(x, wide, gain, parts):
+    rows = x.shape[0]
+    return pl.pallas_call(
+        pixels_back_body,
+        grid=(rows // ROW_TILE,),
+        out_shape=(shape(rows, D, BF), shape(1, D, F32), shape(1, D, F32)),
+        in_specs=[row_spec(ROW_TILE, D), row_spec(ROW_TILE, D), whole_spec(gain)]
+        + [row_spec(ROW_TILE, D)] * len(parts),
+        out_specs=(row_spec(ROW_TILE, D), whole_spec(gain), whole_spec(gain)),
+        name="norm_one_back",
+    )(x, wide, gain, *parts)
+
+
+def result_body(*refs):
+    middle_ref = refs[0]
+    parts = refs[1:-3]
+    out_ref, result_square_ref, branch_square_ref = refs[-3:]
+    branch = total(parts)
+    result = middle_ref[...] + branch
+    out_ref[...] = result.astype(BF)
+    result_square_ref[...] = jnp.sum(result * result, axis=-1, keepdims=True)
+    branch_square_ref[...] = jnp.sum(branch * branch, axis=-1, keepdims=True)
+
+
+def finish(middle, parts):
+    rows = middle.shape[0]
+    return pl.pallas_call(
+        result_body,
+        grid=(rows // ROW_TILE,),
+        out_shape=(shape(rows, D, BF), shape(rows, 1, F32), shape(rows, 1, F32)),
+        in_specs=[row_spec(ROW_TILE, D)] * (1 + len(parts)),
+        out_specs=(row_spec(ROW_TILE, D), row_spec(ROW_TILE, 1), row_spec(ROW_TILE, 1)),
+        name="finish",
+    )(middle, *parts)
+
+
+def qkv_body(tail_ref, xa_ref, xb_ref, w_ref, valid_ref, seg_ref, was_ref, *rest):
+    q_ref, k_ref, v_ref, pack_ref = rest[-4:]
+    width = q_ref.shape[1]
+    x = either(xa_ref, xb_ref)
+    q_ref[...] = feature(nn(x, w_ref[0])).astype(BF)
+    k = (feature(nn(x, w_ref[1])) * valid_ref[...]).astype(BF)
+    v = nn(x, w_ref[2]).astype(BF)
+    k_ref[...] = k
+    v_ref[...] = v
+    kept = pick(seg_ref[...] == tail_ref[0], k)
+    state = fold_heads(pick(same_head(width), tn(kept, v)), width)
+    sums = jnp.sum(kept.astype(F32), axis=0, keepdims=True)
+
+    @pl.when(pl.program_id(0) == 0)
+    def _():
+        pack_ref[...] = was_ref[...]
+
+    pack_ref[0:HEAD, :] += state
+    pack_ref[HEAD:PACK, :] += jnp.broadcast_to(sums, (PACK - HEAD, width))
+
+
+def project_qkv(pair, tail, xa, xb, w, valid, seg, was, made):
+    rows, width = xa.shape[0], w.shape[2]
+    half = rows // ROW_TILE
+    at = lambda cols: row_spec(ROW_TILE, cols, pair * 2 * half)
+    whole = valid.shape[0]
     return pl.pallas_call(
         qkv_body,
-        out_shape=(shape(rows, width, BF),) * 3,
-        in_specs=[vmem()] * 3,
-        out_specs=(vmem(),) * 3,
+        grid=(2 * half,),
+        out_shape=(shape(whole, width, BF),) * 3 + (shape(PACK, width, F32),),
+        in_specs=[
+            smem(), first_spec(ROW_TILE, D, half), second_spec(ROW_TILE, D, half), whole_spec(w),
+            at(1), at(1), whole_spec(was),
+        ]
+        + [anywhere()] * len(made),
+        out_specs=(at(width), at(width), at(width), whole_spec(was)),
+        input_output_aliases={7 + i: i for i in range(len(made))},
         name="project_qkv",
-    )(x, w, valid)
+    )(tail, xa, xb, w, valid, seg, was, *made)
 
 
 def forward_body(
@@ -149,29 +355,9 @@
     )(last, spot, q, k, v, segc, segr)
 
 
-def tail_body(last_ref, k_ref, v_ref, segc_ref, out_ref):
-    rows, width = k_ref.shape
-    tail = last_ref[rows // CHUNK]
-    kept = pick(segc_ref[...] == tail, k_ref[...])
-    state = fold_heads(pick(same_head(width), tn(kept, v_ref[...])), width)
-    sums = jnp.sum(kept.astype(F32), axis=0, keepdims=True)
-    out_ref[0:HEAD, :] = state.astype(BF)
-    out_ref[HEAD:PACK, :] = jnp.broadcast_to(sums, (PACK - HEAD, width)).astype(BF)
-
-
-def tail_pack(last, k, v, segc):
-    return pl.pallas_call(
-        tail_body,
-        out_shape=shape(PACK, k.shape[1], BF),
-        in_specs=[smem()] + [vmem()] * 3,
-        out_specs=vmem(),
-        name="tail_pack",
-    )(last, k, v, segc)
-
-
 def project_body(
     first_ref, num_ref, den_ref, q_ref, pack_ref, segc_ref, valid_ref, w_ref,
-    heads_ref, wide_ref, rinv_ref, out_ref
+    heads_ref, wide_ref, rinv_ref, a_ref, b_ref
 ):
     rows, width = q_ref.shape
     block = same_head(width)
@@ -188,39 +374,90 @@
     heads_ref[...] = heads
     wide_ref[...] = wide
     rinv_ref[...] = rinv
-    out_ref[...] = nn(heads, w_ref[...]).astype(BF)
-
-
-def slot_spec(rows, cols, slot):
-    return pl.BlockSpec((rows, cols), lambda i: (slot, 0))
-
-
-def whole_spec(array):
-    rank = array.ndim
-    return pl.BlockSpec(array.shape, lambda i: (0,) * rank)
-
-
-def project(slot, rows, last, num, den, q, pack, segc, valid, w):
+    put_either(a_ref, b_ref, nn(heads, w_ref[...]).astype(BF))
+
+
+def project(pair, rows, last, num, den, q, pack, segc, valid, w):
     width = q.shape[1]
-    at = lambda cols: slot_spec(rows, cols, slot)
-    mine = lambda cols: slot_spec(rows, cols, 0)
+    half = rows // ROW_TILE
+    at = lambda cols: row_spec(ROW_TILE, cols, pair * 2 * half)
+    mine = lambda cols: row_spec(ROW_TILE, cols)
     return pl.pallas_call(
         project_body,
-        grid=(1,),
-        out_shape=(shape(rows, width, BF), shape(rows, width, F32), shape(rows, width, F32), shape(rows, D, BF)),
+        grid=(2 * half,),
+        out_shape=(shape(2 * rows, width, BF), shape(2 * rows, width, F32), shape(2 * rows, width, F32))
+        + (shape(rows, D, BF),) * 2,
         in_specs=[smem(), at(width), at(width), at(width), whole_spec(pack), at(1), at(1), whole_spec(w)],
-        out_specs=(mine(width), mine(width), mine(width), mine(D)),
+        out_specs=(
+            mine(width), mine(width), mine(width),
+            first_spec(ROW_TILE, D, half), second_spec(ROW_TILE, D, half),
+        ),
         name="project",
     )(last, num, den, q, pack, segc, valid, w)
 
 
+HIDDEN_TILE = 256
+
+
+def mlp_body(
+    xa_ref, xb_ref, ga_ref, gb_ref, up_ref, down_ref,
+    act_ref, hid_ref, na_ref, nb_ref, ba_ref, bb_ref, nacc_ref, bacc_ref
+):
+    rows = xa_ref.shape[0]
+    up, down = up_ref[...], down_ref[...]
+    root = 0.7978845608028654
+    first = pl.program_id(0) == 0
+
+    @pl.when(first)
+    def _():
+        nacc_ref[...] = jnp.zeros_like(nacc_ref)
+        bacc_ref[...] = jnp.zeros_like(bacc_ref)
+
+    for i, (x_ref, g_ref) in enumerate(((xa_ref, ga_ref), (xb_ref, gb_ref))):
+        at = slice(i * rows, (i + 1) * rows)
+        h = nn(x_ref[...], up)
+        grad = nt(g_ref[...], down)
+        square = h * h
+        t = jnp.tanh(root * h * (1.0 + 0.044715 * square))
+        act = (0.5 * h * (1.0 + t)).astype(BF)
+        slope = 0.5 * (1.0 + t) + 0.5 * h * (1.0 - t * t) * (root * (1.0 + 3.0 * 0.044715 * square))
+        hid = (grad * slope).astype(BF)
+        act_ref[at, :] = act
+        hid_ref[at, :] = hid
+        nacc_ref[at, :] += nt(hid, up)
+        bacc_ref[at, :] += nn(act, down)
+
+    @pl.when(pl.program_id(0) == pl.num_programs(0) - 1)
+    def _():
+        na_ref[...] = nacc_ref[0:rows, :].astype(BF)
+        nb_ref[...] = nacc_ref[rows:, :].astype(BF)
+        ba_ref[...] = bacc_ref[0:rows, :].astype(BF)
+        bb_ref[...] = bacc_ref[rows:, :].astype(BF)
+
+
+def mlp(xa, xb, ga, gb, up, down):
+    rows, hidden = xa.shape[0], up.shape[1]
+    col = pl.BlockSpec((2 * rows, HIDDEN_TILE), lambda i: (0, i))
+    return pl.pallas_call(
+        mlp_body,
+        grid=(hidden // HIDDEN_TILE,),
+        out_shape=(shape(2 * rows, hidden, BF),) * 2 + (shape(rows, D, BF),) * 4,
+        in_specs=[whole_spec(xa)] * 4
+        + [pl.BlockSpec((D, HIDDEN_TILE), lambda i: (0, i)), row_spec(HIDDEN_TILE, D)],
+        out_specs=(col, col) + (whole_spec(xa),) * 4,
+        scratch_shapes=[pltpu.VMEM((2 * rows, D), F32)] * 2,
+        name="mlp",
+    )(xa, xb, ga, gb, up, down)
+
+
 def heads_back_body(
-    first_ref, grad_ref, w_ref, wide_ref, rinv_ref, q_ref, segc_ref, ng_ref, dg_ref, pack_ref
+    first_ref, ga_ref, gb_ref, w_ref, wide_ref, rinv_ref, q_ref, segc_ref, was_ref, *rest
 ):
+    ng_ref, dg_ref, pack_ref = rest[-3:]
     width = q_ref.shape[1]
     block = same_head(width)
     ones_block = block.astype(BF)
-    hg = nt(grad_ref[...], w_ref[...])
+    hg = nt(either(ga_ref, gb_ref), w_ref[...])
     rinv = rinv_ref[...]
     ng = (hg * rinv).astype(BF)
     prod = hg * wide_ref[...]
@@ -230,23 +467,34 @@
     ng_ref[...] = ng
     dg_ref[...] = dg
     opened = pick(segc_ref[...] == first_ref[0], q_ref[...])
-    pack_ref[0:HEAD, :] = fold_heads(pick(block, tn(opened, ng)), width)
+
+    @pl.when(pl.program_id(0) == 0)
+    def _():
+        pack_ref[...] = was_ref[...]
+
+    pack_ref[0:HEAD, :] += fold_heads(pick(block, tn(opened, ng)), width)
     sums = jnp.sum(opened.astype(F32) * dg, axis=0, keepdims=True)
-    pack_ref[HEAD:PACK, :] = jnp.broadcast_to(sums, (PACK - HEAD, width))
-
-
-def heads_back(slot, last, grad, w, wide, rinv, q, segc):
-    rows, width = grad.shape[0], q.shape[1]
-    at = lambda cols: slot_spec(rows, cols, slot)
-    mine = lambda cols: slot_spec(rows, cols, 0)
+    pack_ref[HEAD:PACK, :] += jnp.broadcast_to(sums, (PACK - HEAD, width))
+
+
+def heads_back(pair, last, ga, gb, w, wide, rinv, q, segc, was, made):
+    rows, width = ga.shape[0], q.shape[1]
+    half = rows // ROW_TILE
+    at = lambda cols: row_spec(ROW_TILE, cols, pair * 2 * half)
+    mine = lambda cols: row_spec(ROW_TILE, cols)
     return pl.pallas_call(
         heads_back_body,
-        grid=(1,),
-        out_shape=(shape(rows, width, BF), shape(rows, width, F32), shape(PACK, width, F32)),
-        in_specs=[smem(), mine(D), whole_spec(w), mine(width), mine(width), at(width), at(1)],
-        out_specs=(mine(width), mine(width), slot_spec(PACK, width, 0)),
+        grid=(2 * half,),
+        out_shape=(shape(q.shape[0], width, BF), shape(q.shape[0], width, F32), shape(PACK, width, F32)),
+        in_specs=[
+            smem(), first_spec(ROW_TILE, D, half), second_spec(ROW_TILE, D, half), whole_spec(w),
+            mine(width), mine(width), at(width), at(1), whole_spec(was),
+        ]
+        + [anywhere()] * len(made),
+        out_specs=(at(width), at(width), whole_spec(was)),
+        input_output_aliases={9 + i: i for i in range(len(made))},
         name="heads_back",
-    )(last, grad, w, wide, rinv, q, segc)
+    )(last, ga, gb, w, wide, rinv, q, segc, was, *made)
 
 
 def backward_body(
@@ -339,7 +587,7 @@
 
 def mix_body(
     tail_ref, dq_ref, dk_ref, dv_ref, k_ref, v_ref, segc_ref, valid_ref, pack_ref, w_ref,
-    mixed_ref, out_ref
+    mixed_ref, a_ref, b_ref
 ):
     rows, width = k_ref.shape
     block = same_head(width)
@@ -355,36 +603,29 @@
     mixed_ref[:, 0:width] = dq
     mixed_ref[:, width : 2 * width] = dk
     mixed_ref[:, 2 * width : 3 * width] = dv
-    out_ref[...] = (nt(dq, w_ref[0]) + nt(dk, w_ref[1]) + nt(dv, w_ref[2])).astype(BF)
-
-
-def mix(slot, rows, tail, dq, dk, dv, k, v, segc, valid, pack, w):
+    out = nt(dq, w_ref[0]) + nt(dk, w_ref[1]) + nt(dv, w_ref[2])
+    put_either(a_ref, b_ref, out.astype(BF))
+
+
+def mix(pair, rows, tail, dq, dk, dv, k, v, segc, valid, pack, w):
     width = k.shape[1]
-    at = lambda cols: slot_spec(rows, cols, slot)
-    mine = lambda cols: slot_spec(rows, cols, 0)
+    half = rows // ROW_TILE
+    at = lambda cols: row_spec(ROW_TILE, cols, pair * 2 * half)
     return pl.pallas_call(
         mix_body,
-        grid=(1,),
-        out_shape=(shape(rows, 3 * width, BF), shape(rows, D, BF)),
+        grid=(2 * half,),
+        out_shape=(shape(2 * rows, 3 * width, BF),) + (shape(rows, D, BF),) * 2,
         in_specs=[smem()] + [at(width)] * 5 + [at(1)] * 2 + [whole_spec(pack), whole_spec(w)],
-        out_specs=(mine(3 * width), mine(D)),
+        out_specs=(
+            row_spec(ROW_TILE, 3 * width),
+            first_spec(ROW_TILE, D, half), second_spec(ROW_TILE, D, half),
+        ),
         name="mix",
     )(tail, dq, dk, dv, k, v, segc, valid, pack, w)
 
 
-def layer_norm(values, norm_gain, norm_bias):
-    centre = jnp.mean(values, axis=-1, keepdims=True)
-    shifted = values - centre
-    spread = jnp.mean(shifted * shifted, axis=-1, keepdims=True)
-    return shifted * lax.rsqrt(spread + 1e-05) * norm_gain + norm_bias
-
-
 def feature(values):
     return jnp.where(values > 0, values + 1.0, jnp.exp(jnp.minimum(values, 0.0)))
-
-
-def gelu_tanh(values):
-    return jax.nn.gelu(values, approximate=True)
 
 
 def bits_of(count):
@@ -403,13 +644,18 @@
     return [slots[s] for s in range(len(slots))]
 
 
-def scatter_slots(parts):
-    parts = dict(enumerate(parts))
+def scatter_slots(parts, after=None):
+    parts = {s: [part] for s, part in enumerate(parts)}
     for bit in bits_of(lax.axis_size("feat")):
         for s in sorted(parts, reverse=True):
             if s & bit:
-                got = swap(parts.pop(s).astype(BF), "feat", bit)
-                parts[s ^ bit] = parts[s ^ bit].astype(F32) + got.astype(F32)
+                pieces = parts.pop(s)
+                value = pieces[0]
+                if len(pieces) > 1:
+                    value = functools.reduce(jnp.add, [p.astype(F32) for p in pieces]).astype(BF)
+                if after is not None and bit > 1:
+                    value = lax.optimization_barrier((value, after))[0]
+                parts[s ^ bit].append(swap(value, "feat", bit))
     return parts[0]
 
 
@@ -433,6 +679,17 @@
         got = swap(value, "rows", bit)
         value = jnp.concatenate([jnp.where(upper, got, value), jnp.where(upper, value, got)], axis=0)
     return value
+
+
+def sum_pieces(value, count, order, turned):
+    size = value.shape[0] // count
+    return jnp.concatenate(
+        [
+            sum_rows(value[i * size : (i + 1) * size], turned if i % 2 else order)
+            for i in range(count)
+        ],
+        axis=0,
+    )
 
 
 def shifted(pack, hop, groups, reverse):
@@ -477,6 +734,7 @@
     crop_count = crop_offsets.shape[0]
     groups = lax.axis_size("rows")
     members = lax.axis_size("feat")
+    pairs = members // 2
     here = lax.axis_index("rows")
     member = lax.axis_index("feat")
     reach = min(groups - 1, -(-(CROP_MAX - 1) // group_rows))
@@ -501,104 +759,97 @@
     per = local_rows // CHUNK
     chunk_edges = group_start - 1 + jnp.arange(chunks + 1, dtype=jnp.int32) * CHUNK
     last = jnp.sum((crop_offsets[None, :] <= chunk_edges[:, None]).astype(jnp.int32), axis=1) - 1
+    tail = last[-1:]
     order = jnp.arange(chunks, dtype=jnp.int32)
     spot = ((order // per) ^ member) * per + order % per
     segc = segment[:, None]
     segr = segment.reshape(chunks, 1, CHUNK)
     validc = pixel_valid[:, None]
-    local_valid = pixel_valid[:local_rows]
-    local_segment = segment[:local_rows]
-
-    inputs = pixels.astype(F32)
-    normed, norm1_back = jax.vjp(layer_norm, inputs, norm1_gain, norm1_bias)
-    normed_slots = gather_slots(normed.astype(BF))
+    gain1, bias1, gain2, bias2 = (
+        a[None, :] for a in (norm1_gain, norm1_bias, norm2_gain, norm2_bias)
+    )
+    no_pack = jnp.zeros((PACK, width), F32)
+
+    normed_slots = gather_slots(norm_one(pixels, gain1, bias1))
     late_grad = lax.optimization_barrier((out_grad, normed_slots[members // 2]))[0]
     grad_slots = gather_slots(late_grad)
-    made = [
-        project_qkv(normed_slots[s], qkv_weight, validc[s * local_rows : (s + 1) * local_rows])
-        for s in range(members)
-    ]
-    q, k, v = (jnp.concatenate([m[i] for m in made], axis=0) for i in range(3))
-    pack = tail_pack(last, k, v, segc)
-    carry = gather_carry(pack, crops_at, here, groups, reach, False)
+    made, pack = (), no_pack
+    for p in range(pairs):
+        *made, pack = project_qkv(
+            p, tail, normed_slots[2 * p], normed_slots[2 * p + 1], qkv_weight, validc, segc, pack, made
+        )
+    q, k, v = made
+    carry = gather_carry(pack.astype(BF), crops_at, here, groups, reach, False)
     num, den = attend(last, spot, q, k, v, segc, segr)
     sent = {
-        s: project(s, local_rows, last, num, den, q, carry, segc, validc, out_weight)
-        for s in reversed(range(members))
+        p: project(p, local_rows, last, num, den, q, carry, segc, validc, out_weight)
+        for p in reversed(range(pairs))
     }
-    heads_slots, wide_slots, rinv_slots, parts = ([sent[s][i] for s in range(members)] for i in range(4))
-    attended = scatter_slots(parts)
-    middle = inputs + attended
-    normed_two, norm2_back = jax.vjp(layer_norm, middle, norm2_gain, norm2_bias)
-    two_slots = gather_slots(normed_two.astype(BF))
-    active_slots, hidden_slots, two_parts, branch_parts = [], [], [], []
-    for s in range(members):
-        hidden = nn(two_slots[s], up_weight)
-        activated, gelu_back = jax.vjp(gelu_tanh, hidden)
-        activated = activated.astype(BF)
-        hidden_grad = gelu_back(nt(grad_slots[s], down_weight))[0].astype(BF)
-        two_parts.append(nt(hidden_grad, up_weight).astype(BF))
-        branch_parts.append(nn(activated, down_weight).astype(BF))
-        active_slots.append(activated)
-        hidden_slots.append(hidden_grad)
-    normed_two_grad = scatter_slots(two_parts)
-    branch = scatter_slots(branch_parts)
+    parts = [sent[s // 2][3 + s % 2] for s in range(members)]
+    middle, normed_two, attended_square = norm_two(pixels, gain2, bias2, scatter_slots(parts))
+    two_slots = gather_slots(normed_two)
+    hidden = [
+        mlp(*two_slots[2 * p : 2 * p + 2], *grad_slots[2 * p : 2 * p + 2], up_weight, down_weight)
+        for p in range(pairs)
+    ]
+    two_parts = scatter_slots([hidden[s // 2][2 + s % 2] for s in range(members)])
+    branch_parts = scatter_slots([hidden[s // 2][4 + s % 2] for s in range(members)], two_parts[-1])
     grad_all = jnp.concatenate(grad_slots, axis=0)
-    down_grad = tn(jnp.concatenate(active_slots, axis=0), grad_all).astype(BF)
-    up_grad = tn(jnp.concatenate(two_slots, axis=0), jnp.concatenate(hidden_slots, axis=0)).astype(BF)
-    down_grad = lax.psum(down_grad, "rows").astype(F32)
-    up_grad = lax.psum(up_grad, "rows").astype(F32)
-    result = middle + branch
-    middle_part, gain2_grad, bias2_grad = norm2_back(normed_two_grad)
-    middle_grad = out_grad.astype(F32) + middle_part
-    middle_slots = gather_slots(middle_grad.astype(BF))
-    backs = [
-        heads_back(s, last, middle_slots[s], out_weight, wide_slots[s], rinv_slots[s], q, segc)
-        for s in range(members)
-    ]
-    ng, dg = (jnp.concatenate([b[i] for b in backs], axis=0) for i in range(2))
-    grad_pack = functools.reduce(jnp.add, [b[2] for b in backs]).astype(BF)
-    grad_carry = gather_carry(grad_pack, crops_at, here, groups, reach, True)
-    out_weight_grad = tn(jnp.concatenate(heads_slots, axis=0), jnp.concatenate(middle_slots, axis=0))
+    down_grad = tn(jnp.concatenate([h[0] for h in hidden], axis=0), grad_all).astype(BF)
+    up_grad = tn(jnp.concatenate(two_slots, axis=0), jnp.concatenate([h[1] for h in hidden], axis=0)).astype(BF)
+    middle_grad, middle_low, gain2_grad, bias2_grad = norm_two_back(out_grad, middle, gain2, two_parts)
+    middle_slots = gather_slots(middle_low)
+    made, grad_pack = (), no_pack
+    for p in range(pairs):
+        *made, grad_pack = heads_back(
+            p, last, middle_slots[2 * p], middle_slots[2 * p + 1], out_weight,
+            sent[p][1], sent[p][2], q, segc, grad_pack, made
+        )
+    ng, dg = made
+    grad_carry = gather_carry(grad_pack.astype(BF), crops_at, here, groups, reach, True)
+    out_weight_grad = tn(
+        jnp.concatenate([sent[p][0] for p in range(pairs)], axis=0), jnp.concatenate(middle_slots, axis=0)
+    ).astype(BF)
     dq, dk, dv = attend_back(last, spot, q, k, v, ng, dg, segc, segr, carry)
     mixes = {
-        s: mix(s, local_rows, last[-1:], dq, dk, dv, k, v, segc, validc, grad_carry, qkv_weight)
-        for s in reversed(range(members))
+        p: mix(p, local_rows, tail, dq, dk, dv, k, v, segc, validc, grad_carry, qkv_weight)
+        for p in reversed(range(pairs))
     }
-    normed_grad = scatter_slots([mixes[s][1] for s in range(members)])
-    mixed_grad = jnp.concatenate([mixes[s][0] for s in range(members)], axis=0)
+    normed_parts = scatter_slots([mixes[s // 2][1 + s % 2] for s in range(members)])
+    mixed_grad = jnp.concatenate([mixes[p][0] for p in range(pairs)], axis=0)
     qkv_grad = tn(mixed_grad, jnp.concatenate(normed_slots, axis=0)).astype(BF)
+    output, result_square, branch_square = finish(middle, branch_parts)
+    pixels_grad, gain1_grad, bias1_grad = norm_one_back(pixels, middle_grad, gain1, normed_parts)
+
     bits = bits_of(groups)
     turned = bits[1:] + bits[:1]
-    cut = 3 * width // 2
-    qkv_grad = jnp.concatenate([sum_rows(qkv_grad[:cut], bits), sum_rows(qkv_grad[cut:], turned)], axis=0)
+    down_grad = lax.psum(down_grad, "rows").astype(F32)
+    up_grad = sum_pieces(up_grad, 4, bits, turned).astype(F32)
+    out_weight_grad = sum_rows(out_weight_grad, turned).astype(F32)
+    qkv_grad = sum_pieces(qkv_grad, 2, bits, turned)
     qkv_grad = jnp.swapaxes(qkv_grad.reshape(3, width, D), 1, 2).astype(F32)
-    out_weight_grad = sum_rows(out_weight_grad.astype(BF), turned).astype(F32)
-    input_part, gain1_grad, bias1_grad = norm1_back(normed_grad)
-    pixels_grad = (middle_grad + input_part).astype(BF)
+
     crop_onehot = (
-        local_segment[:, None] == jnp.arange(crop_count, dtype=jnp.int32)[None, :]
+        segment[:local_rows, None] == jnp.arange(crop_count, dtype=jnp.int32)[None, :]
     ).astype(F32)
     squares = (
-        jnp.stack(
-            [
-                jnp.sum(result * result, axis=1),
-                jnp.sum(attended * attended, axis=1),
-                jnp.sum(branch * branch, axis=1),
-                jnp.ones((local_rows,), F32),
-            ]
+        jnp.concatenate(
+            [result_square, attended_square, branch_square, jnp.ones((local_rows, 1), F32)], axis=1
         )
-        * local_valid[None, :]
-    )
-    crop_sums = jnp.dot(squares, crop_onehot, precision=precise)
-    early = sum_everywhere(jnp.concatenate([gain2_grad, bias2_grad, crop_sums.reshape(-1)]))
-    gain2_grad, bias2_grad = early[:D], early[D : 2 * D]
-    crop_sums = early[2 * D :].reshape(4, crop_count)
-    late = sum_everywhere(jnp.concatenate([gain1_grad, bias1_grad]))
-    gain1_grad, bias1_grad = late[:D], late[D:]
+        * validc[:local_rows]
+    )
+    crop_sums = lax.dot_general(
+        squares, crop_onehot, (((0,), (0,)), ((), ())), precision=precise, preferred_element_type=F32
+    )
+    sums = jnp.concatenate(
+        [gain1_grad[0], bias1_grad[0], gain2_grad[0], bias2_grad[0], crop_sums.reshape(-1)]
+    )
+    sums = sum_everywhere(sums)
+    gain1_grad, bias1_grad, gain2_grad, bias2_grad = sums[: 4 * D].reshape(4, D)
+    crop_sums = sums[4 * D :].reshape(4, crop_count)
     crop_rms = jnp.sqrt(crop_sums[:3] / (D * jnp.maximum(crop_sums[3], 1.0))[None, :])
     return (
-        result.astype(BF),
+        output,
         pixels_grad,
         qkv_grad,
         out_weight_grad,

time: 470 us -> 548 us (1.17)
  waiting for transfers between devices: 176 us -> 255 us
  Pallas kernels: 94.1 us -> 134 us
  matrix products: 46.9 us -> 20.1 us
  other arithmetic: 48.8 us -> 31.4 us
  starting transfers between devices: 49.1 us -> 60.1 us
  local copies, waits for them, and re-layouts: 26.7 us -> 16.2 us
    ppermute x52 -> x71, waiting for transfers between devices: 154 us -> 255 us  [swap(): lax.ppermute(value, axis, [(i, i ^ bit) for i in range(lax.axis_size(axis...]
    pallas_call x17 -> x15, Pallas kernels: 59.9 us -> 100 us  [the longest x2 28.9 us: mlp(): pl.pallas_call(mlp_body, grid=(hidden // HIDDEN_TILE,), out_shape=(shape(...]
    dot_general x17 -> x1, matrix products: 26.8 us -> 0.29 us  [on_device(): lax.dot_general(squares, crop_onehot, (((0,), (0,)), ((), ())), precision...]
    psum x1, waiting for transfers between devices: 21.8 us -> 0.01 us  [on_device(): down_grad = lax.psum(down_grad, 'rows').astype(F32)]
    reduce_sum x8 -> x0, other arithmetic: 15.2 us -> none  [the longest x2 5.41 us: layer_norm(): shifted = values - centre]
    ppermute x52 -> x71, starting transfers between devices: 39.6 us -> 50.2 us  [swap(): lax.ppermute(value, axis, [(i, i ^ bit) for i in range(lax.axis_size(axis...]
    convert_element_type x9 -> x8, other arithmetic: 16.3 us -> 7.44 us  [the longest x1 2.48 us: on_device(): up_grad = sum_pieces(up_grad, 4, bits, turned).astype(F32)]
    unnamed x148 -> x70, local copies, waits for them, and re-layouts: 12.4 us -> 5.32 us
  transfers between devices with their start and end apart: 57 -> 76, of which waited for: 21 -> 41; matrix products, arithmetic and copies ran while one was open for 22% -> 11% of each run, Pallas kernels for 18% -> 21%
where the time goes in v3:
time: 548 us; the launch traced here: 538 us
  waiting for transfers between devices  255 us (47%)
  Pallas kernels  134 us (24%)
  starting transfers between devices  60.1 us (11%)
  other arithmetic  31.4 us (6%)
  between operations  20.5 us (4%)
  matrix products  20.1 us (4%)
  local copies, waits for them, and re-layouts  16.2 us (3%)
    ppermute x71, waiting for transfers between devices, swap(): lax.ppermute(value, axis, [(i, i ^ bit) for i in range(lax.axis_size(axis...  255 us
    ppermute x71, starting transfers between devices, swap(): lax.ppermute(value, axis, [(i, i ^ bit) for i in range(lax.axis_size(axis...  50.2 us
    pallas_call x2, Pallas kernels, mlp(): pl.pallas_call(mlp_body, grid=(hidden // HIDDEN_TILE,), out_shape=(shape(...  28.9 us
    pallas_call x1, Pallas kernels, attend_back(): pl.pallas_call(backward_body, out_shape=(shape(rows, width, BF), shape(ro...  20.5 us
    dot_general x4, matrix products, tn(): lax.dot_general(a, b, (((0,), (0,)), ((), ())), preferred_element_type=F32)  19.9 us
    pallas_call x2, Pallas kernels, mix(): pl.pallas_call(mix_body, grid=(2 * half,), out_shape=(shape(2 * rows, 3 *...  15.9 us
    pallas_call x1, Pallas kernels, attend(): pl.pallas_call(forward_body, out_shape=(shape(rows, width, F32),) * 2, in...  13.5 us
    pallas_call x2, Pallas kernels, project_qkv(): pl.pallas_call(qkv_body, grid=(2 * half,), out_shape=(shape(whole, width,...  13.1 us
  transfers between devices with their start and end apart: 76, of which 41 were waited for; matrix products, arithmetic and copies ran while one was open for 11% of the time, Pallas kernels for 21%

profile of v3, /device:TPU:0, one launch (start us, length us, event | category | flops | bytes accessed | tf_op | source)
XLA Modules:
  0.0 537.8 jit_solution(16488188651850496127)
XLA Ops:
  7.2 2.4 norm_one.1.xa_ref
  10.1 2.5 collective-permute-start
  18.1 13.0 %collective-permute-done.xa_ref = bf16[384,1024]{1,0:T(8,128)(2,1)S(1)} collective-permute-done((bf16[384,1024]{1,0:T(8,128)(2,1)}, bf16[384,1024]{1,0:T(8,128)(2,1)S(1)}, u32[]{:S(2)}, u32[]{:S(2)}) %collective-permute-start) | collective-permute-done | bytes 786464 | tf_op jit(solution)/shard_map/ppermute | solution.py:636
  33.4 6.5 %project_qkv.2 = (bf16[1536,256]{1,0:T(8,128)(2,1)}, bf16[1536,256]{1,0:T(8,128)(2,1)}, bf16[1536,256]{1,0:T(8,128)(2,1)}, f32[80,256]{1,0:T(8,128)}) custom-call(s32[1]{0:T(128)} %slice.186.tail_ref, bf16[384,1024]{1,0:T(8,128)(2,1)} %norm_one.1.xa_ref, bf16[384,1024]{1,0:T(8,128)(2,1)} %copy-done.4, bf16[3,1024,256]{2,1,0:T(8,128)(2,1)} %w_ref.15, ...), custom_call_target="tpu_custom_call" | custom-call | tf_op jit(solution)/shard_map/project_qkv/pallas_call | solution.py:289
  40.9 6.5 %project_qkv.3 = (bf16[1536,256]{1,0:T(8,128)(2,1)}, bf16[1536,256]{1,0:T(8,128)(2,1)}, bf16[1536,256]{1,0:T(8,128)(2,1)}, f32[80,256]{1,0:T(8,128)}) custom-call(s32[1]{0:T(128)} %slice.186.tail_ref, bf16[384,1024]{1,0:T(8,128)(2,1)} %copy-done.6, bf16[384,1024]{1,0:T(8,128)(2,1)} %copy-done.8, ...), custom_call_target="tpu_custom_call", output_to_operand_aliasing={{0}: (7, {}), {1}: (8, {}), {2}: (9, {})} | custom-call | tf_op jit(solution)/shard_map/project_qkv/pallas_call | solution.py:289
  48.3 3.7 collective-permute-start.4
  52.0 3.6 collective-permute-start.3
  60.0 13.5 %attend.1 = (f32[1536,256]{1,0:T(8,128)}, f32[1536,256]{1,0:T(8,128)}) custom-call(s32[13]{0:T(128)} %copy-done.23, s32[12]{0:T(128)} %fusion.74.spot_ref, bf16[1536,256]{1,0:T(8,128)(2,1)} %get-tuple-element.77.q_ref, bf16[1536,256]{1,0:T(8,128)(2,1)} %get-tuple-element.78.k_ref, bf16[1536,256]{1,0:T(8,128)(2,1)} %get-tuple-element.79.v_ref, ...), custom_call_target="tpu_custom_call" | custom-call | tf_op jit(solution)/shard_map/attend/pallas_call | solution.py:348
  74.2 5.8 %project.3 = (bf16[768,256]{1,0:T(8,128)(2,1)}, f32[768,256]{1,0:T(8,128)}, f32[768,256]{1,0:T(8,128)}, bf16[384,1024]{1,0:T(8,128)(2,1)}, bf16[384,1024]{1,0:T(8,128)(2,1)}) custom-call(s32[13]{0:T(128)} %copy-done.23, f32[1536,256]{1,0:T(8,128)} %get-tuple-element.80.num_ref, f32[1536,256]{1,0:T(8,128)} %get-tuple-element.81.den_ref, ...), custom_call_target="tpu_custom_call" | custom-call | tf_op jit(solution)/shard_map/project/pallas_call | solution.py:385
  80.1 5.8 %project.2 = (bf16[768,256]{1,0:T(8,128)(2,1)}, f32[768,256]{1,0:T(8,128)}, f32[768,256]{1,0:T(8,128)}, bf16[384,1024]{1,0:T(8,128)(2,1)}, bf16[384,1024]{1,0:T(8,128)(2,1)}) custom-call(s32[13]{0:T(128)} %copy-done.23, f32[1536,256]{1,0:T(8,128)} %get-tuple-element.80.num_ref, f32[1536,256]{1,0:T(8,128)} %get-tuple-element.81.den_ref, ...), custom_call_target="tpu_custom_call" | custom-call | tf_op jit(solution)/shard_map/project/pallas_call | solution.py:385
  88.8 18.5 %collective-permute-done.7.refs_5_ = bf16[384,1024]{1,0:T(8,128)(2,1)} collective-permute-done((bf16[384,1024]{1,0:T(8,128)(2,1)S(1)}, bf16[384,1024]{1,0:T(8,128)(2,1)}, u32[]{:S(2)}, u32[]{:S(2)}) %collective-permute-start.7) | collective-permute-done | bytes 786464 | tf_op jit(solution)/shard_map/ppermute | solution.py:636
  107.3 3.2 norm_two.1
  112.5 11.6 %collective-permute-done.13.ga_ref = bf16[384,1024]{1,0:T(8,128)(2,1)S(1)} collective-permute-done((bf16[384,1024]{1,0:T(8,128)(2,1)S(1)}, bf16[384,1024]{1,0:T(8,128)(2,1)S(1)}, u32[]{:S(2)}, u32[]{:S(2)}) %collective-permute-start.13) | collective-permute-done | bytes 786464 | tf_op jit(solution)/shard_map/ppermute | solution.py:636
  124.0 16.1 %collective-permute-done.11.xa_ref = bf16[384,1024]{1,0:T(8,128)(2,1)} collective-permute-done((bf16[384,1024]{1,0:T(8,128)(2,1)}, bf16[384,1024]{1,0:T(8,128)(2,1)}, u32[]{:S(2)}, u32[]{:S(2)}) %collective-permute-start.11) | collective-permute-done | bytes 786464 | tf_op jit(solution)/shard_map/ppermute | solution.py:636
  144.7 14.3 %mlp.2 = (bf16[768,1024]{1,0:T(8,128)(2,1)}, bf16[768,1024]{1,0:T(8,128)(2,1)}, bf16[384,1024]{1,0:T(8,128)(2,1)}, bf16[384,1024]{1,0:T(8,128)(2,1)}, bf16[384,1...) custom-call(bf16[384,1024]{1,0:T(8,128)(2,1)} %get-tuple-element.88.xa_ref, bf16[384,1024]{1,0:T(8,128)(2,1)} %collective-permute-done.8.xb_ref, ...), custom_call_target="tpu_custom_call" | custom-call | tf_op jit(solution)/shard_map/mlp/pallas_call | solution.py:441
  159.6 14.7 %mlp.3 = (bf16[768,1024]{1,0:T(8,128)(2,1)}, bf16[768,1024]{1,0:T(8,128)(2,1)}, bf16[384,1024]{1,0:T(8,128)(2,1)}, bf16[384,1024]{1,0:T(8,128)(2,1)}, bf16[384,1...) custom-call(bf16[384,1024]{1,0:T(8,128)(2,1)} %collective-permute-done.11.xa_ref, ...), custom_call_target="tpu_custom_call" | custom-call | tf_op jit(solution)/shard_map/mlp/pallas_call | solution.py:441
  174.2 6.5 %fusion.46 = bf16[1024,1024]{1,0:T(8,128)(2,1)S(1)} fusion(bf16[768,1024]{1,0:T(8,128)(2,1)} %get-tuple-element.125, bf16[768,1024]{1,0:T(8,128)(2,1)} %get-tuple-element.124, bf16[384,1024]{1,0:T(8,128)(2,1)} %collective-permute-done.12.xb_ref, bf16[384,1024]{1,0:T(8,128)(2,1)} %collective-permute-done.11.xa_ref, ...), kind=kOutput, calls=%fused_computation.42 | convolution fusion | flops 3241148416 | bytes 8388608 | tf_op jit(solution)/shard_map/dot_general | solution.py:31
  185.7 6.0 %fusion.41 = bf16[1024,1024]{1,0:T(8,128)(2,1)} fusion(bf16[384,1024]{1,0:T(8,128)(2,1)} %collective-permute-done.14.gb_ref, bf16[384,1024]{1,0:T(8,128)(2,1)S(1)} %copy-done.10, bf16[384,1024]{1,0:T(8,128)(2,1)S(1)} %copy-done.12, bf16[384,1024]{1,0:T(8,128)(2,1)S(1)} %copy-done.2, bf16[768,1024]{1,0:T(8,128)(2,1)S(1)} %copy-done.28, ...), kind=kOutput, calls=%fused_computation.41 | convolution fusion | flops 3241148416 | bytes 8388608 | tf_op jit(solution)/shard_map/dot_general | solution.py:31
  192.7 4.4 collective-permute-done.46
  199.1 16.9 %collective-permute-done.53 = bf16[64,1024]{1,0:T(8,128)(2,1)S(1)} collective-permute-done((bf16[64,1024]{1,0:T(8,128)(2,1)S(1)}, bf16[64,1024]{1,0:T(8,128)(2,1)S(1)}, u32[]{:S(2)}, u32[]{:S(2)}) %collective-permute-start.53) | collective-permute-done | bytes 131104 | tf_op jit(solution)/shard_map/ppermute | solution.py:636
  216.1 13.7 %collective-permute-done.47 = bf16[64,1024]{1,0:T(8,128)(2,1)S(1)} collective-permute-done((bf16[64,1024]{1,0:T(8,128)(2,1)S(1)}, bf16[64,1024]{1,0:T(8,128)(2,1)S(1)}, u32[]{:S(2)}, u32[]{:S(2)}) %collective-permute-start.47) | collective-permute-done | bytes 131104 | tf_op jit(solution)/shard_map/ppermute | solution.py:636
  229.8 5.4 %collective-permute-done.59 = bf16[64,1024]{1,0:T(8,128)(2,1)S(1)} collective-permute-done((bf16[64,1024]{1,0:T(8,128)(2,1)S(1)}, bf16[64,1024]{1,0:T(8,128)(2,1)S(1)}, u32[]{:S(2)}, u32[]{:S(2)}) %collective-permute-start.59) | collective-permute-done | bytes 131104 | tf_op jit(solution)/shard_map/ppermute | solution.py:636
  235.3 12.6 %collective-permute-done.65 = bf16[64,1024]{1,0:T(8,128)(2,1)S(1)} collective-permute-done((bf16[64,1024]{1,0:T(8,128)(2,1)S(1)}, bf16[64,1024]{1,0:T(8,128)(2,1)S(1)}, u32[]{:S(2)}, u32[]{:S(2)}) %collective-permute-start.65) | collective-permute-done | bytes 131104 | tf_op jit(solution)/shard_map/ppermute | solution.py:636
  248.0 4.2 collective-permute-done.54
  252.2 5.1 collective-permute-done.48
  257.5 6.2 %collective-permute-done.60 = bf16[32,1024]{1,0:T(8,128)(2,1)S(1)} collective-permute-done((bf16[32,1024]{1,0:T(8,128)(2,1)S(1)}, bf16[32,1024]{1,0:T(8,128)(2,1)S(1)}, u32[]{:S(2)}, u32[]{:S(2)}) %collective-permute-start.60) | collective-permute-done | bytes 65568 | tf_op jit(solution)/shard_map/ppermute | solution.py:636
  264.1 3.8 collective-permute-done.66
  268.4 3.8 collective-permute-done.55
  272.2 5.1 collective-permute-done.49
  277.8 10.1 %collective-permute-done.61 = bf16[32,1024]{1,0:T(8,128)(2,1)S(1)} collective-permute-done((bf16[32,1024]{1,0:T(8,128)(2,1)S(1)}, bf16[32,1024]{1,0:T(8,128)(2,1)S(1)}, u32[]{:S(2)}, u32[]{:S(2)}) %collective-permute-start.61) | collective-permute-done | bytes 65568 | tf_op jit(solution)/shard_map/ppermute | solution.py:636
  288.7 3.4 collective-permute-done.67
  292.2 13.8 %collective-permute-done.56 = bf16[64,1024]{1,0:T(8,128)(2,1)S(1)} collective-permute-done((bf16[64,1024]{1,0:T(8,128)(2,1)S(1)}, bf16[64,1024]{1,0:T(8,128)(2,1)S(1)}, u32[]{:S(2)}, u32[]{:S(2)}) %collective-permute-start.56) | collective-permute-done | bytes 131104 | tf_op jit(solution)/shard_map/ppermute | solution.py:636
  306.0 5.5 %collective-permute-done.50 = bf16[64,1024]{1,0:T(8,128)(2,1)S(1)} collective-permute-done((bf16[64,1024]{1,0:T(8,128)(2,1)S(1)}, bf16[64,1024]{1,0:T(8,128)(2,1)S(1)}, u32[]{:S(2)}, u32[]{:S(2)}) %collective-permute-start.50) | collective-permute-done | bytes 131104 | tf_op jit(solution)/shard_map/ppermute | solution.py:636
  311.7 6.1 %collective-permute-done.62 = bf16[64,1024]{1,0:T(8,128)(2,1)S(1)} collective-permute-done((bf16[64,1024]{1,0:T(8,128)(2,1)S(1)}, bf16[64,1024]{1,0:T(8,128)(2,1)S(1)}, u32[]{:S(2)}, u32[]{:S(2)}) %collective-permute-start.62) | collective-permute-done | bytes 131104 | tf_op jit(solution)/shard_map/ppermute | solution.py:636
  318.6 5.8 %collective-permute-done.68 = bf16[64,1024]{1,0:T(8,128)(2,1)S(1)} collective-permute-done((bf16[64,1024]{1,0:T(8,128)(2,1)S(1)}, bf16[64,1024]{1,0:T(8,128)(2,1)S(1)}, u32[]{:S(2)}, u32[]{:S(2)}) %collective-permute-start.68) | collective-permute-done | bytes 131104 | tf_op jit(solution)/shard_map/ppermute | solution.py:636
  329.9 4.2 collective-permute-done.51
  335.2 2.1 collective-permute-start.69
  338.2 4.9 norm_two_back.1
  346.5 15.7 %collective-permute-done.20.ga_ref = bf16[384,1024]{1,0:T(8,128)(2,1)} collective-permute-done((bf16[384,1024]{1,0:T(8,128)(2,1)}, bf16[384,1024]{1,0:T(8,128)(2,1)}, u32[]{:S(2)}, u32[]{:S(2)}) %collective-permute-start.20) | collective-permute-done | bytes 786464 | tf_op jit(solution)/shard_map/ppermute | solution.py:636
  364.4 2.5 convert_element_type.391
  366.9 4.1 convert_element_type.393
  370.9 3.1 finish.1
  376.5 6.2 %heads_back.2 = (bf16[1536,256]{1,0:T(8,128)(2,1)}, f32[1536,256]{1,0:T(8,128)}, f32[80,256]{1,0:T(8,128)}) custom-call(s32[13]{0:T(128)} %copy-done.23, bf16[384,1024]{1,0:T(8,128)(2,1)} %get-tuple-element.101.ga_ref, bf16[384,1024]{1,0:T(8,128)(2,1)} %collective-permute-done.22.gb_ref, bf16[256,1024]{1,0:T(8,128)(2,1)} %w_ref.13, ...), custom_call_target="tpu_custom_call" | custom-call | tf_op jit(solution)/shard_map/heads_back/pallas_call | solution.py:485
  382.7 6.3 %heads_back.3 = (bf16[1536,256]{1,0:T(8,128)(2,1)}, f32[1536,256]{1,0:T(8,128)}, f32[80,256]{1,0:T(8,128)}) custom-call(s32[13]{0:T(128)} %copy-done.23, bf16[384,1024]{1,0:T(8,128)(2,1)} %collective-permute-done.20.ga_ref, bf16[384,1024]{1,0:T(8,128)(2,1)} %collective-permute-done.21.gb_ref, ...), custom_call_target="tpu_custom_call", output_to_operand_aliasing={{0}: (9, {}), {1}: (10, {})} | custom-call | tf_op jit(solution)/shard_map/heads_back/pallas_call | solution.py:485
  392.5 2.8 fusion.56
  395.4 3.3 collective-permute-start.40
  398.8 20.5 %attend_back.1 = (bf16[1536,256]{1,0:T(8,128)(2,1)}, f32[1536,256]{1,0:T(8,128)}, f32[1536,256]{1,0:T(8,128)}) custom-call(s32[13]{0:T(128)} %copy-done.23, s32[12]{0:T(128)} %fusion.74.spot_ref, bf16[1536,256]{1,0:T(8,128)(2,1)} %get-tuple-element.77.q_ref, bf16[1536,256]{1,0:T(8,128)(2,1)} %get-tuple-element.78.k_ref, ...), custom_call_target="tpu_custom_call" | custom-call | tf_op jit(solution)/shard_map/attend_back/pallas_call | solution.py:573
  420.0 7.9 %mix.3 = (bf16[768,768]{1,0:T(8,128)(2,1)}, bf16[384,1024]{1,0:T(8,128)(2,1)}, bf16[384,1024]{1,0:T(8,128)(2,1)}) custom-call(s32[1]{0:T(128)} %slice.186.tail_ref, bf16[1536,256]{1,0:T(8,128)(2,1)} %get-tuple-element.111.dq_ref, f32[1536,256]{1,0:T(8,128)} %get-tuple-element.112.dk_ref, f32[1536,256]{1,0:T(8,128)} %get-tuple-element.113.dv_ref, ...), custom_call_target="tpu_custom_call" | custom-call | tf_op jit(solution)/shard_map/mix/pallas_call | solution.py:614
  427.9 8.0 %mix.2 = (bf16[768,768]{1,0:T(8,128)(2,1)}, bf16[384,1024]{1,0:T(8,128)(2,1)}, bf16[384,1024]{1,0:T(8,128)(2,1)}) custom-call(s32[1]{0:T(128)} %slice.186.tail_ref, bf16[1536,256]{1,0:T(8,128)(2,1)} %get-tuple-element.111.dq_ref, f32[1536,256]{1,0:T(8,128)} %get-tuple-element.112.dk_ref, f32[1536,256]{1,0:T(8,128)} %get-tuple-element.113.dv_ref, ...), custom_call_target="tpu_custom_call" | custom-call | tf_op jit(solution)/shard_map/mix/pallas_call | solution.py:614
  435.9 4.5 fusion.51
  440.6 3.5 collective-permute-start.41
  446.8 3.3 collective-permute-done.41
  452.0 2.7 collective-permute-done.28
  454.7 3.4 collective-permute-done.34
  460.6 2.3 collective-permute-done.43
  463.0 10.6 %collective-permute-done.35 = bf16[96,1024]{1,0:T(8,128)(2,1)S(1)} collective-permute-done((bf16[96,1024]{1,0:T(8,128)(2,1)S(1)}, bf16[96,1024]{1,0:T(8,128)(2,1)S(1)}, u32[]{:S(2)}, u32[]{:S(2)}) %collective-permute-start.35) | collective-permute-done | bytes 196640 | tf_op jit(solution)/shard_map/ppermute | solution.py:636
  480.7 2.4 collective-permute-done.37
  483.3 8.8 %collective-permute-done.31 = bf16[48,1024]{1,0:T(8,128)(2,1)S(1)} collective-permute-done((bf16[48,1024]{1,0:T(8,128)(2,1)S(1)}, bf16[48,1024]{1,0:T(8,128)(2,1)S(1)}, u32[]{:S(2)}, u32[]{:S(2)}) %collective-permute-start.31) | collective-permute-done | bytes 98336 | tf_op jit(solution)/shard_map/ppermute | solution.py:636
  492.5 2.4 collective-permute-start.27
  497.2 5.6 %collective-permute-done.32 = bf16[96,1024]{1,0:T(8,128)(2,1)S(1)} collective-permute-done((bf16[96,1024]{1,0:T(8,128)(2,1)S(1)}, bf16[96,1024]{1,0:T(8,128)(2,1)S(1)}, u32[]{:S(2)}, u32[]{:S(2)}) %collective-permute-start.32) | collective-permute-done | bytes 196640 | tf_op jit(solution)/shard_map/ppermute | solution.py:636
  505.8 4.5 norm_one_back.1
  522.3 2.1 collective-permute-done.73
  524.3 2.9 collective-permute-start.74
  527.4 2.1 copy.74
  (312 shorter events, 84.5 us)
Async XLA Ops:
  7.2 359.7 %all-reduce.2.cloned.1.call-start = ((), (), s32[]{:S(2)}) async-start(), calls=%async_computation | async-start | bytes 4194304 | tf_op jit(solution)/shard_map/psum | solution.py:826
  9.7 22.8 %collective-permute-start.2 = (bf16[384,1024]{1,0:T(8,128)(2,1)}, bf16[384,1024]{1,0:T(8,128)(2,1)S(1)}, u32[]{:S(2)}, u32[]{:S(2)}) collective-permute-start(bf16[384,1024]{1,0:T(8,128)(2,1)} %norm_one.1.xa_ref), channel_id=1, source_target_pairs={{0,1},{1,0},{2,3},{3,2},{4,5},{5,4},{6,7},{7,6},{8,9},{9,8},{10,11... | collective-permute-start | bytes 2359304 | tf_op jit(solution)/shard_map/ppermute | solution.py:636
  10.1 20.9 %collective-permute-start = (bf16[384,1024]{1,0:T(8,128)(2,1)}, bf16[384,1024]{1,0:T(8,128)(2,1)S(1)}, u32[]{:S(2)}, u32[]{:S(2)}) collective-permute-start(bf16[384,1024]{1,0:T(8,128)(2,1)} %norm_one.1.xa_ref), channel_id=1, source_target_pairs={{0,2},{1,3},{2,0},{3,1},{4,6},{5,7},{6,4},{7,5},{8,10},{9,11},{10,... | collective-permute-start | bytes 2359304 | tf_op jit(solution)/shard_map/ppermute | solution.py:636
  31.0 8.9 %collective-permute-start.1 = (bf16[384,1024]{1,0:T(8,128)(2,1)S(1)}, bf16[384,1024]{1,0:T(8,128)(2,1)S(1)}, u32[]{:S(2)}, u32[]{:S(2)}) collective-permute-start(bf16[384,1024]{1,0:T(8,128)(2,1)S(1)} %collective-permute-done.xa_ref), channel_id=1, source_target_pairs={{0,1},{1,0},{2,3},{3,2},{4,5},{5,4},{6,7},{7,6},{8,9},{9,8},{10,11... | collective-permute-start | bytes 2359304 | tf_op jit(solution)/shard_map/ppermute | solution.py:636
  48.3 25.2 %collective-permute-start.4 = (bf16[80,256]{1,0:T(8,128)(2,1)S(1)}, bf16[80,256]{1,0:T(8,128)(2,1)S(1)}, u32[]{:S(2)}, u32[]{:S(2)}) collective-permute-start(bf16[80,256]{1,0:T(8,128)(2,1)S(1)} %convert_element_type.303), channel_id=1, source_target_pairs={{0,8},{4,12},{8,16},{12,20},{16,24},{20,28},{1,9},{5,13},{9,17},{1... | collective-permute-start | bytes 122888 | tf_op jit(solution)/shard_map/ppermute | solution.py:700
  52.0 21.5 %collective-permute-start.3 = (bf16[80,256]{1,0:T(8,128)(2,1)S(1)}, bf16[80,256]{1,0:T(8,128)(2,1)S(1)}, u32[]{:S(2)}, u32[]{:S(2)}) collective-permute-start(bf16[80,256]{1,0:T(8,128)(2,1)S(1)} %convert_element_type.303), channel_id=1, source_target_pairs={{0,4},{4,8},{8,12},{12,16},{16,20},{20,24},{24,28},{1,5},{5,9},{9,... | collective-permute-start | bytes 122888 | tf_op jit(solution)/shard_map/ppermute | solution.py:700
  80.0 6.4 %collective-permute-start.6 = (bf16[384,1024]{1,0:T(8,128)(2,1)}, bf16[384,1024]{1,0:T(8,128)(2,1)S(1)}, u32[]{:S(2)}, u32[]{:S(2)}) collective-permute-start(bf16[384,1024]{1,0:T(8,128)(2,1)} %get-tuple-element.86), channel_id=1, source_target_pairs={{0,1},{1,0},{2,3},{3,2},{4,5},{5,4},{6,7},{7,6},{8,9},{9,8},{10,11... | collective-permute-start | bytes 2359304 | tf_op jit(solution)/shard_map/ppermute | solution.py:636
  86.7 20.6 %collective-permute-start.7 = (bf16[384,1024]{1,0:T(8,128)(2,1)S(1)}, bf16[384,1024]{1,0:T(8,128)(2,1)}, u32[]{:S(2)}, u32[]{:S(2)}) collective-permute-start(bf16[384,1024]{1,0:T(8,128)(2,1)S(1)} %add_convert_fusion.3), channel_id=1, source_target_pairs={{0,2},{1,3},{2,0},{3,1},{4,6},{5,7},{6,4},{7,5},{8,10},{9,11},{10,... | collective-permute-start | bytes 2359304 | tf_op jit(solution)/shard_map/ppermute | solution.py:636
  88.3 35.7 %collective-permute-start.13 = (bf16[384,1024]{1,0:T(8,128)(2,1)S(1)}, bf16[384,1024]{1,0:T(8,128)(2,1)S(1)}, u32[]{:S(2)}, u32[]{:S(2)}) collective-permute-start(bf16[384,1024]{1,0:T(8,128)(2,1)S(1)} %copy-done.1), channel_id=1, source_target_pairs={{0,2},{1,3},{2,0},{3,1},{4,6},{5,7},{6,4},{7,5},{8,10},{9,11},{10,... | collective-permute-start | bytes 2359304 | tf_op jit(solution)/shard_map/ppermute | solution.py:636
  110.4 29.7 %collective-permute-start.11 = (bf16[384,1024]{1,0:T(8,128)(2,1)}, bf16[384,1024]{1,0:T(8,128)(2,1)}, u32[]{:S(2)}, u32[]{:S(2)}) collective-permute-start(bf16[384,1024]{1,0:T(8,128)(2,1)} %get-tuple-element.88.xa_ref), channel_id=1, source_target_pairs={{0,2},{1,3},{2,0},{3,1},{4,6},{5,7},{6,4},{7,5},{8,10},{9,11},{10,... | collective-permute-start | bytes 2359304 | tf_op jit(solution)/shard_map/ppermute | solution.py:636
  111.9 31.8 %collective-permute-start.9 = (bf16[384,1024]{1,0:T(8,128)(2,1)S(1)}, bf16[384,1024]{1,0:T(8,128)(2,1)S(1)}, u32[]{:S(2)}, u32[]{:S(2)}) collective-permute-start(bf16[384,1024]{1,0:T(8,128)(2,1)S(1)} %copy-done.1), channel_id=1, source_target_pairs={{0,1},{1,0},{2,3},{3,2},{4,5},{5,4},{6,7},{7,6},{8,9},{9,8},{10,11... | collective-permute-start | bytes 2359304 | tf_op jit(solution)/shard_map/ppermute | solution.py:636
  112.0 31.9 %collective-permute-start.8 = (bf16[384,1024]{1,0:T(8,128)(2,1)}, bf16[384,1024]{1,0:T(8,128)(2,1)}, u32[]{:S(2)}, u32[]{:S(2)}) collective-permute-start(bf16[384,1024]{1,0:T(8,128)(2,1)} %get-tuple-element.88.xa_ref), channel_id=1, source_target_pairs={{0,1},{1,0},{2,3},{3,2},{4,5},{5,4},{6,7},{7,6},{8,9},{9,8},{10,11... | collective-permute-start | bytes 2359304 | tf_op jit(solution)/shard_map/ppermute | solution.py:636
  124.0 35.5 %collective-permute-start.14 = (bf16[384,1024]{1,0:T(8,128)(2,1)S(1)}, bf16[384,1024]{1,0:T(8,128)(2,1)}, u32[]{:S(2)}, u32[]{:S(2)}) collective-permute-start(bf16[384,1024]{1,0:T(8,128)(2,1)S(1)} %collective-permute-done.13.ga_ref), channel_id=1, source_target_pairs={{0,1},{1,0},{2,3},{3,2},{4,5},{5,4},{6,7},{7,6},{8,9},{9,8},{10,11... | collective-permute-start | bytes 2359304 | tf_op jit(solution)/shard_map/ppermute | solution.py:636
  140.1 19.5 %collective-permute-start.12 = (bf16[384,1024]{1,0:T(8,128)(2,1)}, bf16[384,1024]{1,0:T(8,128)(2,1)}, u32[]{:S(2)}, u32[]{:S(2)}) collective-permute-start(bf16[384,1024]{1,0:T(8,128)(2,1)} %collective-permute-done.11.xa_ref), channel_id=1, source_target_pairs={{0,1},{1,0},{2,3},{3,2},{4,5},{5,4},{6,7},{7,6},{8,9},{9,8},{10,11... | collective-permute-start | bytes 2359304 | tf_op jit(solution)/shard_map/ppermute | solution.py:636
  159.0 212.0 %collective-permute-start.10 = (bf16[384,1024]{1,0:T(8,128)(2,1)}, bf16[384,1024]{1,0:T(8,128)(2,1)}, u32[]{:S(2)}, u32[]{:S(2)}) collective-permute-start(bf16[384,1024]{1,0:T(8,128)(2,1)} %get-tuple-element.91), channel_id=1, source_target_pairs={{0,1},{1,0},{2,3},{3,2},{4,5},{5,4},{6,7},{7,6},{8,9},{9,8},{10,11... | collective-permute-start | bytes 2359304 | tf_op jit(solution)/shard_map/ppermute | solution.py:636
  181.7 10.2 %collective-permute-start.64 = (bf16[128,1024]{1,0:T(8,128)(2,1)}, bf16[128,1024]{1,0:T(8,128)(2,1)S(1)}, u32[]{:S(2)}, u32[]{:S(2)}) collective-permute-start(bf16[128,1024]{1,0:T(8,128)(2,1)} %get-tuple-element.141), channel_id=1, source_target_pairs={{0,8},{4,12},{8,0},{12,4},{16,24},{20,28},{24,16},{28,20},{1,9},{5... | collective-permute-start | bytes 786440 | tf_op jit(solution)/shard_map/ppermute | solution.py:636
  183.3 9.4 %collective-permute-start.58 = (bf16[128,1024]{1,0:T(8,128)(2,1)}, bf16[128,1024]{1,0:T(8,128)(2,1)S(1)}, u32[]{:S(2)}, u32[]{:S(2)}) collective-permute-start(bf16[128,1024]{1,0:T(8,128)(2,1)} %get-tuple-element.142), channel_id=1, source_target_pairs={{0,4},{4,0},{8,12},{12,8},{16,20},{20,16},{24,28},{28,24},{1,5},{5... | collective-permute-start | bytes 786440 | tf_op jit(solution)/shard_map/ppermute | solution.py:636
  184.8 12.2 %collective-permute-start.46 = (bf16[128,1024]{1,0:T(8,128)(2,1)}, bf16[128,1024]{1,0:T(8,128)(2,1)S(1)}, u32[]{:S(2)}, u32[]{:S(2)}) collective-permute-start(bf16[128,1024]{1,0:T(8,128)(2,1)} %get-tuple-element.143), channel_id=1, source_target_pairs={{0,4},{4,0},{8,12},{12,8},{16,20},{20,16},{24,28},{28,24},{1,5},{5... | collective-permute-start | bytes 786440 | tf_op jit(solution)/shard_map/ppermute | solution.py:636
  185.3 11.8 %collective-permute-start.52 = (bf16[128,1024]{1,0:T(8,128)(2,1)S(1)}, bf16[128,1024]{1,0:T(8,128)(2,1)S(1)}, u32[]{:S(2)}, u32[]{:S(2)}) collective-permute-start(bf16[128,1024]{1,0:T(8,128)(2,1)S(1)} %get-tuple-element.144), channel_id=1, source_target_pairs={{0,8},{4,12},{8,0},{12,4},{16,24},{20,28},{24,16},{28,20},{1,9},{5... | collective-permute-start | bytes 786440 | tf_op jit(solution)/shard_map/ppermute | solution.py:636
  191.8 143.4 %collective-permute-start.19 = (bf16[384,1024]{1,0:T(8,128)(2,1)}, bf16[384,1024]{1,0:T(8,128)(2,1)S(1)}, u32[]{:S(2)}, u32[]{:S(2)}) collective-permute-start(bf16[384,1024]{1,0:T(8,128)(2,1)} %get-tuple-element.99), channel_id=1, source_target_pairs={{0,1},{1,0},{2,3},{3,2},{4,5},{5,4},{6,7},{7,6},{8,9},{9,8},{10,11... | collective-permute-start | bytes 2359304 | tf_op jit(solution)/shard_map/ppermute | solution.py:636
  192.7 135.0 %collective-permute-start.15 = (bf16[384,1024]{1,0:T(8,128)(2,1)}, bf16[384,1024]{1,0:T(8,128)(2,1)S(1)}, u32[]{:S(2)}, u32[]{:S(2)}) collective-permute-start(bf16[384,1024]{1,0:T(8,128)(2,1)} %get-tuple-element.93), channel_id=1, source_target_pairs={{0,1},{1,0},{2,3},{3,2},{4,5},{5,4},{6,7},{7,6},{8,9},{9,8},{10,11... | collective-permute-start | bytes 2359304 | tf_op jit(solution)/shard_map/ppermute | solution.py:636
  197.0 127.4 %collective-permute-start.16 = (bf16[384,1024]{1,0:T(8,128)(2,1)}, bf16[384,1024]{1,0:T(8,128)(2,1)S(1)}, u32[]{:S(2)}, u32[]{:S(2)}) collective-permute-start(bf16[384,1024]{1,0:T(8,128)(2,1)} %get-tuple-element.95), channel_id=1, source_target_pairs={{0,1},{1,0},{2,3},{3,2},{4,5},{5,4},{6,7},{7,6},{8,9},{9,8},{10,11... | collective-permute-start | bytes 2359304 | tf_op jit(solution)/shard_map/ppermute | solution.py:636
  197.8 18.3 %collective-permute-start.53 = (bf16[64,1024]{1,0:T(8,128)(2,1)S(1)}, bf16[64,1024]{1,0:T(8,128)(2,1)S(1)}, u32[]{:S(2)}, u32[]{:S(2)}) collective-permute-start(bf16[64,1024]{1,0:T(8,128)(2,1)S(1)} %broadcast_select_fusion.30), channel_id=1, source_target_pairs={{0,16},{4,20},{8,24},{12,28},{16,0},{20,4},{24,8},{28,12},{1,17},{... | collective-permute-start | bytes 393224 | tf_op jit(solution)/shard_map/ppermute | solution.py:636
  216.0 13.7 %collective-permute-start.47 = (bf16[64,1024]{1,0:T(8,128)(2,1)S(1)}, bf16[64,1024]{1,0:T(8,128)(2,1)S(1)}, u32[]{:S(2)}, u32[]{:S(2)}) collective-permute-start(bf16[64,1024]{1,0:T(8,128)(2,1)S(1)} %broadcast_select_fusion.24), channel_id=1, source_target_pairs={{0,8},{4,12},{8,0},{12,4},{16,24},{20,28},{24,16},{28,20},{1,9},{5... | collective-permute-start | bytes 393224 | tf_op jit(solution)/shard_map/ppermute | solution.py:636
  229.8 5.5 %collective-permute-start.59 = (bf16[64,1024]{1,0:T(8,128)(2,1)S(1)}, bf16[64,1024]{1,0:T(8,128)(2,1)S(1)}, u32[]{:S(2)}, u32[]{:S(2)}) collective-permute-start(bf16[64,1024]{1,0:T(8,128)(2,1)S(1)} %broadcast_select_fusion.21), channel_id=1, source_target_pairs={{0,8},{4,12},{8,0},{12,4},{16,24},{20,28},{24,16},{28,20},{1,9},{5... | collective-permute-start | bytes 393224 | tf_op jit(solution)/shard_map/ppermute | solution.py:636
  235.2 12.7 %collective-permute-start.65 = (bf16[64,1024]{1,0:T(8,128)(2,1)S(1)}, bf16[64,1024]{1,0:T(8,128)(2,1)S(1)}, u32[]{:S(2)}, u32[]{:S(2)}) collective-permute-start(bf16[64,1024]{1,0:T(8,128)(2,1)S(1)} %broadcast_select_fusion.27), channel_id=1, source_target_pairs={{0,16},{4,20},{8,24},{12,28},{16,0},{20,4},{24,8},{28,12},{1,17},{... | collective-permute-start | bytes 393224 | tf_op jit(solution)/shard_map/ppermute | solution.py:636
  252.2 5.2 collective-permute-start.48
  257.4 6.3 %collective-permute-start.60 = (bf16[32,1024]{1,0:T(8,128)(2,1)S(1)}, bf16[32,1024]{1,0:T(8,128)(2,1)S(1)}, u32[]{:S(2)}, u32[]{:S(2)}) collective-permute-start(bf16[32,1024]{1,0:T(8,128)(2,1)S(1)} %broadcast_select_fusion.42), channel_id=1, source_target_pairs={{0,16},{4,20},{8,24},{12,28},{16,0},{20,4},{24,8},{28,12},{1,17},{... | collective-permute-start | bytes 196616 | tf_op jit(solution)/shard_map/ppermute | solution.py:636
  272.2 5.2 collective-permute-start.49
  277.4 10.5 %collective-permute-start.61 = (bf16[32,1024]{1,0:T(8,128)(2,1)S(1)}, bf16[32,1024]{1,0:T(8,128)(2,1)S(1)}, u32[]{:S(2)}, u32[]{:S(2)}) collective-permute-start(bf16[32,1024]{1,0:T(8,128)(2,1)S(1)} %add_convert_fusion.21), channel_id=1, source_target_pairs={{0,16},{4,20},{8,24},{12,28},{16,0},{20,4},{24,8},{28,12},{1,17},{... | collective-permute-start | bytes 196616 | tf_op jit(solution)/shard_map/ppermute | solution.py:636
  292.2 13.8 %collective-permute-start.56 = (bf16[64,1024]{1,0:T(8,128)(2,1)S(1)}, bf16[64,1024]{1,0:T(8,128)(2,1)S(1)}, u32[]{:S(2)}, u32[]{:S(2)}) collective-permute-start(bf16[64,1024]{1,0:T(8,128)(2,1)S(1)} %pad_maximum_fusion.12), channel_id=1, source_target_pairs={{0,16},{4,20},{8,24},{12,28},{16,0},{20,4},{24,8},{28,12},{1,17},{... | collective-permute-start | bytes 393224 | tf_op jit(solution)/shard_map/ppermute | solution.py:636
  306.0 5.5 %collective-permute-start.50 = (bf16[64,1024]{1,0:T(8,128)(2,1)S(1)}, bf16[64,1024]{1,0:T(8,128)(2,1)S(1)}, u32[]{:S(2)}, u32[]{:S(2)}) collective-permute-start(bf16[64,1024]{1,0:T(8,128)(2,1)S(1)} %pad_maximum_fusion.11), channel_id=1, source_target_pairs={{0,8},{4,12},{8,0},{12,4},{16,24},{20,28},{24,16},{28,20},{1,9},{5... | collective-permute-start | bytes 393224 | tf_op jit(solution)/shard_map/ppermute | solution.py:636
  311.5 6.3 %collective-permute-start.62 = (bf16[64,1024]{1,0:T(8,128)(2,1)S(1)}, bf16[64,1024]{1,0:T(8,128)(2,1)S(1)}, u32[]{:S(2)}, u32[]{:S(2)}) collective-permute-start(bf16[64,1024]{1,0:T(8,128)(2,1)S(1)} %pad_maximum_fusion.13), channel_id=1, source_target_pairs={{0,8},{4,12},{8,0},{12,4},{16,24},{20,28},{24,16},{28,20},{1,9},{5... | collective-permute-start | bytes 393224 | tf_op jit(solution)/shard_map/ppermute | solution.py:636
  317.8 6.6 %collective-permute-start.68 = (bf16[64,1024]{1,0:T(8,128)(2,1)S(1)}, bf16[64,1024]{1,0:T(8,128)(2,1)S(1)}, u32[]{:S(2)}, u32[]{:S(2)}) collective-permute-start(bf16[64,1024]{1,0:T(8,128)(2,1)S(1)} %pad_maximum_fusion.14), channel_id=1, source_target_pairs={{0,16},{4,20},{8,24},{12,28},{16,0},{20,4},{24,8},{28,12},{1,17},{... | collective-permute-start | bytes 393224 | tf_op jit(solution)/shard_map/ppermute | solution.py:636
  324.4 21.3 %collective-permute-start.57 = (bf16[128,1024]{1,0:T(8,128)(2,1)}, bf16[128,1024]{1,0:T(8,128)(2,1)S(1)}, u32[]{:S(2)}, u32[]{:S(2)}) collective-permute-start(bf16[128,1024]{1,0:T(8,128)(2,1)} %pad_maximum_fusion.5), channel_id=1, source_target_pairs={{0,8},{4,12},{8,0},{12,4},{16,24},{20,28},{24,16},{28,20},{1,9},{5... | collective-permute-start | bytes 786440 | tf_op jit(solution)/shard_map/ppermute | solution.py:636
  324.8 12.5 %collective-permute-start.17 = (bf16[384,1024]{1,0:T(8,128)(2,1)S(1)}, bf16[384,1024]{1,0:T(8,128)(2,1)S(1)}, u32[]{:S(2)}, u32[]{:S(2)}) collective-permute-start(bf16[384,1024]{1,0:T(8,128)(2,1)S(1)} %add_convert_fusion.1), channel_id=1, source_target_pairs={{0,2},{1,3},{2,0},{3,1},{4,6},{5,7},{6,4},{7,5},{8,10},{9,11},{10,... | collective-permute-start | bytes 2359304 | tf_op jit(solution)/shard_map/ppermute | solution.py:636
  327.7 6.4 %collective-permute-start.51 = (bf16[128,1024]{1,0:T(8,128)(2,1)S(1)}, bf16[128,1024]{1,0:T(8,128)(2,1)S(1)}, u32[]{:S(2)}, u32[]{:S(2)}) collective-permute-start(bf16[128,1024]{1,0:T(8,128)(2,1)S(1)} %pad_maximum_fusion.4), channel_id=1, source_target_pairs={{0,4},{4,0},{8,12},{12,8},{16,20},{20,16},{24,28},{28,24},{1,5},{5... | collective-permute-start | bytes 786440 | tf_op jit(solution)/shard_map/ppermute | solution.py:636
  334.1 12.2 %collective-permute-start.63 = (bf16[128,1024]{1,0:T(8,128)(2,1)}, bf16[128,1024]{1,0:T(8,128)(2,1)}, u32[]{:S(2)}, u32[]{:S(2)}) collective-permute-start(bf16[128,1024]{1,0:T(8,128)(2,1)} %pad_maximum_fusion.6), channel_id=1, source_target_pairs={{0,4},{4,0},{8,12},{12,8},{16,20},{20,16},{24,28},{28,24},{1,5},{5... | collective-permute-start | bytes 786440 | tf_op jit(solution)/shard_map/ppermute | solution.py:636
  335.2 28.0 %collective-permute-start.69 = (bf16[128,1024]{1,0:T(8,128)(2,1)}, bf16[128,1024]{1,0:T(8,128)(2,1)}, u32[]{:S(2)}, u32[]{:S(2)}) collective-permute-start(bf16[128,1024]{1,0:T(8,128)(2,1)} %pad_maximum_fusion.7), channel_id=1, source_target_pairs={{0,8},{4,12},{8,0},{12,4},{16,24},{20,28},{24,16},{28,20},{1,9},{5... | collective-permute-start | bytes 786440 | tf_op jit(solution)/shard_map/ppermute | solution.py:636
  343.1 19.1 %collective-permute-start.20 = (bf16[384,1024]{1,0:T(8,128)(2,1)}, bf16[384,1024]{1,0:T(8,128)(2,1)}, u32[]{:S(2)}, u32[]{:S(2)}) collective-permute-start(bf16[384,1024]{1,0:T(8,128)(2,1)} %get-tuple-element.101.ga_ref), channel_id=1, source_target_pairs={{0,2},{1,3},{2,0},{3,1},{4,6},{5,7},{6,4},{7,5},{8,10},{9,11},{10,... | collective-permute-start | bytes 2359304 | tf_op jit(solution)/shard_map/ppermute | solution.py:636
  345.8 25.1 %collective-permute-start.18 = (bf16[384,1024]{1,0:T(8,128)(2,1)}, bf16[384,1024]{1,0:T(8,128)(2,1)}, u32[]{:S(2)}, u32[]{:S(2)}) collective-permute-start(bf16[384,1024]{1,0:T(8,128)(2,1)} %add_convert_fusion.2), channel_id=1, source_target_pairs={{0,2},{1,3},{2,0},{3,1},{4,6},{5,7},{6,4},{7,5},{8,10},{9,11},{10,... | collective-permute-start | bytes 2359304 | tf_op jit(solution)/shard_map/ppermute | solution.py:636
  346.4 30.0 %collective-permute-start.22 = (bf16[384,1024]{1,0:T(8,128)(2,1)}, bf16[384,1024]{1,0:T(8,128)(2,1)}, u32[]{:S(2)}, u32[]{:S(2)}) collective-permute-start(bf16[384,1024]{1,0:T(8,128)(2,1)} %get-tuple-element.101.ga_ref), channel_id=1, source_target_pairs={{0,1},{1,0},{2,3},{3,2},{4,5},{5,4},{6,7},{7,6},{8,9},{9,8},{10,11... | collective-permute-start | bytes 2359304 | tf_op jit(solution)/shard_map/ppermute | solution.py:636
  362.2 20.4 %collective-permute-start.21 = (bf16[384,1024]{1,0:T(8,128)(2,1)}, bf16[384,1024]{1,0:T(8,128)(2,1)}, u32[]{:S(2)}, u32[]{:S(2)}) collective-permute-start(bf16[384,1024]{1,0:T(8,128)(2,1)} %collective-permute-done.20.ga_ref), channel_id=1, source_target_pairs={{0,1},{1,0},{2,3},{3,2},{4,5},{5,4},{6,7},{7,6},{8,9},{9,8},{10,11... | collective-permute-start | bytes 2359304 | tf_op jit(solution)/shard_map/ppermute | solution.py:636
  389.9 29.4 %collective-permute-start.24 = (bf16[80,256]{1,0:T(8,128)(2,1)S(1)}, bf16[80,256]{1,0:T(8,128)(2,1)S(1)}, u32[]{:S(2)}, u32[]{:S(2)}) collective-permute-start(bf16[80,256]{1,0:T(8,128)(2,1)S(1)} %convert_element_type.315), channel_id=1, source_target_pairs={{8,0},{12,4},{16,8},{20,12},{24,16},{28,20},{9,1},{13,5},{17,9},{2... | collective-permute-start | bytes 122888 | tf_op jit(solution)/shard_map/ppermute | solution.py:700
  391.2 28.1 %collective-permute-start.23 = (bf16[80,256]{1,0:T(8,128)(2,1)S(1)}, bf16[80,256]{1,0:T(8,128)(2,1)S(1)}, u32[]{:S(2)}, u32[]{:S(2)}) collective-permute-start(bf16[80,256]{1,0:T(8,128)(2,1)S(1)} %convert_element_type.315), channel_id=1, source_target_pairs={{4,0},{8,4},{12,8},{16,12},{20,16},{24,20},{28,24},{5,1},{9,5},{13... | collective-permute-start | bytes 122888 | tf_op jit(solution)/shard_map/ppermute | solution.py:700
  395.4 45.0 %collective-permute-start.40 = (bf16[128,1024]{1,0:T(8,128)(2,1)S(1)}, bf16[128,1024]{1,0:T(8,128)(2,1)S(1)}, u32[]{:S(2)}, u32[]{:S(2)}) collective-permute-start(bf16[128,1024]{1,0:T(8,128)(2,1)S(1)} %broadcast_select_fusion.12), channel_id=1, source_target_pairs={{0,8},{4,12},{8,0},{12,4},{16,24},{20,28},{24,16},{28,20},{1,9},{5... | collective-permute-start | bytes 786440 | tf_op jit(solution)/shard_map/ppermute | solution.py:636
  440.6 9.5 %collective-permute-start.41 = (bf16[64,1024]{1,0:T(8,128)(2,1)S(1)}, bf16[64,1024]{1,0:T(8,128)(2,1)S(1)}, u32[]{:S(2)}, u32[]{:S(2)}) collective-permute-start(bf16[64,1024]{1,0:T(8,128)(2,1)S(1)} %broadcast_select_fusion.33), channel_id=1, source_target_pairs={{0,16},{4,20},{8,24},{12,28},{16,0},{20,4},{24,8},{28,12},{1,17},{... | collective-permute-start | bytes 393224 | tf_op jit(solution)/shard_map/ppermute | solution.py:636
  444.1 10.5 %collective-permute-start.28 = (bf16[192,1024]{1,0:T(8,128)(2,1)S(1)}, bf16[192,1024]{1,0:T(8,128)(2,1)S(1)}, u32[]{:S(2)}, u32[]{:S(2)}) collective-permute-start(bf16[192,1024]{1,0:T(8,128)(2,1)S(1)} %get-tuple-element.147), channel_id=1, source_target_pairs={{0,4},{4,0},{8,12},{12,8},{16,20},{20,16},{24,28},{28,24},{1,5},{5... | collective-permute-start | bytes 1179656 | tf_op jit(solution)/shard_map/ppermute | solution.py:636
  445.2 12.8 %collective-permute-start.34 = (bf16[192,1024]{1,0:T(8,128)(2,1)S(1)}, bf16[192,1024]{1,0:T(8,128)(2,1)S(1)}, u32[]{:S(2)}, u32[]{:S(2)}) collective-permute-start(bf16[192,1024]{1,0:T(8,128)(2,1)S(1)} %get-tuple-element.148), channel_id=1, source_target_pairs={{0,8},{4,12},{8,0},{12,4},{16,24},{20,28},{24,16},{28,20},{1,9},{5... | collective-permute-start | bytes 1179656 | tf_op jit(solution)/shard_map/ppermute | solution.py:636
  446.3 45.9 %collective-permute-start.26 = (bf16[384,1024]{1,0:T(8,128)(2,1)S(1)}, bf16[384,1024]{1,0:T(8,128)(2,1)S(1)}, u32[]{:S(2)}, u32[]{:S(2)}) collective-permute-start(bf16[384,1024]{1,0:T(8,128)(2,1)S(1)} %copy-done.30), channel_id=1, source_target_pairs={{0,1},{1,0},{2,3},{3,2},{4,5},{5,4},{6,7},{7,6},{8,9},{9,8},{10,11... | collective-permute-start | bytes 2359304 | tf_op jit(solution)/shard_map/ppermute | solution.py:636
  446.3 57.2 %collective-permute-start.25 = (bf16[384,1024]{1,0:T(8,128)(2,1)S(1)}, bf16[384,1024]{1,0:T(8,128)(2,1)S(1)}, u32[]{:S(2)}, u32[]{:S(2)}) collective-permute-start(bf16[384,1024]{1,0:T(8,128)(2,1)S(1)} %copy-done.29), channel_id=1, source_target_pairs={{0,1},{1,0},{2,3},{3,2},{4,5},{5,4},{6,7},{7,6},{8,9},{9,8},{10,11... | collective-permute-start | bytes 2359304 | tf_op jit(solution)/shard_map/ppermute | solution.py:636
  450.2 8.4 %collective-permute-start.42 = (bf16[32,1024]{1,0:T(8,128)(2,1)S(1)}, bf16[32,1024]{1,0:T(8,128)(2,1)S(1)}, u32[]{:S(2)}, u32[]{:S(2)}) collective-permute-start(bf16[32,1024]{1,0:T(8,128)(2,1)S(1)} %broadcast_select_fusion.54), channel_id=1, source_target_pairs={{0,4},{4,0},{8,12},{12,8},{16,20},{20,16},{24,28},{28,24},{1,5},{5... | collective-permute-start | bytes 196616 | tf_op jit(solution)/shard_map/ppermute | solution.py:636
  459.0 14.6 %collective-permute-start.35 = (bf16[96,1024]{1,0:T(8,128)(2,1)S(1)}, bf16[96,1024]{1,0:T(8,128)(2,1)S(1)}, u32[]{:S(2)}, u32[]{:S(2)}) collective-permute-start(bf16[96,1024]{1,0:T(8,128)(2,1)S(1)} %broadcast_select_fusion.15), channel_id=1, source_target_pairs={{0,16},{4,20},{8,24},{12,28},{16,0},{20,4},{24,8},{28,12},{1,17},{... | collective-permute-start | bytes 589832 | tf_op jit(solution)/shard_map/ppermute | solution.py:636
  459.1 14.7 %collective-permute-start.29 = (bf16[96,1024]{1,0:T(8,128)(2,1)S(1)}, bf16[96,1024]{1,0:T(8,128)(2,1)S(1)}, u32[]{:S(2)}, u32[]{:S(2)}) collective-permute-start(bf16[96,1024]{1,0:T(8,128)(2,1)S(1)} %broadcast_select_fusion.18), channel_id=1, source_target_pairs={{0,8},{4,12},{8,0},{12,4},{16,24},{20,28},{24,16},{28,20},{1,9},{5... | collective-permute-start | bytes 589832 | tf_op jit(solution)/shard_map/ppermute | solution.py:636
  463.0 13.0 %collective-permute-start.44 = (bf16[64,1024]{1,0:T(8,128)(2,1)S(1)}, bf16[64,1024]{1,0:T(8,128)(2,1)S(1)}, u32[]{:S(2)}, u32[]{:S(2)}) collective-permute-start(bf16[64,1024]{1,0:T(8,128)(2,1)S(1)} %pad_maximum_fusion.10), channel_id=1, source_target_pairs={{0,16},{4,20},{8,24},{12,28},{16,0},{20,4},{24,8},{28,12},{1,17},{... | collective-permute-start | bytes 393224 | tf_op jit(solution)/shard_map/ppermute | solution.py:636
  473.9 5.6 %collective-permute-start.30 = (bf16[48,1024]{1,0:T(8,128)(2,1)S(1)}, bf16[48,1024]{1,0:T(8,128)(2,1)S(1)}, u32[]{:S(2)}, u32[]{:S(2)}) collective-permute-start(bf16[48,1024]{1,0:T(8,128)(2,1)S(1)} %broadcast_select_fusion.39), channel_id=1, source_target_pairs={{0,16},{4,20},{8,24},{12,28},{16,0},{20,4},{24,8},{28,12},{1,17},{... | collective-permute-start | bytes 294920 | tf_op jit(solution)/shard_map/ppermute | solution.py:636
  476.7 35.1 %collective-permute-start.45 = (bf16[128,1024]{1,0:T(8,128)(2,1)}, bf16[128,1024]{1,0:T(8,128)(2,1)}, u32[]{:S(2)}, u32[]{:S(2)}) collective-permute-start(bf16[128,1024]{1,0:T(8,128)(2,1)} %pad_maximum_fusion.3), channel_id=1, source_target_pairs={{0,8},{4,12},{8,0},{12,4},{16,24},{20,28},{24,16},{28,20},{1,9},{5... | collective-permute-start | bytes 786440 | tf_op jit(solution)/shard_map/ppermute | solution.py:636
  479.6 12.6 %collective-permute-start.31 = (bf16[48,1024]{1,0:T(8,128)(2,1)S(1)}, bf16[48,1024]{1,0:T(8,128)(2,1)S(1)}, u32[]{:S(2)}, u32[]{:S(2)}) collective-permute-start(bf16[48,1024]{1,0:T(8,128)(2,1)S(1)} %add_convert_fusion.19), channel_id=1, source_target_pairs={{0,16},{4,20},{8,24},{12,28},{16,0},{20,4},{24,8},{28,12},{1,17},{... | collective-permute-start | bytes 294920 | tf_op jit(solution)/shard_map/ppermute | solution.py:636
  483.2 12.0 %collective-permute-start.38 = (bf16[96,1024]{1,0:T(8,128)(2,1)S(1)}, bf16[96,1024]{1,0:T(8,128)(2,1)S(1)}, u32[]{:S(2)}, u32[]{:S(2)}) collective-permute-start(bf16[96,1024]{1,0:T(8,128)(2,1)S(1)} %pad_maximum_fusion.9), channel_id=1, source_target_pairs={{0,16},{4,20},{8,24},{12,28},{16,0},{20,4},{24,8},{28,12},{1,17},{... | collective-permute-start | bytes 589832 | tf_op jit(solution)/shard_map/ppermute | solution.py:636
  492.5 12.4 %collective-permute-start.27 = (bf16[384,1024]{1,0:T(8,128)(2,1)S(1)}, bf16[384,1024]{1,0:T(8,128)(2,1)S(1)}, u32[]{:S(2)}, u32[]{:S(2)}) collective-permute-start(bf16[384,1024]{1,0:T(8,128)(2,1)S(1)} %add_convert_fusion), channel_id=1, source_target_pairs={{0,2},{1,3},{2,0},{3,1},{4,6},{5,7},{6,4},{7,5},{8,10},{9,11},{10,... | collective-permute-start | bytes 2359304 | tf_op jit(solution)/shard_map/ppermute | solution.py:636
  495.0 7.9 %collective-permute-start.32 = (bf16[96,1024]{1,0:T(8,128)(2,1)S(1)}, bf16[96,1024]{1,0:T(8,128)(2,1)S(1)}, u32[]{:S(2)}, u32[]{:S(2)}) collective-permute-start(bf16[96,1024]{1,0:T(8,128)(2,1)S(1)} %pad_maximum_fusion.8), channel_id=1, source_target_pairs={{0,8},{4,12},{8,0},{12,4},{16,24},{20,28},{24,16},{28,20},{1,9},{5... | collective-permute-start | bytes 589832 | tf_op jit(solution)/shard_map/ppermute | solution.py:636
  495.3 22.5 %collective-permute-start.39 = (bf16[192,1024]{1,0:T(8,128)(2,1)S(1)}, bf16[192,1024]{1,0:T(8,128)(2,1)}, u32[]{:S(2)}, u32[]{:S(2)}) collective-permute-start(bf16[192,1024]{1,0:T(8,128)(2,1)S(1)} %pad_maximum_fusion.2), channel_id=1, source_target_pairs={{0,8},{4,12},{8,0},{12,4},{16,24},{20,28},{24,16},{28,20},{1,9},{5... | collective-permute-start | bytes 1179656 | tf_op jit(solution)/shard_map/ppermute | solution.py:636
  503.0 18.1 %collective-permute-start.33 = (bf16[192,1024]{1,0:T(8,128)(2,1)S(1)}, bf16[192,1024]{1,0:T(8,128)(2,1)}, u32[]{:S(2)}, u32[]{:S(2)}) collective-permute-start(bf16[192,1024]{1,0:T(8,128)(2,1)S(1)} %pad_maximum_fusion.1), channel_id=1, source_target_pairs={{0,4},{4,0},{8,12},{12,8},{16,20},{20,16},{24,28},{28,24},{1,5},{5... | collective-permute-start | bytes 1179656 | tf_op jit(solution)/shard_map/ppermute | solution.py:636
  524.3 5.1 collective-permute-start.74
  (46 other events, 495.5 us)
Sparse Core Ops, SparseCore 0:
  191.9 118.2 all-reduce.1

commit v4 on v3

v4 whole, which is shorter than its diff:
```python
import functools

import jax
import jax.numpy as jnp
from jax import lax
from jax.experimental import pallas as pl
from jax.experimental.pallas import tpu as pltpu
from jax.sharding import PartitionSpec as P

D = 1024
HEAD = 64
CHUNK = 384
CROP_MAX = 3072
PACK = HEAD + 16

BF = jnp.bfloat16
F32 = jnp.float32
precise = lax.Precision.HIGHEST


def nn(a, b):
    return lax.dot_general(a, b, (((1,), (0,)), ((), ())), preferred_element_type=F32)


def nt(a, b):
    return lax.dot_general(a, b, (((1,), (1,)), ((), ())), preferred_element_type=F32)


def tn(a, b):
    return lax.dot_general(a, b, (((0,), (0,)), ((), ())), preferred_element_type=F32)


def same_head(width):
    row = lax.broadcasted_iota(jnp.int32, (width, width), 0) // HEAD
    col = lax.broadcasted_iota(jnp.int32, (width, width), 1) // HEAD
    return row == col


def lane_head(rows, width):
    return lax.broadcasted_iota(jnp.int32, (rows, width), 1) // HEAD


def causal(rows):
    row = lax.broadcasted_iota(jnp.int32, (rows, rows), 0)
    col = lax.broadcasted_iota(jnp.int32, (rows, rows), 1)
    return row >= col


def fold_heads(full, width):
    out = full[0:HEAD]
    for h in range(1, width // HEAD):
        out = out + full[h * HEAD : (h + 1) * HEAD]
    return out


def spread_heads(part, width, block):
    tall = jnp.concatenate([part] * (width // HEAD), axis=0)
    return jnp.where(block, tall, jnp.zeros_like(tall))


def pick(mask, value):
    return jnp.where(mask, value, jnp.zeros_like(value))


def vmem():
    return pl.BlockSpec(memory_space=pltpu.VMEM)


def smem():
    return pl.BlockSpec(memory_space=pltpu.SMEM)


def shape(rows, cols, kind):
    return jax.ShapeDtypeStruct((rows, cols), kind)


ROW_TILE = 192


def tiles(rows):
    return [slice(i, i + ROW_TILE) for i in range(0, rows, ROW_TILE)]


def kernel(body, name, out_shape, in_specs, megabytes, flops=0, scratch=(), aliases=None):
    outs = vmem() if not isinstance(out_shape, tuple) else (vmem(),) * len(out_shape)
    return pl.pallas_call(
        body,
        out_shape=out_shape,
        in_specs=in_specs,
        out_specs=outs,
        scratch_shapes=list(scratch),
        input_output_aliases=aliases or {},
        compiler_params=pltpu.CompilerParams(vmem_limit_bytes=megabytes << 20),
        cost_estimate=pl.CostEstimate(flops=int(flops), bytes_accessed=0, transcendentals=0),
        name=name,
    )


US = 10**9


def normal(values):
    centre = jnp.mean(values, axis=-1, keepdims=True)
    moved = values - centre
    scale = lax.rsqrt(jnp.mean(moved * moved, axis=-1, keepdims=True) + 1e-05)
    return moved * scale, scale


def normal_back(grad, gain, xhat, scale):
    g = grad * gain
    return scale * (
        g - jnp.mean(g, axis=-1, keepdims=True) - xhat * jnp.mean(g * xhat, axis=-1, keepdims=True)
    )


def total(refs):
    value = refs[0][...].astype(F32)
    for ref in refs[1:]:
        value = value + ref[...].astype(F32)
    return value


def norm_body(x_ref, gain_ref, bias_ref, out_ref):
    for at in tiles(x_ref.shape[0]):
        xhat, _ = normal(x_ref[at, :].astype(F32))
        out_ref[at, :] = (xhat * gain_ref[...] + bias_ref[...]).astype(BF)


def norm_one(x, gain, bias):
    call = kernel(norm_body, "norm_one", shape(x.shape[0], D, BF), [vmem()] * 3, 8, 2 * US)
    return call(x, gain, bias)


def total(refs, at):
    value = refs[0][at, :].astype(F32)
    for ref in refs[1:]:
        value = value + ref[at, :].astype(F32)
    return value


def middle_body(*refs):
    x_ref, gain_ref, bias_ref = refs[:3]
    parts = refs[3:-3]
    middle_ref, out_ref, square_ref = refs[-3:]
    for at in tiles(x_ref.shape[0]):
        attended = total(parts, at)
        middle = x_ref[at, :].astype(F32) + attended
        middle_ref[at, :] = middle
        xhat, _ = normal(middle)
        out_ref[at, :] = (xhat * gain_ref[...] + bias_ref[...]).astype(BF)
        square_ref[at, :] = jnp.sum(attended * attended, axis=-1, keepdims=True)


def norm_two(x, gain, bias, parts):
    rows = x.shape[0]
    call = kernel(
        middle_body, "norm_two", (shape(rows, D, F32), shape(rows, D, BF), shape(rows, 1, F32)),
        [vmem()] * (3 + len(parts)), 12, 3 * US,
    )
    return call(x, gain, bias, *parts)


def middle_back_body(*refs):
    grad_ref, middle_ref, gain_ref = refs[:3]
    parts = refs[3:-4]
    wide_ref, low_ref, gain_grad_ref, bias_grad_ref = refs[-4:]
    gain_grad = bias_grad = jnp.zeros(gain_ref.shape, F32)
    for at in tiles(grad_ref.shape[0]):
        grad = total(parts, at)
        xhat, scale = normal(middle_ref[at, :])
        gain_grad = gain_grad + jnp.sum(grad * xhat, axis=0, keepdims=True)
        bias_grad = bias_grad + jnp.sum(grad, axis=0, keepdims=True)
        out = grad_ref[at, :].astype(F32) + normal_back(grad, gain_ref[...], xhat, scale)
        wide_ref[at, :] = out
        low_ref[at, :] = out.astype(BF)
    gain_grad_ref[...] = gain_grad
    bias_grad_ref[...] = bias_grad


def norm_two_back(grad, middle, gain, parts):
    rows = grad.shape[0]
    call = kernel(
        middle_back_body, "norm_two_back",
        (shape(rows, D, F32), shape(rows, D, BF), shape(1, D, F32), shape(1, D, F32)),
        [vmem()] * (3 + len(parts)), 16, 4 * US,
    )
    return call(grad, middle, gain, *parts)


def pixels_back_body(*refs):
    x_ref, wide_ref, gain_ref = refs[:3]
    parts = refs[3:-3]
    out_ref, gain_grad_ref, bias_grad_ref = refs[-3:]
    gain_grad = bias_grad = jnp.zeros(gain_ref.shape, F32)
    for at in tiles(x_ref.shape[0]):
        grad = total(parts, at)
        xhat, scale = normal(x_ref[at, :].astype(F32))
        gain_grad = gain_grad + jnp.sum(grad * xhat, axis=0, keepdims=True)
        bias_grad = bias_grad + jnp.sum(grad, axis=0, keepdims=True)
        out_ref[at, :] = (wide_ref[at, :] + normal_back(grad, gain_ref[...], xhat, scale)).astype(BF)
    gain_grad_ref[...] = gain_grad
    bias_grad_ref[...] = bias_grad


def norm_one_back(x, wide, gain, parts):
    rows = x.shape[0]
    call = kernel(
        pixels_back_body, "norm_one_back", (shape(rows, D, BF), shape(1, D, F32), shape(1, D, F32)),
        [vmem()] * (3 + len(parts)), 16, 4 * US,
    )
    return call(x, wide, gain, *parts)


def result_body(*refs):
    middle_ref = refs[0]
    parts = refs[1:-3]
    out_ref, result_square_ref, branch_square_ref = refs[-3:]
    for at in tiles(middle_ref.shape[0]):
        branch = total(parts, at)
        result = middle_ref[at, :] + branch
        out_ref[at, :] = result.astype(BF)
        result_square_ref[at, :] = jnp.sum(result * result, axis=-1, keepdims=True)
        branch_square_ref[at, :] = jnp.sum(branch * branch, axis=-1, keepdims=True)


def finish(middle, parts):
    rows = middle.shape[0]
    call = kernel(
        result_body, "finish", (shape(rows, D, BF), shape(rows, 1, F32), shape(rows, 1, F32)),
        [vmem()] * (1 + len(parts)), 12, 2 * US,
    )
    return call(middle, *parts)


def pair_slices(pair, rows):
    for i in range(2):
        yield i, slice(i * rows, (i + 1) * rows), slice((2 * pair + i) * rows, (2 * pair + i + 1) * rows)


def qkv_body(pair, tail_ref, xa_ref, xb_ref, w_ref, valid_ref, seg_ref, was_ref, *rest):
    q_ref, k_ref, v_ref, pack_ref = rest[-4:]
    width = q_ref.shape[1]
    block = same_head(width)
    state, sums = was_ref[0:HEAD, :], was_ref[HEAD:PACK, :]
    for i, _, at in pair_slices(pair, xa_ref.shape[0]):
        x = (xa_ref, xb_ref)[i][...]
        q_ref[at, :] = feature(nn(x, w_ref[0])).astype(BF)
        k = (feature(nn(x, w_ref[1])) * valid_ref[at, :]).astype(BF)
        v = nn(x, w_ref[2]).astype(BF)
        k_ref[at, :] = k
        v_ref[at, :] = v
        kept = pick(seg_ref[at, :] == tail_ref[0], k)
        state = state + fold_heads(pick(block, tn(kept, v)), width)
        sums = sums + jnp.sum(kept.astype(F32), axis=0, keepdims=True)
    pack_ref[0:HEAD, :] = state
    pack_ref[HEAD:PACK, :] = sums


def project_qkv(pair, tail, xa, xb, w, valid, seg, was, made):
    width, whole = w.shape[2], valid.shape[0]
    call = kernel(
        functools.partial(qkv_body, pair), "project_qkv",
        (shape(whole, width, BF),) * 3 + (shape(PACK, width, F32),),
        [smem()] + [vmem()] * (6 + len(made)), 16, 4 * US,
        aliases={7 + i: i for i in range(len(made))},
    )
    return call(tail, xa, xb, w, valid, seg, was, *made)


def swap_heads(x):
    return jnp.concatenate(
        [pltpu.roll(x[:, i : i + 2 * HEAD], HEAD, 1) for i in range(0, x.shape[1], 2 * HEAD)], axis=1
    )


def forward_body(
    last_ref, spot_ref, q_ref, k_ref, v_ref, segc_ref, segr_ref, num_ref, den_ref, st_ref, ks_ref
):
    rows, width = q_ref.shape
    size = CHUNK
    block = same_head(width)
    ones_block = block.astype(BF)
    lanes = lane_head(size, width)
    even = (lanes % 2) == 0
    lower = causal(size)
    st_ref[...] = jnp.zeros_like(st_ref)
    ks_ref[...] = jnp.zeros_like(ks_ref)

    def step(c, carry):
        spot = spot_ref[c]
        at = pl.ds(pl.multiple_of(spot * size, size), size)
        q, k, v = q_ref[at, :], k_ref[at, :], v_ref[at, :]
        seg = segc_ref[at, :]
        keep = (lower & (seg == segr_ref[spot])).astype(BF)
        before, after = last_ref[c], last_ref[c + 1]
        carried = (seg == before).astype(F32)
        sums = [jnp.zeros((size, width), F32)] * 2
        for h in range(width // HEAD):
            mine = lanes == h
            score = nt(pick(mine, q), k).astype(BF) * keep
            both = jnp.where(mine, v, (lanes == (h ^ 1)).astype(BF))
            sums[h % 2] = sums[h % 2] + nn(score, both)
        num = jnp.where(even, sums[0], sums[1])
        den = swap_heads(jnp.where(even, sums[1], sums[0]))
        num_ref[at, :] = num + carried * nn(q, st_ref[...].astype(BF))
        den_ref[at, :] = den + carried * nn((q.astype(F32) * ks_ref[0:1, :]).astype(BF), ones_block)
        kept = pick(seg == after, k)
        cont = (before == after).astype(F32)
        st_ref[...] = cont * st_ref[...] + pick(block, tn(kept, v))
        ks_ref[...] = cont * ks_ref[...] + jnp.sum(kept.astype(F32), axis=0, keepdims=True)
        return carry

    lax.fori_loop(0, rows // size, step, 0)


def attend(last, spot, q, k, v, segc, segr):
    rows, width = q.shape
    call = kernel(
        forward_body, "attend", (shape(rows, width, F32),) * 2, [smem()] * 2 + [vmem()] * 5, 24, 7 * US,
        scratch=[pltpu.VMEM((width, width), F32), pltpu.VMEM((8, width), F32)],
    )
    return call(last, spot, q, k, v, segc, segr)


def project_body(
    pair, first_ref, num_ref, den_ref, q_ref, pack_ref, segc_ref, valid_ref, w_ref,
    heads_ref, wide_ref, rinv_ref, a_ref, b_ref
):
    width = q_ref.shape[1]
    block = same_head(width)
    state = spread_heads(pack_ref[0:HEAD, :], width, block).astype(BF)
    sums = pack_ref[HEAD : HEAD + 1, :]
    for i, own, at in pair_slices(pair, a_ref.shape[0]):
        q = q_ref[at, :]
        opening = (segc_ref[at, :] == first_ref[0]).astype(F32)
        valid = valid_ref[at, :]
        num = num_ref[at, :] + opening * nn(q, state)
        den = den_ref[at, :] + opening * nn((q.astype(F32) * sums).astype(BF), block.astype(BF))
        rinv = valid / (den + 1e-06 + 1.0 - valid)
        wide = num * rinv
        heads = wide.astype(BF)
        heads_ref[own, :] = heads
        wide_ref[own, :] = wide
        rinv_ref[own, :] = rinv
        (a_ref, b_ref)[i][...] = nn(heads, w_ref[...]).astype(BF)


def project(pair, rows, last, num, den, q, pack, segc, valid, w):
    width = q.shape[1]
    call = kernel(
        functools.partial(project_body, pair), "project",
        (shape(2 * rows, width, BF), shape(2 * rows, width, F32), shape(2 * rows, width, F32))
        + (shape(rows, D, BF),) * 2,
        [smem()] + [vmem()] * 7, 12, 3 * US,
    )
    return call(last, num, den, q, pack, segc, valid, w)


def mlp_body(
    xa_ref, xb_ref, ga_ref, gb_ref, up_ref, down_ref, act_ref, hid_ref, na_ref, nb_ref, ba_ref, bb_ref
):
    root = 0.7978845608028654
    tile = min(512, up_ref.shape[1])
    for i, own, _ in pair_slices(0, xa_ref.shape[0]):
        x, g = (xa_ref, xb_ref)[i][...], (ga_ref, gb_ref)[i][...]
        for j in range(0, up_ref.shape[1], tile):
            cols = slice(j, j + tile)
            h = nn(x, up_ref[:, cols])
            grad = nt(g, down_ref[cols, :])
            square = h * h
            t = jnp.tanh(root * h * (1.0 + 0.044715 * square))
            plus = 0.5 * (1.0 + t)
            slope = plus + 0.5 * h * (1.0 - t * t) * (root + (3.0 * 0.044715 * root) * square)
            act_ref[own, cols] = (h * plus).astype(BF)
            hid_ref[own, cols] = (grad * slope).astype(BF)
        (na_ref, nb_ref)[i][...] = nt(hid_ref[own, :], up_ref[...]).astype(BF)
        (ba_ref, bb_ref)[i][...] = nn(act_ref[own, :], down_ref[...]).astype(BF)


def mlp(xa, xb, ga, gb, up, down):
    rows, hidden = xa.shape[0], up.shape[1]
    call = kernel(
        mlp_body, "mlp", (shape(2 * rows, hidden, BF),) * 2 + (shape(rows, D, BF),) * 4,
        [vmem()] * 6, 32, 9 * US,
    )
    return call(xa, xb, ga, gb, up, down)


def heads_back_body(
    pair, first_ref, ga_ref, gb_ref, w_ref, wide_ref, rinv_ref, q_ref, segc_ref, was_ref, *rest
):
    ng_ref, dg_ref, pack_ref = rest[-3:]
    width = q_ref.shape[1]
    block = same_head(width)
    ones_block = block.astype(BF)
    state, sums = was_ref[0:HEAD, :], was_ref[HEAD:PACK, :]
    for i, own, at in pair_slices(pair, ga_ref.shape[0]):
        hg = nt((ga_ref, gb_ref)[i][...], w_ref[...])
        rinv = rinv_ref[own, :]
        ng = (hg * rinv).astype(BF)
        prod = hg * wide_ref[own, :]
        high = prod.astype(BF)
        low = (prod - high.astype(F32)).astype(BF)
        dg = -(nn(high, ones_block) + nn(low, ones_block)) * rinv
        ng_ref[at, :] = ng
        dg_ref[at, :] = dg
        opened = pick(segc_ref[at, :] == first_ref[0], q_ref[at, :])
        state = state + fold_heads(pick(block, tn(opened, ng)), width)
        sums = sums + jnp.sum(opened.astype(F32) * dg, axis=0, keepdims=True)
    pack_ref[0:HEAD, :] = state
    pack_ref[HEAD:PACK, :] = sums


def heads_back(pair, last, ga, gb, w, wide, rinv, q, segc, was, made):
    whole, width = q.shape
    call = kernel(
        functools.partial(heads_back_body, pair), "heads_back",
        (shape(whole, width, BF), shape(whole, width, F32), shape(PACK, width, F32)),
        [smem()] + [vmem()] * (8 + len(made)), 16, 4 * US,
        aliases={9 + i: i for i in range(len(made))},
    )
    return call(last, ga, gb, w, wide, rinv, q, segc, was, *made)


def backward_body(
    last_ref, spot_ref, q_ref, k_ref, v_ref, ng_ref, dg_ref, segc_ref, segr_ref, pack_ref,
    dq_ref, dk_ref, dv_ref, all_ref, sums_ref, st_ref, ks_ref
):
    rows, width = q_ref.shape
    size = CHUNK
    count = rows // size
    block = same_head(width)
    lanes = lane_head(size, width)
    half = (lax.broadcasted_iota(jnp.int32, (size, width), 1) % HEAD) < HEAD // 2
    lower = causal(size)
    st_ref[...] = spread_heads(pack_ref[0:HEAD, :], width, block)
    ks_ref[...] = jnp.broadcast_to(pack_ref[HEAD : HEAD + 1, :], ks_ref.shape)

    def collect(c, carry):
        at = pl.ds(pl.multiple_of(spot_ref[c] * size, size), size)
        all_ref[c] = st_ref[...].astype(BF)
        sums_ref[c] = ks_ref[...]
        before, after = last_ref[c], last_ref[c + 1]
        kept = pick(segc_ref[at, :] == after, k_ref[at, :])
        cont = (before == after).astype(F32)
        st_ref[...] = cont * st_ref[...] + pick(block, tn(kept, v_ref[at, :]))
        ks_ref[...] = cont * ks_ref[...] + jnp.sum(kept.astype(F32), axis=0, keepdims=True)
        return carry

    lax.fori_loop(0, count, collect, 0)
    st_ref[...] = jnp.zeros_like(st_ref)
    ks_ref[...] = jnp.zeros_like(ks_ref)

    def step(i, carry):
        c = count - 1 - i
        spot = spot_ref[c]
        at = pl.ds(pl.multiple_of(spot * size, size), size)
        q, k, v, ng, dg = q_ref[at, :], k_ref[at, :], v_ref[at, :], ng_ref[at, :], dg_ref[at, :]
        seg = segc_ref[at, :]
        keep = (lower & (seg == segr_ref[spot])).astype(BF)
        before, after = last_ref[c], last_ref[c + 1]
        opened = seg == before
        carried = opened.astype(F32)
        tail = (seg == after).astype(F32)
        grad_state = st_ref[...].astype(BF)
        moved = swap_heads(dg)
        high = moved.astype(BF)
        low = (moved - high.astype(F32)).astype(BF)
        terms = jnp.where(half, high, low) * jnp.asarray(2.0 / HEAD, BF)
        one = jnp.ones((), BF)
        dq = carried * (nt(ng, all_ref[c]) + dg * sums_ref[c][0:1, :])
        dk = tail * (nt(v, grad_state) + ks_ref[0:1, :])
        dv = tail * nn(k, grad_state)
        for h in range(width // HEAD):
            mine = lanes == h
            qh, kh, nh = pick(mine, q), pick(mine, k), pick(mine, ng)
            score = nt(qh, k).astype(BF) * keep
            left = jnp.where(mine, ng, pick(lanes == (h ^ 1), terms))
            back = nt(left, jnp.where(mine, v, one)).astype(BF) * keep
            dq = dq + nn(back, kh)
            dk = dk + tn(back, qh)
            dv = dv + tn(score, nh)
        dq_ref[at, :] = (dq * jnp.minimum(q.astype(F32), 1.0)).astype(BF)
        dk_ref[at, :] = dk
        dv_ref[at, :] = dv
        cont = (before == after).astype(F32)
        st_ref[...] = cont * st_ref[...] + pick(block, tn(pick(opened, q), ng))
        ks_ref[...] = cont * ks_ref[...] + jnp.sum(carried * q.astype(F32) * dg, axis=0, keepdims=True)
        return carry

    lax.fori_loop(0, count, step, 0)


def attend_back(last, spot, q, k, v, ng, dg, segc, segr, pack):
    rows, width = q.shape
    count = rows // CHUNK
    call = kernel(
        backward_body, "attend_back",
        (shape(rows, width, BF), shape(rows, width, F32), shape(rows, width, F32)),
        [smem()] * 2 + [vmem()] * 8, 32, 15 * US,
        scratch=[
            pltpu.VMEM((count, width, width), BF),
            pltpu.VMEM((count, 8, width), F32),
            pltpu.VMEM((width, width), F32),
            pltpu.VMEM((8, width), F32),
        ],
    )
    return call(last, spot, q, k, v, ng, dg, segc, segr, pack)


def mix_body(
    pair, tail_ref, dq_ref, dk_ref, dv_ref, k_ref, v_ref, segc_ref, valid_ref, pack_ref, w_ref,
    mixed_ref, a_ref, b_ref
):
    width = k_ref.shape[1]
    block = same_head(width)
    state = spread_heads(pack_ref[0:HEAD, :], width, block).astype(BF)
    sums = pack_ref[HEAD : HEAD + 1, :]
    for i, own, at in pair_slices(pair, a_ref.shape[0]):
        tail = (segc_ref[at, :] == tail_ref[0]).astype(F32)
        k = k_ref[at, :]
        dk = dk_ref[at, :] + tail * (nt(v_ref[at, :], state) + sums)
        dv = dv_ref[at, :] + tail * nn(k, state)
        dq = dq_ref[at, :]
        dk = (valid_ref[at, :] * dk * jnp.minimum(k.astype(F32), 1.0)).astype(BF)
        dv = dv.astype(BF)
        mixed_ref[own, 0:width] = dq
        mixed_ref[own, width : 2 * width] = dk
        mixed_ref[own, 2 * width : 3 * width] = dv
        out = nt(dq, w_ref[0]) + nt(dk, w_ref[1]) + nt(dv, w_ref[2])
        (a_ref, b_ref)[i][...] = out.astype(BF)


def mix(pair, rows, tail, dq, dk, dv, k, v, segc, valid, pack, w):
    width = k.shape[1]
    call = kernel(
        functools.partial(mix_body, pair), "mix",
        (shape(2 * rows, 3 * width, BF),) + (shape(rows, D, BF),) * 2,
        [smem()] + [vmem()] * 9, 16, 4 * US,
    )
    return call(tail, dq, dk, dv, k, v, segc, valid, pack, w)


def feature(values):
    return jnp.where(values > 0, values + 1.0, jnp.exp(jnp.minimum(values, 0.0)))


def bits_of(count):
    return [1 << b for b in range(count.bit_length() - 1)]


def swap(value, axis, bit):
    return lax.ppermute(value, axis, [(i, i ^ bit) for i in range(lax.axis_size(axis))])


def gather_slots(value):
    slots = {0: value}
    for bit in reversed(bits_of(lax.axis_size("feat"))):
        for s in sorted(slots):
            slots[s | bit] = swap(slots[s], "feat", bit)
    return [slots[s] for s in range(len(slots))]


def scatter_slots(parts, after=None):
    parts = {s: [part] for s, part in enumerate(parts)}
    for bit in bits_of(lax.axis_size("feat")):
        for s in sorted(parts, reverse=True):
            if s & bit:
                pieces = parts.pop(s)
                value = pieces[0]
                if len(pieces) > 1:
                    value = functools.reduce(jnp.add, [p.astype(F32) for p in pieces]).astype(BF)
                if after is not None and bit > 1:
                    value = lax.optimization_barrier((value, after))[0]
                parts[s ^ bit].append(swap(value, "feat", bit))
    return parts[0]


def sum_everywhere(value):
    for axis in ("feat", "rows"):
        for bit in bits_of(lax.axis_size(axis)):
            value = value + swap(value, axis, bit)
    return value


def sum_rows(value, order):
    here = lax.axis_index("rows")
    for bit in order:
        half = value.shape[0] // 2
        upper = (here & bit) != 0
        low, high = value[:half], value[half:]
        got = swap(jnp.where(upper, low, high), "rows", bit)
        value = (jnp.where(upper, high, low).astype(F32) + got.astype(F32)).astype(BF)
    for bit in reversed(order):
        upper = (here & bit) != 0
        got = swap(value, "rows", bit)
        value = jnp.concatenate([jnp.where(upper, got, value), jnp.where(upper, value, got)], axis=0)
    return value


def sum_pieces(value, count, order, turned):
    size = value.shape[0] // count
    return jnp.concatenate(
        [
            sum_rows(value[i * size : (i + 1) * size], turned if i % 2 else order)
            for i in range(count)
        ],
        axis=0,
    )


def shifted(pack, hop, groups, reverse):
    if reverse:
        pairs = [(i, i - hop) for i in range(hop, groups)]
    else:
        pairs = [(i, i + hop) for i in range(groups - hop)]
    return lax.ppermute(pack, "rows", pairs)


def gather_carry(pack, crops_at, here, groups, reach, reverse):
    total = jnp.zeros(pack.shape, F32)
    mine = crops_at[here + 1] if reverse else crops_at[here]
    for hop in range(1, reach + 1):
        got = shifted(pack, hop, groups, reverse).astype(F32)
        other = here + hop if reverse else here - hop
        inside = (other < groups) if reverse else (other >= 0)
        at = jnp.clip(other, 0, groups - 1)
        theirs = crops_at[at] if reverse else crops_at[at + 1]
        total = total + jnp.where(inside & (theirs == mine), got, 0.0)
    return total


def on_device(
    pixels,
    qkv_weight,
    out_weight,
    up_weight,
    down_weight,
    norm1_gain,
    norm1_bias,
    norm2_gain,
    norm2_bias,
    crop_lengths,
    crop_offsets,
    pixel_mask,
    out_grad,
):
    local_rows = pixels.shape[0]
    group_rows = pixel_mask.shape[0]
    width = qkv_weight.shape[2]
    crop_count = crop_offsets.shape[0]
    groups = lax.axis_size("rows")
    members = lax.axis_size("feat")
    pairs = members // 2
    here = lax.axis_index("rows")
    member = lax.axis_index("feat")
    reach = min(groups - 1, -(-(CROP_MAX - 1) // group_rows))
    group_start = here * group_rows
    slot_ids = jnp.arange(members, dtype=jnp.int32) ^ member
    in_group = (slot_ids[:, None] * local_rows + jnp.arange(local_rows, dtype=jnp.int32)[None, :]).reshape(-1)
    places = group_start + in_group
    started = crop_offsets[None, :] <= places[:, None]
    crop_ends = crop_offsets + crop_lengths
    segment = jnp.sum(started.astype(jnp.int32), axis=1) - 1
    inside = jnp.sum((started & (places[:, None] < crop_ends[None, :])).astype(jnp.int32), axis=1)
    mask = jnp.concatenate(
        [
            lax.dynamic_slice_in_dim(pixel_mask, (member ^ s) * local_rows, local_rows)
            for s in range(members)
        ]
    )
    pixel_valid = (mask * inside).astype(F32)
    edges = jnp.arange(groups + 1, dtype=jnp.int32) * group_rows - 1
    crops_at = jnp.sum((crop_offsets[None, :] <= edges[:, None]).astype(jnp.int32), axis=1) - 1
    chunks = group_rows // CHUNK
    per = local_rows // CHUNK
    chunk_edges = group_start - 1 + jnp.arange(chunks + 1, dtype=jnp.int32) * CHUNK
    last = jnp.sum((crop_offsets[None, :] <= chunk_edges[:, None]).astype(jnp.int32), axis=1) - 1
    tail = last[-1:]
    order = jnp.arange(chunks, dtype=jnp.int32)
    spot = ((order // per) ^ member) * per + order % per
    segc = segment[:, None]
    segr = segment.reshape(chunks, 1, CHUNK)
    validc = pixel_valid[:, None]
    gain1, bias1, gain2, bias2 = (
        a[None, :] for a in (norm1_gain, norm1_bias, norm2_gain, norm2_bias)
    )
    no_pack = jnp.zeros((PACK, width), F32)

    normed_slots = gather_slots(norm_one(pixels, gain1, bias1))
    late_grad = lax.optimization_barrier((out_grad, normed_slots[members // 2]))[0]
    grad_slots = gather_slots(late_grad)
    made, pack = (), no_pack
    for p in range(pairs):
        *made, pack = project_qkv(
            p, tail, normed_slots[2 * p], normed_slots[2 * p + 1], qkv_weight, validc, segc, pack, made
        )
    q, k, v = made
    carry = gather_carry(pack.astype(BF), crops_at, here, groups, reach, False)
    num, den = attend(last, spot, q, k, v, segc, segr)
    sent = {
        p: project(p, local_rows, last, num, den, q, carry, segc, validc, out_weight)
        for p in reversed(range(pairs))
    }
    parts = [sent[s // 2][3 + s % 2] for s in range(members)]
    middle, normed_two, attended_square = norm_two(pixels, gain2, bias2, scatter_slots(parts))
    two_slots = gather_slots(normed_two)
    hidden = [
        mlp(*two_slots[2 * p : 2 * p + 2], *grad_slots[2 * p : 2 * p + 2], up_weight, down_weight)
        for p in range(pairs)
    ]
    two_parts = scatter_slots([hidden[s // 2][2 + s % 2] for s in range(members)])
    branch_parts = scatter_slots([hidden[s // 2][4 + s % 2] for s in range(members)], two_parts[-1])
    grad_all = jnp.concatenate(grad_slots, axis=0)
    down_grad = tn(jnp.concatenate([h[0] for h in hidden], axis=0), grad_all).astype(BF)
    up_grad = tn(jnp.concatenate(two_slots, axis=0), jnp.concatenate([h[1] for h in hidden], axis=0)).astype(BF)
    middle_grad, middle_low, gain2_grad, bias2_grad = norm_two_back(out_grad, middle, gain2, two_parts)
    middle_slots = gather_slots(middle_low)
    made, grad_pack = (), no_pack
    for p in range(pairs):
        *made, grad_pack = heads_back(
            p, last, middle_slots[2 * p], middle_slots[2 * p + 1], out_weight,
            sent[p][1], sent[p][2], q, segc, grad_pack, made
        )
    ng, dg = made
    grad_carry = gather_carry(grad_pack.astype(BF), crops_at, here, groups, reach, True)
    out_weight_grad = tn(
        jnp.concatenate([sent[p][0] for p in range(pairs)], axis=0), jnp.concatenate(middle_slots, axis=0)
    ).astype(BF)
    dq, dk, dv = attend_back(last, spot, q, k, v, ng, dg, segc, segr, carry)
    mixes = {
        p: mix(p, local_rows, tail, dq, dk, dv, k, v, segc, validc, grad_carry, qkv_weight)
        for p in reversed(range(pairs))
    }
    normed_parts = scatter_slots([mixes[s // 2][1 + s % 2] for s in range(members)])
    mixed_grad = jnp.concatenate([mixes[p][0] for p in range(pairs)], axis=0)
    qkv_grad = tn(mixed_grad, jnp.concatenate(normed_slots, axis=0)).astype(BF)
    output, result_square, branch_square = finish(middle, branch_parts)
    pixels_grad, gain1_grad, bias1_grad = norm_one_back(pixels, middle_grad, gain1, normed_parts)

    bits = bits_of(groups)
    turned = bits[1:] + bits[:1]
    down_grad = lax.psum(down_grad, "rows").astype(F32)
    up_grad = lax.psum(up_grad, "rows").astype(F32)
    out_weight_grad = sum_rows(out_weight_grad, turned).astype(F32)
    qkv_grad = sum_pieces(qkv_grad, 2, bits, turned)
    qkv_grad = jnp.swapaxes(qkv_grad.reshape(3, width, D), 1, 2).astype(F32)

    crop_onehot = (
        segment[:local_rows, None] == jnp.arange(crop_count, dtype=jnp.int32)[None, :]
    ).astype(F32)
    squares = (
        jnp.concatenate(
            [result_square, attended_square, branch_square, jnp.ones((local_rows, 1), F32)], axis=1
        )
        * validc[:local_rows]
    )
    crop_sums = lax.dot_general(
        squares, crop_onehot, (((0,), (0,)), ((), ())), precision=precise, preferred_element_type=F32
    )
    sums = jnp.concatenate(
        [gain1_grad[0], bias1_grad[0], gain2_grad[0], bias2_grad[0], crop_sums.reshape(-1)]
    )
    sums = sum_everywhere(sums)
    gain1_grad, bias1_grad, gain2_grad, bias2_grad = sums[: 4 * D].reshape(4, D)
    crop_sums = sums[4 * D :].reshape(4, crop_count)
    crop_rms = jnp.sqrt(crop_sums[:3] / (D * jnp.maximum(crop_sums[3], 1.0))[None, :])
    return (
        output,
        pixels_grad,
        qkv_grad,
        out_weight_grad,
        up_grad,
        down_grad,
        gain1_grad,
        bias1_grad,
        gain2_grad,
        bias2_grad,
        crop_rms,
    )


def solution(mesh):
    split = P(("rows", "feat"), None)
    qkv, rows_feat, cols_feat = P(None, None, "feat"), P("feat", None), P(None, "feat")
    in_specs = (
        (split, qkv, rows_feat, cols_feat, rows_feat) + (P(),) * 6 + (P("rows"), split)
    )
    out_specs = (split, split, qkv, rows_feat, cols_feat, rows_feat) + (P(),) * 5
    return jax.shard_map(
        on_device, mesh=mesh, in_specs=in_specs, out_specs=out_specs, check_vma=False
    )
```

time: 548 us -> 401 us (0.73)
  Pallas kernels: 134 us -> 67.4 us
  waiting for transfers between devices: 255 us -> 196 us
  starting transfers between devices: 60.1 us -> 44.8 us
  local copies, waits for them, and re-layouts: 16.2 us -> 31.3 us
  other arithmetic: 31.4 us -> 17.4 us
    ppermute x71 -> x47, waiting for transfers between devices: 255 us -> 176 us  [swap(): lax.ppermute(value, axis, [(i, i ^ bit) for i in range(lax.axis_size(axis...]
    pallas_call x17, Pallas kernels: 134 us -> 67.4 us  [the longest x2 16.6 us: mlp(): return call(xa, xb, ga, gb, up, down)]
    psum x1, waiting for transfers between devices: 0.01 us -> 19.6 us  [on_device(): up_grad = lax.psum(up_grad, 'rows').astype(F32)]
    unnamed x70 -> x168, local copies, waits for them, and re-layouts: 5.32 us -> 24.7 us
    ppermute x71 -> x47, starting transfers between devices: 50.2 us -> 35 us  [swap(): lax.ppermute(value, axis, [(i, i ^ bit) for i in range(lax.axis_size(axis...]
  transfers between devices with their start and end apart: 76 -> 52, of which waited for: 41 -> 25; matrix products, arithmetic and copies ran while one was open for 11% -> 10% of each run, Pallas kernels for 21% -> 13%
where the time goes in v4:
time: 401 us; the launch traced here: 395 us
  waiting for transfers between devices  196 us (49%)
  Pallas kernels  67.4 us (17%)
  starting transfers between devices  44.8 us (11%)
  local copies, waits for them, and re-layouts  31.3 us (8%)
  between operations  21.1 us (5%)
  other arithmetic  17.4 us (4%)
  matrix products  16.9 us (4%)
    ppermute x47, waiting for transfers between devices, swap(): lax.ppermute(value, axis, [(i, i ^ bit) for i in range(lax.axis_size(axis...  176 us
    ppermute x47, starting transfers between devices, swap(): lax.ppermute(value, axis, [(i, i ^ bit) for i in range(lax.axis_size(axis...  35 us
    unnamed x168, local copies, waits for them, and re-layouts  24.7 us
    psum x1, waiting for transfers between devices, on_device(): up_grad = lax.psum(up_grad, 'rows').astype(F32)  19.6 us
    dot_general x4, matrix products, tn(): lax.dot_general(a, b, (((0,), (0,)), ((), ())), preferred_element_type=F32)  16.7 us
    pallas_call x2, Pallas kernels, mlp(): return call(xa, xb, ga, gb, up, down)  16.6 us
    pallas_call x1, Pallas kernels, attend_back(): return call(last, spot, q, k, v, ng, dg, segc, segr, pack)  13.8 us
    ppermute x4, starting transfers between devices, shifted(): return lax.ppermute(pack, 'rows', pairs)  9.7 us
  transfers between devices with their start and end apart: 52, of which 25 were waited for; matrix products, arithmetic and copies ran while one was open for 10% of the time, Pallas kernels for 13%

profile of v4, /device:TPU:0, one launch (start us, length us, event | category | flops | bytes accessed | tf_op | source)
XLA Modules:
  0.0 394.5 jit_solution(15165694205280879384)
XLA Ops:
  10.8 2.6 collective-permute-start
  20.2 11.5 %collective-permute-done.xa_ref = bf16[384,1024]{1,0:T(8,128)(2,1)} collective-permute-done((bf16[384,1024]{1,0:T(8,128)(2,1)S(1)}, bf16[384,1024]{1,0:T(8,128)(2,1)}, u32[]{:S(2)}, u32[]{:S(2)}) %collective-permute-start) | collective-permute-done | bytes 786464 | tf_op jit(solution)/shard_map/ppermute | solution.py:553
  31.7 1.4 fusion.62.valid_ref
  33.1 1.7 copy-done.2
  34.8 3.0 project_qkv.2
  37.8 4.1 %project_qkv.3 = (bf16[1536,256]{1,0:T(8,128)(2,1)S(1)}, bf16[1536,256]{1,0:T(8,128)(2,1)S(1)}, bf16[1536,256]{1,0:T(8,128)(2,1)S(1)}, f32[80,256]{1,0:T(8,128)S(1)}) custom-call(s32[1]{0:T(128)} %slice.102.tail_ref, bf16[384,1024]{1,0:T(8,128)(2,1)} %collective-permute-done.xa_ref, ...), custom_call_target="tpu_custom_call", output_to_operand_aliasing={{0}: (7, {}), {1}: (8, {}), {2}: (9, {})} | custom-call | flops 4000000000 | tf_op jit(solution)/shard_map/project_qkv/pallas_call | solution.py:267
  42.0 3.7 collective-permute-start.4
  45.7 3.4 collective-permute-start.3
  49.1 6.2 %attend.1 = (f32[1536,256]{1,0:T(8,128)S(1)}, f32[1536,256]{1,0:T(8,128)S(1)}) custom-call(s32[5]{0:T(128)S(1)} %broadcast_add_fusion.2.last_ref.first_ref, s32[4]{0:T(128)S(1)} %iota_xor_fusion.spot_ref, bf16[1536,256]{1,0:T(8,128)(2,1)S(1)} %get-tuple-element.77.q_ref, bf16[1536,256]{1,0:T(8,128)(2,1)S(1)} %get-tuple-element.78.k_ref, ...), custom_call_target="tpu_custom_call" | custom-call | flops 7000000000 | tf_op jit(solution)/shard_map/attend/pallas_call | solution.py:322
  55.4 1.5 project.3
  58.8 1.5 project.2
  61.4 1.6 collective-permute-start.7
  63.5 18.4 %collective-permute-done.7.refs_5_ = bf16[384,1024]{1,0:T(8,128)(2,1)S(1)} collective-permute-done((bf16[384,1024]{1,0:T(8,128)(2,1)S(1)}, bf16[384,1024]{1,0:T(8,128)(2,1)S(1)}, u32[]{:S(2)}, u32[]{:S(2)}) %collective-permute-start.7) | collective-permute-done | bytes 786464 | tf_op jit(solution)/shard_map/ppermute | solution.py:553
  84.0 1.5 collective-permute-start.11
  85.5 13.2 %collective-permute-done.13.ga_ref = bf16[384,1024]{1,0:T(8,128)(2,1)S(1)} collective-permute-done((bf16[384,1024]{1,0:T(8,128)(2,1)S(1)}, bf16[384,1024]{1,0:T(8,128)(2,1)S(1)}, u32[]{:S(2)}, u32[]{:S(2)}) %collective-permute-start.13) | collective-permute-done | bytes 786464 | tf_op jit(solution)/shard_map/ppermute | solution.py:553
  98.7 16.0 %collective-permute-done.11.xa_ref = bf16[384,1024]{1,0:T(8,128)(2,1)S(1)} collective-permute-done((bf16[384,1024]{1,0:T(8,128)(2,1)S(1)}, bf16[384,1024]{1,0:T(8,128)(2,1)S(1)}, u32[]{:S(2)}, u32[]{:S(2)}) %collective-permute-start.11) | collective-permute-done | bytes 786464 | tf_op jit(solution)/shard_map/ppermute | solution.py:553
  114.8 2.3 collective-permute-done.12.xb_ref
  117.0 8.6 %mlp.3 = (bf16[768,1024]{1,0:T(8,128)(2,1)S(1)}, bf16[768,1024]{1,0:T(8,128)(2,1)S(1)}, bf16[384,1024]{1,0:T(8,128)(2,1)S(1)}, bf16[384,1024]{1,0:T(8,128)(2,1)S...) custom-call(bf16[384,1024]{1,0:T(8,128)(2,1)S(1)} %collective-permute-done.11.xa_ref, ...), custom_call_target="tpu_custom_call" | custom-call | flops 8999999488 | tf_op jit(solution)/shard_map/mlp/pallas_call | solution.py:386
  130.3 1.5 collective-permute-start.17
  132.5 8.0 %mlp.2 = (bf16[768,1024]{1,0:T(8,128)(2,1)S(1)}, bf16[768,1024]{1,0:T(8,128)(2,1)S(1)}, bf16[384,1024]{1,0:T(8,128)(2,1)S(1)}, bf16[384,1024]{1,0:T(8,128)(2,1)}...) custom-call(bf16[384,1024]{1,0:T(8,128)(2,1)S(1)} %get-tuple-element.88.xa_ref, ...), custom_call_target="tpu_custom_call" | custom-call | flops 8999999488 | tf_op jit(solution)/shard_map/mlp/pallas_call | solution.py:386
  150.0 2.3 add_convert_fusion.2
  152.3 1.4 copy-done.38
  154.9 2.9 norm_two_back.1
  159.0 1.5 collective-permute-start.20
  161.1 4.9 %fusion.41 = bf16[1024,1024]{1,0:T(8,128)(2,1)} fusion(bf16[384,1024]{1,0:T(8,128)(2,1)S(1)} %copy-done.23, bf16[384,1024]{1,0:T(8,128)(2,1)S(1)} %copy-done.15, bf16[384,1024]{1,0:T(8,128)(2,1)S(1)} %copy-done.28, bf16[384,1024]{1,0:T(8,128)(2,1)S(1)} %copy-done.4, bf16[768,1024]{1,0:T(8,128)(2,1)S(1)} %copy-done.68, bf16[768,1024]{1,0:T(8,128)(2,1)S(1)} %copy-done.72), kind=kOutput, calls=%fused_computation.41 | convolution fusion | flops 3241148416 | bytes 8388608 | tf_op jit(solution)/shard_map/dot_general | solution.py:30
  166.1 5.2 %fusion.46 = bf16[1024,1024]{1,0:T(8,128)(2,1)} fusion(bf16[768,1024]{1,0:T(8,128)(2,1)S(1)} %copy-done.66, bf16[768,1024]{1,0:T(8,128)(2,1)S(1)} %copy-done.70, bf16[384,1024]{1,0:T(8,128)(2,1)S(1)} %copy-done.21, bf16[384,1024]{1,0:T(8,128)(2,1)S(1)} %copy-done.19, bf16[384,1024]{1,0:T(8,128)(2,1)S(1)} %copy-done.25, bf16[384,1024]{1,0:T(8,128)(2,1)S(1)} %copy-done.17), kind=kOutput, calls=%fused_computation.42 | convolution fusion | flops 3241148416 | bytes 8388608 | tf_op jit(solution)/shard_map/dot_general | solution.py:30
  171.3 8.2 %collective-permute-done.20.ga_ref = bf16[384,1024]{1,0:T(8,128)(2,1)} collective-permute-done((bf16[384,1024]{1,0:T(8,128)(2,1)S(1)}, bf16[384,1024]{1,0:T(8,128)(2,1)}, u32[]{:S(2)}, u32[]{:S(2)}) %collective-permute-start.20) | collective-permute-done | bytes 786464 | tf_op jit(solution)/shard_map/ppermute | solution.py:553
  179.5 16.0 %collective-permute-done.18.refs_3_ = bf16[384,1024]{1,0:T(8,128)(2,1)} collective-permute-done((bf16[384,1024]{1,0:T(8,128)(2,1)}, bf16[384,1024]{1,0:T(8,128)(2,1)}, u32[]{:S(2)}, u32[]{:S(2)}) %collective-permute-start.18) | collective-permute-done | bytes 786464 | tf_op jit(solution)/shard_map/ppermute | solution.py:553
  195.5 1.4 copy-done.39
  198.1 2.8 finish.1
  205.9 3.0 heads_back.2
  209.0 3.2 heads_back.3
  212.2 1.3 collective-permute-start.24
  213.5 1.3 collective-permute-start.23
  214.8 2.8 fusion.56
  217.6 3.7 collective-permute-start.40
  221.3 13.8 %attend_back.1 = (bf16[1536,256]{1,0:T(8,128)(2,1)S(1)}, f32[1536,256]{1,0:T(8,128)S(1)}, f32[1536,256]{1,0:T(8,128)S(1)}) custom-call(s32[5]{0:T(128)S(1)} %broadcast_add_fusion.2.last_ref.first_ref, s32[4]{0:T(128)S(1)} %iota_xor_fusion.spot_ref, bf16[1536,256]{1,0:T(8,128)(2,1)S(1)} %copy-done.52, bf16[1536,256]{1,0:T(8,128)(2,1)S(1)} %copy-done.54, ...), custom_call_target="tpu_custom_call" | custom-call | flops 15000000512 | tf_op jit(solution)/shard_map/attend_back/pallas_call | solution.py:508
  235.2 2.4 mix.3
  237.7 2.6 mix.2
  240.3 3.8 fusion.51
  244.3 3.8 collective-permute-start.41
  249.8 8.2 %collective-permute-done.41 = bf16[64,1024]{1,0:T(8,128)(2,1)S(1)} collective-permute-done((bf16[64,1024]{1,0:T(8,128)(2,1)S(1)}, bf16[64,1024]{1,0:T(8,128)(2,1)S(1)}, u32[]{:S(2)}, u32[]{:S(2)}) %collective-permute-start.41) | collective-permute-done | bytes 131104 | tf_op jit(solution)/shard_map/ppermute | solution.py:553
  258.7 4.6 %collective-permute-done.34 = bf16[192,1024]{1,0:T(8,128)(2,1)S(1)} collective-permute-done((bf16[192,1024]{1,0:T(8,128)(2,1)S(1)}, bf16[192,1024]{1,0:T(8,128)(2,1)S(1)}, u32[]{:S(2)}, u32[]{:S(2)}) %collective-permute-start.34) | collective-permute-done | bytes 393248 | tf_op jit(solution)/shard_map/ppermute | solution.py:553
  263.8 1.3 collective-permute-start.43
  266.6 2.9 collective-permute-done.43
  270.3 16.3 %collective-permute-done.35 = bf16[96,1024]{1,0:T(8,128)(2,1)S(1)} collective-permute-done((bf16[96,1024]{1,0:T(8,128)(2,1)S(1)}, bf16[96,1024]{1,0:T(8,128)(2,1)S(1)}, u32[]{:S(2)}, u32[]{:S(2)}) %collective-permute-start.35) | collective-permute-done | bytes 196640 | tf_op jit(solution)/shard_map/ppermute | solution.py:553
  287.5 6.4 %collective-permute-done.44 = bf16[64,1024]{1,0:T(8,128)(2,1)S(1)} collective-permute-done((bf16[64,1024]{1,0:T(8,128)(2,1)S(1)}, bf16[64,1024]{1,0:T(8,128)(2,1)S(1)}, u32[]{:S(2)}, u32[]{:S(2)}) %collective-permute-start.44) | collective-permute-done | bytes 131104 | tf_op jit(solution)/shard_map/ppermute | solution.py:553
  294.2 1.3 collective-permute-start.37
  295.9 1.7 collective-permute-start.31
  297.6 1.5 collective-permute-done.37
  299.1 1.4 collective-permute-start.38
  300.5 13.4 %collective-permute-done.31 = bf16[48,1024]{1,0:T(8,128)(2,1)S(1)} collective-permute-done((bf16[48,1024]{1,0:T(8,128)(2,1)S(1)}, bf16[48,1024]{1,0:T(8,128)(2,1)S(1)}, u32[]{:S(2)}, u32[]{:S(2)}) %collective-permute-start.31) | collective-permute-done | bytes 98336 | tf_op jit(solution)/shard_map/ppermute | solution.py:553
  314.4 1.5 collective-permute-start.27
  316.0 10.0 %collective-permute-done.38 = bf16[96,1024]{1,0:T(8,128)(2,1)S(1)} collective-permute-done((bf16[96,1024]{1,0:T(8,128)(2,1)S(1)}, bf16[96,1024]{1,0:T(8,128)(2,1)S(1)}, u32[]{:S(2)}, u32[]{:S(2)}) %collective-permute-start.38) | collective-permute-done | bytes 196640 | tf_op jit(solution)/shard_map/ppermute | solution.py:553
  326.2 15.5 %collective-permute-done.32 = bf16[96,1024]{1,0:T(8,128)(2,1)S(1)} collective-permute-done((bf16[96,1024]{1,0:T(8,128)(2,1)S(1)}, bf16[96,1024]{1,0:T(8,128)(2,1)S(1)}, u32[]{:S(2)}, u32[]{:S(2)}) %collective-permute-start.32) | collective-permute-done | bytes 196640 | tf_op jit(solution)/shard_map/ppermute | solution.py:553
  341.9 2.4 norm_one_back.1
  347.0 19.6 %all-reduce.3.cloned.1.call-done = (bf16[1024,1024]{1,0:T(8,128)(2,1)}, bf16[1024,1024]{1,0:T(8,128)(2,1)}) async-done(((bf16[1024,1024]{1,0:T(8,128)(2,1)}, bf16[1024,1024]{1,0:T(8,128)(2,1)}), (bf16[1024,1024]{1,0:T(8,128)(2,1)}, bf16[1024,1024]{1,0:T(8,128)(2,1)})) %all-reduce.3.cloned.1.call-update) | async-done | bytes 4194320 | tf_op jit(solution)/shard_map/psum | solution.py:744
  366.6 4.2 %convert_element_type.247 = f32[1024,1024]{1,0:T(8,128)} convert(bf16[1024,1024]{1,0:T(8,128)(2,1)} %get-tuple-element.137) | non-fusion elementwise | flops 1048576 | bytes 6291456 | tf_op jit(solution)/shard_map/convert_element_type | solution.py:744
  370.8 2.5 convert_element_type.249
  373.3 1.4 collective-permute-start.48
  374.9 2.3 collective-permute-done.48
  378.0 3.0 collective-permute-done.49
  381.1 2.1 copy.74
  383.2 2.7 collective-permute-done.50
  (320 shorter events, 47.4 us)
Async XLA Ops:
  7.2 359.4 %all-reduce.3.cloned.1.call-start = ((), (), s32[]{:S(2)}) async-start(), calls=%async_computation | async-start | bytes 8388608 | tf_op jit(solution)/shard_map/psum | solution.py:744
  10.3 27.5 %copy-start.8 = (bf16[384,1024]{1,0:T(8,128)(2,1)}, bf16[384,1024]{1,0:T(8,128)(2,1)S(1)}, u32[]{:S(2)}) copy-start(bf16[384,1024]{1,0:T(8,128)(2,1)S(1)} %norm_one.1.xa_ref) | copy-start | bytes 2359300
  10.3 22.8 %collective-permute-start.2 = (bf16[384,1024]{1,0:T(8,128)(2,1)S(1)}, bf16[384,1024]{1,0:T(8,128)(2,1)S(1)}, u32[]{:S(2)}, u32[]{:S(2)}) collective-permute-start(bf16[384,1024]{1,0:T(8,128)(2,1)S(1)} %norm_one.1.xa_ref), channel_id=1, source_target_pairs={{0,1},{1,0},{2,3},{3,2},{4,5},{5,4},{6,7},{7,6},{8,9},{9,8},{10,11... | collective-permute-start | bytes 2359304 | tf_op jit(solution)/shard_map/ppermute | solution.py:553
  10.8 20.8 %collective-permute-start = (bf16[384,1024]{1,0:T(8,128)(2,1)S(1)}, bf16[384,1024]{1,0:T(8,128)(2,1)}, u32[]{:S(2)}, u32[]{:S(2)}) collective-permute-start(bf16[384,1024]{1,0:T(8,128)(2,1)S(1)} %norm_one.1.xa_ref), channel_id=1, source_target_pairs={{0,2},{1,3},{2,0},{3,1},{4,6},{5,7},{6,4},{7,5},{8,10},{9,11},{10,... | collective-permute-start | bytes 2359304 | tf_op jit(solution)/shard_map/ppermute | solution.py:553
  13.7 131.8 %copy-start.74 = (s32[1536]{0:T(1024)}, s32[1536]{0:T(1024)S(1)}, u32[]{:S(2)}) copy-start(s32[1536]{0:T(1024)S(1)} %broadcast_add_fusion) | copy-start | bytes 18436
  31.7 6.1 %collective-permute-start.1 = (bf16[384,1024]{1,0:T(8,128)(2,1)}, bf16[384,1024]{1,0:T(8,128)(2,1)S(1)}, u32[]{:S(2)}, u32[]{:S(2)}) collective-permute-start(bf16[384,1024]{1,0:T(8,128)(2,1)} %collective-permute-done.xa_ref), channel_id=1, source_target_pairs={{0,1},{1,0},{2,3},{3,2},{4,5},{5,4},{6,7},{7,6},{8,9},{9,8},{10,11... | collective-permute-start | bytes 2359304 | tf_op jit(solution)/shard_map/ppermute | solution.py:553
  42.0 13.3 %collective-permute-start.4 = (bf16[80,256]{1,0:T(8,128)(2,1)S(1)}, bf16[80,256]{1,0:T(8,128)(2,1)S(1)}, u32[]{:S(2)}, u32[]{:S(2)}) collective-permute-start(bf16[80,256]{1,0:T(8,128)(2,1)S(1)} %convert_element_type.195), channel_id=1, source_target_pairs={{0,8},{4,12},{8,16},{12,20},{16,24},{20,28},{1,9},{5,13},{9,17},{1... | collective-permute-start | bytes 122888 | tf_op jit(solution)/shard_map/ppermute | solution.py:617
  45.7 9.6 %collective-permute-start.3 = (bf16[80,256]{1,0:T(8,128)(2,1)S(1)}, bf16[80,256]{1,0:T(8,128)(2,1)S(1)}, u32[]{:S(2)}, u32[]{:S(2)}) collective-permute-start(bf16[80,256]{1,0:T(8,128)(2,1)S(1)} %convert_element_type.195), channel_id=1, source_target_pairs={{0,4},{4,8},{8,12},{12,16},{16,20},{20,24},{24,28},{1,5},{5,9},{9,... | collective-permute-start | bytes 122888 | tf_op jit(solution)/shard_map/ppermute | solution.py:617
  58.7 23.1 %copy-start.6 = (bf16[384,1024]{1,0:T(8,128)(2,1)S(1)}, bf16[384,1024]{1,0:T(8,128)(2,1)}, u32[]{:S(2)}) copy-start(bf16[384,1024]{1,0:T(8,128)(2,1)} %refs_0_.5) | copy-start | bytes 2359300
  58.7 23.1 %copy-start.33 = (f32[1024]{0:T(1024)S(1)}, f32[1024]{0:T(1024)}, u32[]{:S(2)}) copy-start(f32[1024]{0:T(1024)} %param.21) | copy-start | bytes 12292
  58.7 23.1 %copy-start.34 = (f32[1024]{0:T(1024)S(1)}, f32[1024]{0:T(1024)}, u32[]{:S(2)}) copy-start(f32[1024]{0:T(1024)} %param.20) | copy-start | bytes 12292
  58.7 2.4 collective-permute-start.6
  60.4 3.1 collective-permute-start.5
  61.4 20.5 %collective-permute-start.7 = (bf16[384,1024]{1,0:T(8,128)(2,1)S(1)}, bf16[384,1024]{1,0:T(8,128)(2,1)S(1)}, u32[]{:S(2)}, u32[]{:S(2)}) collective-permute-start(bf16[384,1024]{1,0:T(8,128)(2,1)S(1)} %add_convert_fusion.3), channel_id=1, source_target_pairs={{0,2},{1,3},{2,0},{3,1},{4,6},{5,7},{6,4},{7,5},{8,10},{9,11},{10,... | collective-permute-start | bytes 2359304 | tf_op jit(solution)/shard_map/ppermute | solution.py:553
  63.0 35.7 %collective-permute-start.13 = (bf16[384,1024]{1,0:T(8,128)(2,1)S(1)}, bf16[384,1024]{1,0:T(8,128)(2,1)S(1)}, u32[]{:S(2)}, u32[]{:S(2)}) collective-permute-start(bf16[384,1024]{1,0:T(8,128)(2,1)S(1)} %copy-done.4), channel_id=1, source_target_pairs={{0,2},{1,3},{2,0},{3,1},{4,6},{5,7},{6,4},{7,5},{8,10},{9,11},{10,... | collective-permute-start | bytes 2359304 | tf_op jit(solution)/shard_map/ppermute | solution.py:553
  81.9 35.2 %copy-start = (bf16[1024,1024]{1,0:T(8,128)(2,1)S(1)}, bf16[1024,1024]{1,0:T(8,128)(2,1)}, u32[]{:S(2)}) copy-start(bf16[1024,1024]{1,0:T(8,128)(2,1)} %up_ref.3) | copy-start | bytes 6291460
  81.9 35.2 %copy-start.1 = (bf16[1024,1024]{1,0:T(8,128)(2,1)S(1)}, bf16[1024,1024]{1,0:T(8,128)(2,1)}, u32[]{:S(2)}) copy-start(bf16[1024,1024]{1,0:T(8,128)(2,1)} %down_ref.3) | copy-start | bytes 6291460
  84.0 48.5 %copy-start.16 = (bf16[384,1024]{1,0:T(8,128)(2,1)}, bf16[384,1024]{1,0:T(8,128)(2,1)S(1)}, u32[]{:S(2)}) copy-start(bf16[384,1024]{1,0:T(8,128)(2,1)S(1)} %get-tuple-element.88.xa_ref) | copy-start | bytes 2359300
  84.0 30.8 %collective-permute-start.11 = (bf16[384,1024]{1,0:T(8,128)(2,1)S(1)}, bf16[384,1024]{1,0:T(8,128)(2,1)S(1)}, u32[]{:S(2)}, u32[]{:S(2)}) collective-permute-start(bf16[384,1024]{1,0:T(8,128)(2,1)S(1)} %get-tuple-element.88.xa_ref), channel_id=1, source_target_pairs={{0,2},{1,3},{2,0},{3,1},{4,6},{5,7},{6,4},{7,5},{8,10},{9,11},{10,... | collective-permute-start | bytes 2359304 | tf_op jit(solution)/shard_map/ppermute | solution.py:553
  98.7 26.9 %copy-start.14 = (bf16[384,1024]{1,0:T(8,128)(2,1)}, bf16[384,1024]{1,0:T(8,128)(2,1)S(1)}, u32[]{:S(2)}) copy-start(bf16[384,1024]{1,0:T(8,128)(2,1)S(1)} %collective-permute-done.13.ga_ref) | copy-start | bytes 2359300
  98.7 16.1 %collective-permute-start.14 = (bf16[384,1024]{1,0:T(8,128)(2,1)S(1)}, bf16[384,1024]{1,0:T(8,128)(2,1)S(1)}, u32[]{:S(2)}, u32[]{:S(2)}) collective-permute-start(bf16[384,1024]{1,0:T(8,128)(2,1)S(1)} %collective-permute-done.13.ga_ref), channel_id=1, source_target_pairs={{0,1},{1,0},{2,3},{3,2},{4,5},{5,4},{6,7},{7,6},{8,9},{9,8},{10,11... | collective-permute-start | bytes 2359304 | tf_op jit(solution)/shard_map/ppermute | solution.py:553
  114.7 2.3 collective-permute-start.12
  126.8 2.3 collective-permute-start.16
  126.9 4.9 %collective-permute-start.9 = (bf16[384,1024]{1,0:T(8,128)(2,1)S(1)}, bf16[384,1024]{1,0:T(8,128)(2,1)S(1)}, u32[]{:S(2)}, u32[]{:S(2)}) collective-permute-start(bf16[384,1024]{1,0:T(8,128)(2,1)S(1)} %copy-done.4), channel_id=1, source_target_pairs={{0,1},{1,0},{2,3},{3,2},{4,5},{5,4},{6,7},{7,6},{8,9},{9,8},{10,11... | collective-permute-start | bytes 2359304 | tf_op jit(solution)/shard_map/ppermute | solution.py:553
  127.3 5.1 %collective-permute-start.8 = (bf16[384,1024]{1,0:T(8,128)(2,1)S(1)}, bf16[384,1024]{1,0:T(8,128)(2,1)S(1)}, u32[]{:S(2)}, u32[]{:S(2)}) collective-permute-start(bf16[384,1024]{1,0:T(8,128)(2,1)S(1)} %get-tuple-element.88.xa_ref), channel_id=1, source_target_pairs={{0,1},{1,0},{2,3},{3,2},{4,5},{5,4},{6,7},{7,6},{8,9},{9,8},{10,11... | collective-permute-start | bytes 2359304 | tf_op jit(solution)/shard_map/ppermute | solution.py:553
  127.4 22.6 %collective-permute-start.15 = (bf16[384,1024]{1,0:T(8,128)(2,1)}, bf16[384,1024]{1,0:T(8,128)(2,1)}, u32[]{:S(2)}, u32[]{:S(2)}) collective-permute-start(bf16[384,1024]{1,0:T(8,128)(2,1)} %get-tuple-element.93), channel_id=1, source_target_pairs={{0,1},{1,0},{2,3},{3,2},{4,5},{5,4},{6,7},{7,6},{8,9},{9,8},{10,11... | collective-permute-start | bytes 2359304 | tf_op jit(solution)/shard_map/ppermute | solution.py:553
  130.3 22.1 %collective-permute-start.17 = (bf16[384,1024]{1,0:T(8,128)(2,1)}, bf16[384,1024]{1,0:T(8,128)(2,1)}, u32[]{:S(2)}, u32[]{:S(2)}) collective-permute-start(bf16[384,1024]{1,0:T(8,128)(2,1)} %add_convert_fusion.1), channel_id=1, source_target_pairs={{0,2},{1,3},{2,0},{3,1},{4,6},{5,7},{6,4},{7,5},{8,10},{9,11},{10,... | collective-permute-start | bytes 2359304 | tf_op jit(solution)/shard_map/ppermute | solution.py:553
  145.4 6.9 %collective-permute-start.19 = (bf16[384,1024]{1,0:T(8,128)(2,1)}, bf16[384,1024]{1,0:T(8,128)(2,1)}, u32[]{:S(2)}, u32[]{:S(2)}) collective-permute-start(bf16[384,1024]{1,0:T(8,128)(2,1)} %get-tuple-element.99), channel_id=1, source_target_pairs={{0,1},{1,0},{2,3},{3,2},{4,5},{5,4},{6,7},{7,6},{8,9},{9,8},{10,11... | collective-permute-start | bytes 2359304 | tf_op jit(solution)/shard_map/ppermute | solution.py:553
  149.6 29.9 %collective-permute-start.10 = (bf16[384,1024]{1,0:T(8,128)(2,1)}, bf16[384,1024]{1,0:T(8,128)(2,1)}, u32[]{:S(2)}, u32[]{:S(2)}) collective-permute-start(bf16[384,1024]{1,0:T(8,128)(2,1)} %copy-done.26), channel_id=1, source_target_pairs={{0,1},{1,0},{2,3},{3,2},{4,5},{5,4},{6,7},{7,6},{8,9},{9,8},{10,11... | collective-permute-start | bytes 2359304 | tf_op jit(solution)/shard_map/ppermute | solution.py:553
  159.0 20.5 %collective-permute-start.20 = (bf16[384,1024]{1,0:T(8,128)(2,1)S(1)}, bf16[384,1024]{1,0:T(8,128)(2,1)}, u32[]{:S(2)}, u32[]{:S(2)}) collective-permute-start(bf16[384,1024]{1,0:T(8,128)(2,1)S(1)} %get-tuple-element.101.ga_ref), channel_id=1, source_target_pairs={{0,2},{1,3},{2,0},{3,1},{4,6},{5,7},{6,4},{7,5},{8,10},{9,11},{10,... | collective-permute-start | bytes 2359304 | tf_op jit(solution)/shard_map/ppermute | solution.py:553
  160.5 35.0 %collective-permute-start.18 = (bf16[384,1024]{1,0:T(8,128)(2,1)}, bf16[384,1024]{1,0:T(8,128)(2,1)}, u32[]{:S(2)}, u32[]{:S(2)}) collective-permute-start(bf16[384,1024]{1,0:T(8,128)(2,1)} %add_convert_fusion.2), channel_id=1, source_target_pairs={{0,2},{1,3},{2,0},{3,1},{4,6},{5,7},{6,4},{7,5},{8,10},{9,11},{10,... | collective-permute-start | bytes 2359304 | tf_op jit(solution)/shard_map/ppermute | solution.py:553
  166.1 35.4 %collective-permute-start.22 = (bf16[384,1024]{1,0:T(8,128)(2,1)S(1)}, bf16[384,1024]{1,0:T(8,128)(2,1)}, u32[]{:S(2)}, u32[]{:S(2)}) collective-permute-start(bf16[384,1024]{1,0:T(8,128)(2,1)S(1)} %get-tuple-element.101.ga_ref), channel_id=1, source_target_pairs={{0,1},{1,0},{2,3},{3,2},{4,5},{5,4},{6,7},{7,6},{8,9},{9,8},{10,11... | collective-permute-start | bytes 2359304 | tf_op jit(solution)/shard_map/ppermute | solution.py:553
  179.5 29.4 %collective-permute-start.21 = (bf16[384,1024]{1,0:T(8,128)(2,1)}, bf16[384,1024]{1,0:T(8,128)(2,1)}, u32[]{:S(2)}, u32[]{:S(2)}) collective-permute-start(bf16[384,1024]{1,0:T(8,128)(2,1)} %collective-permute-done.20.ga_ref), channel_id=1, source_target_pairs={{0,1},{1,0},{2,3},{3,2},{4,5},{5,4},{6,7},{7,6},{8,9},{9,8},{10,11... | collective-permute-start | bytes 2359304 | tf_op jit(solution)/shard_map/ppermute | solution.py:553
  212.2 23.0 %collective-permute-start.24 = (bf16[80,256]{1,0:T(8,128)(2,1)S(1)}, bf16[80,256]{1,0:T(8,128)(2,1)S(1)}, u32[]{:S(2)}, u32[]{:S(2)}) collective-permute-start(bf16[80,256]{1,0:T(8,128)(2,1)S(1)} %convert_element_type.207), channel_id=1, source_target_pairs={{8,0},{12,4},{16,8},{20,12},{24,16},{28,20},{9,1},{13,5},{17,9},{2... | collective-permute-start | bytes 122888 | tf_op jit(solution)/shard_map/ppermute | solution.py:617
  213.5 21.7 %collective-permute-start.23 = (bf16[80,256]{1,0:T(8,128)(2,1)S(1)}, bf16[80,256]{1,0:T(8,128)(2,1)S(1)}, u32[]{:S(2)}, u32[]{:S(2)}) collective-permute-start(bf16[80,256]{1,0:T(8,128)(2,1)S(1)} %convert_element_type.207), channel_id=1, source_target_pairs={{4,0},{8,4},{12,8},{16,12},{20,16},{24,20},{28,24},{5,1},{9,5},{13... | collective-permute-start | bytes 122888 | tf_op jit(solution)/shard_map/ppermute | solution.py:617
  217.6 26.4 %collective-permute-start.40 = (bf16[128,1024]{1,0:T(8,128)(2,1)S(1)}, bf16[128,1024]{1,0:T(8,128)(2,1)S(1)}, u32[]{:S(2)}, u32[]{:S(2)}) collective-permute-start(bf16[128,1024]{1,0:T(8,128)(2,1)S(1)} %broadcast_select_fusion.8), channel_id=1, source_target_pairs={{0,8},{4,12},{8,0},{12,4},{16,24},{20,28},{24,16},{28,20},{1,9},{5... | collective-permute-start | bytes 786440 | tf_op jit(solution)/shard_map/ppermute | solution.py:553
  244.3 13.7 %collective-permute-start.41 = (bf16[64,1024]{1,0:T(8,128)(2,1)S(1)}, bf16[64,1024]{1,0:T(8,128)(2,1)S(1)}, u32[]{:S(2)}, u32[]{:S(2)}) collective-permute-start(bf16[64,1024]{1,0:T(8,128)(2,1)S(1)} %broadcast_select_fusion.17), channel_id=1, source_target_pairs={{0,16},{4,20},{8,24},{12,28},{16,0},{20,4},{24,8},{28,12},{1,17},{... | collective-permute-start | bytes 393224 | tf_op jit(solution)/shard_map/ppermute | solution.py:553
  248.1 10.6 %collective-permute-start.28 = (bf16[192,1024]{1,0:T(8,128)(2,1)S(1)}, bf16[192,1024]{1,0:T(8,128)(2,1)S(1)}, u32[]{:S(2)}, u32[]{:S(2)}) collective-permute-start(bf16[192,1024]{1,0:T(8,128)(2,1)S(1)} %get-tuple-element.141), channel_id=1, source_target_pairs={{0,4},{4,0},{8,12},{12,8},{16,20},{20,16},{24,28},{28,24},{1,5},{5... | collective-permute-start | bytes 1179656 | tf_op jit(solution)/shard_map/ppermute | solution.py:553
  248.8 14.5 %collective-permute-start.34 = (bf16[192,1024]{1,0:T(8,128)(2,1)S(1)}, bf16[192,1024]{1,0:T(8,128)(2,1)S(1)}, u32[]{:S(2)}, u32[]{:S(2)}) collective-permute-start(bf16[192,1024]{1,0:T(8,128)(2,1)S(1)} %get-tuple-element.142), channel_id=1, source_target_pairs={{0,8},{4,12},{8,0},{12,4},{16,24},{20,28},{24,16},{28,20},{1,9},{5... | collective-permute-start | bytes 1179656 | tf_op jit(solution)/shard_map/ppermute | solution.py:553
  249.2 64.8 %collective-permute-start.26 = (bf16[384,1024]{1,0:T(8,128)(2,1)S(1)}, bf16[384,1024]{1,0:T(8,128)(2,1)S(1)}, u32[]{:S(2)}, u32[]{:S(2)}) collective-permute-start(bf16[384,1024]{1,0:T(8,128)(2,1)S(1)} %get-tuple-element.118), channel_id=1, source_target_pairs={{0,1},{1,0},{2,3},{3,2},{4,5},{5,4},{6,7},{7,6},{8,9},{9,8},{10,11... | collective-permute-start | bytes 2359304 | tf_op jit(solution)/shard_map/ppermute | solution.py:553
  249.2 92.6 %collective-permute-start.25 = (bf16[384,1024]{1,0:T(8,128)(2,1)S(1)}, bf16[384,1024]{1,0:T(8,128)(2,1)S(1)}, u32[]{:S(2)}, u32[]{:S(2)}) collective-permute-start(bf16[384,1024]{1,0:T(8,128)(2,1)S(1)} %get-tuple-element.116), channel_id=1, source_target_pairs={{0,1},{1,0},{2,3},{3,2},{4,5},{5,4},{6,7},{7,6},{8,9},{9,8},{10,11... | collective-permute-start | bytes 2359304 | tf_op jit(solution)/shard_map/ppermute | solution.py:553
  258.0 5.7 %collective-permute-start.42 = (bf16[32,1024]{1,0:T(8,128)(2,1)S(1)}, bf16[32,1024]{1,0:T(8,128)(2,1)S(1)}, u32[]{:S(2)}, u32[]{:S(2)}) collective-permute-start(bf16[32,1024]{1,0:T(8,128)(2,1)S(1)} %broadcast_select_fusion.26), channel_id=1, source_target_pairs={{0,4},{4,0},{8,12},{12,8},{16,20},{20,16},{24,28},{28,24},{1,5},{5... | collective-permute-start | bytes 196616 | tf_op jit(solution)/shard_map/ppermute | solution.py:553
  263.8 5.7 %collective-permute-start.43 = (bf16[32,1024]{1,0:T(8,128)(2,1)S(1)}, bf16[32,1024]{1,0:T(8,128)(2,1)S(1)}, u32[]{:S(2)}, u32[]{:S(2)}) collective-permute-start(bf16[32,1024]{1,0:T(8,128)(2,1)S(1)} %add_convert_fusion.12), channel_id=1, source_target_pairs={{0,4},{4,0},{8,12},{12,8},{16,20},{20,16},{24,28},{28,24},{1,5},{5... | collective-permute-start | bytes 196616 | tf_op jit(solution)/shard_map/ppermute | solution.py:553
  265.1 21.6 %collective-permute-start.35 = (bf16[96,1024]{1,0:T(8,128)(2,1)S(1)}, bf16[96,1024]{1,0:T(8,128)(2,1)S(1)}, u32[]{:S(2)}, u32[]{:S(2)}) collective-permute-start(bf16[96,1024]{1,0:T(8,128)(2,1)S(1)} %broadcast_select_fusion.11), channel_id=1, source_target_pairs={{0,16},{4,20},{8,24},{12,28},{16,0},{20,4},{24,8},{28,12},{1,17},{... | collective-permute-start | bytes 589832 | tf_op jit(solution)/shard_map/ppermute | solution.py:553
  265.6 21.7 %collective-permute-start.29 = (bf16[96,1024]{1,0:T(8,128)(2,1)S(1)}, bf16[96,1024]{1,0:T(8,128)(2,1)S(1)}, u32[]{:S(2)}, u32[]{:S(2)}) collective-permute-start(bf16[96,1024]{1,0:T(8,128)(2,1)S(1)} %broadcast_select_fusion.14), channel_id=1, source_target_pairs={{0,8},{4,12},{8,0},{12,4},{16,24},{20,28},{24,16},{28,20},{1,9},{5... | collective-permute-start | bytes 589832 | tf_op jit(solution)/shard_map/ppermute | solution.py:553
  269.5 24.4 %collective-permute-start.44 = (bf16[64,1024]{1,0:T(8,128)(2,1)S(1)}, bf16[64,1024]{1,0:T(8,128)(2,1)S(1)}, u32[]{:S(2)}, u32[]{:S(2)}) collective-permute-start(bf16[64,1024]{1,0:T(8,128)(2,1)S(1)} %pad_maximum_fusion.6), channel_id=1, source_target_pairs={{0,16},{4,20},{8,24},{12,28},{16,0},{20,4},{24,8},{28,12},{1,17},{... | collective-permute-start | bytes 393224 | tf_op jit(solution)/shard_map/ppermute | solution.py:553
  286.8 7.4 %collective-permute-start.36 = (bf16[48,1024]{1,0:T(8,128)(2,1)S(1)}, bf16[48,1024]{1,0:T(8,128)(2,1)S(1)}, u32[]{:S(2)}, u32[]{:S(2)}) collective-permute-start(bf16[48,1024]{1,0:T(8,128)(2,1)S(1)} %broadcast_select_fusion.20), channel_id=1, source_target_pairs={{0,4},{4,0},{8,12},{12,8},{16,20},{20,16},{24,28},{28,24},{1,5},{5... | collective-permute-start | bytes 294920 | tf_op jit(solution)/shard_map/ppermute | solution.py:553
  287.4 8.4 %collective-permute-start.30 = (bf16[48,1024]{1,0:T(8,128)(2,1)S(1)}, bf16[48,1024]{1,0:T(8,128)(2,1)S(1)}, u32[]{:S(2)}, u32[]{:S(2)}) collective-permute-start(bf16[48,1024]{1,0:T(8,128)(2,1)S(1)} %broadcast_select_fusion.23), channel_id=1, source_target_pairs={{0,16},{4,20},{8,24},{12,28},{16,0},{20,4},{24,8},{28,12},{1,17},{... | collective-permute-start | bytes 294920 | tf_op jit(solution)/shard_map/ppermute | solution.py:553
  294.0 21.8 %collective-permute-start.45 = (bf16[128,1024]{1,0:T(8,128)(2,1)S(1)}, bf16[128,1024]{1,0:T(8,128)(2,1)S(1)}, u32[]{:S(2)}, u32[]{:S(2)}) collective-permute-start(bf16[128,1024]{1,0:T(8,128)(2,1)S(1)} %pad_maximum_fusion.3), channel_id=1, source_target_pairs={{0,8},{4,12},{8,0},{12,4},{16,24},{20,28},{24,16},{28,20},{1,9},{5... | collective-permute-start | bytes 786440 | tf_op jit(solution)/shard_map/ppermute | solution.py:553
  294.2 4.9 %collective-permute-start.37 = (bf16[48,1024]{1,0:T(8,128)(2,1)S(1)}, bf16[48,1024]{1,0:T(8,128)(2,1)S(1)}, u32[]{:S(2)}, u32[]{:S(2)}) collective-permute-start(bf16[48,1024]{1,0:T(8,128)(2,1)S(1)} %add_convert_fusion.10), channel_id=1, source_target_pairs={{0,4},{4,0},{8,12},{12,8},{16,20},{20,16},{24,28},{28,24},{1,5},{5... | collective-permute-start | bytes 294920 | tf_op jit(solution)/shard_map/ppermute | solution.py:553
  295.9 18.0 %collective-permute-start.31 = (bf16[48,1024]{1,0:T(8,128)(2,1)S(1)}, bf16[48,1024]{1,0:T(8,128)(2,1)S(1)}, u32[]{:S(2)}, u32[]{:S(2)}) collective-permute-start(bf16[48,1024]{1,0:T(8,128)(2,1)S(1)} %add_convert_fusion.11), channel_id=1, source_target_pairs={{0,16},{4,20},{8,24},{12,28},{16,0},{20,4},{24,8},{28,12},{1,17},{... | collective-permute-start | bytes 294920 | tf_op jit(solution)/shard_map/ppermute | solution.py:553
  299.1 26.9 %collective-permute-start.38 = (bf16[96,1024]{1,0:T(8,128)(2,1)S(1)}, bf16[96,1024]{1,0:T(8,128)(2,1)S(1)}, u32[]{:S(2)}, u32[]{:S(2)}) collective-permute-start(bf16[96,1024]{1,0:T(8,128)(2,1)S(1)} %pad_maximum_fusion.5), channel_id=1, source_target_pairs={{0,16},{4,20},{8,24},{12,28},{16,0},{20,4},{24,8},{28,12},{1,17},{... | collective-permute-start | bytes 589832 | tf_op jit(solution)/shard_map/ppermute | solution.py:553
  313.9 27.9 %copy-start.7 = (bf16[384,1024]{1,0:T(8,128)(2,1)S(1)}, bf16[384,1024]{1,0:T(8,128)(2,1)}, u32[]{:S(2)}) copy-start(bf16[384,1024]{1,0:T(8,128)(2,1)} %refs_0_.5) | copy-start | bytes 2359300
  313.9 27.9 %copy-start.36 = (f32[1024]{0:T(1024)S(1)}, f32[1024]{0:T(1024)}, u32[]{:S(2)}) copy-start(f32[1024]{0:T(1024)} %param.18) | copy-start | bytes 12292
  314.0 27.9 %copy-start.62 = (f32[384,1024]{1,0:T(8,128)S(1)}, f32[384,1024]{1,0:T(8,128)}, u32[]{:S(2)}) copy-start(f32[384,1024]{1,0:T(8,128)} %copy-done.61) | copy-start | bytes 4718596
  314.0 27.7 %collective-permute-start.32 = (bf16[96,1024]{1,0:T(8,128)(2,1)S(1)}, bf16[96,1024]{1,0:T(8,128)(2,1)S(1)}, u32[]{:S(2)}, u32[]{:S(2)}) collective-permute-start(bf16[96,1024]{1,0:T(8,128)(2,1)S(1)} %pad_maximum_fusion.4), channel_id=1, source_target_pairs={{0,8},{4,12},{8,0},{12,4},{16,24},{20,28},{24,16},{28,20},{1,9},{5... | collective-permute-start | bytes 589832 | tf_op jit(solution)/shard_map/ppermute | solution.py:553
  314.4 27.4 %collective-permute-start.27 = (bf16[384,1024]{1,0:T(8,128)(2,1)S(1)}, bf16[384,1024]{1,0:T(8,128)(2,1)S(1)}, u32[]{:S(2)}, u32[]{:S(2)}) collective-permute-start(bf16[384,1024]{1,0:T(8,128)(2,1)S(1)} %add_convert_fusion), channel_id=1, source_target_pairs={{0,2},{1,3},{2,0},{3,1},{4,6},{5,7},{6,4},{7,5},{8,10},{9,11},{10,... | collective-permute-start | bytes 2359304 | tf_op jit(solution)/shard_map/ppermute | solution.py:553
  326.1 48.6 %collective-permute-start.39 = (bf16[192,1024]{1,0:T(8,128)(2,1)S(1)}, bf16[192,1024]{1,0:T(8,128)(2,1)S(1)}, u32[]{:S(2)}, u32[]{:S(2)}) collective-permute-start(bf16[192,1024]{1,0:T(8,128)(2,1)S(1)} %pad_maximum_fusion.2), channel_id=1, source_target_pairs={{0,8},{4,12},{8,0},{12,4},{16,24},{20,28},{24,16},{28,20},{1,9},{5... | collective-permute-start | bytes 1179656 | tf_op jit(solution)/shard_map/ppermute | solution.py:553
  344.2 1.3 collective-permute-start.46
  344.4 33.4 %collective-permute-start.33 = (bf16[192,1024]{1,0:T(8,128)(2,1)S(1)}, bf16[192,1024]{1,0:T(8,128)(2,1)S(1)}, u32[]{:S(2)}, u32[]{:S(2)}) collective-permute-start(bf16[192,1024]{1,0:T(8,128)(2,1)S(1)} %pad_maximum_fusion.1), channel_id=1, source_target_pairs={{0,4},{4,0},{8,12},{12,8},{16,20},{20,16},{24,28},{28,24},{1,5},{5... | collective-permute-start | bytes 1179656 | tf_op jit(solution)/shard_map/ppermute | solution.py:553
  345.5 27.8 %collective-permute-start.47 = (f32[4224]{0:T(1024)S(1)}, f32[4224]{0:T(1024)S(1)}, u32[]{:S(2)}, u32[]{:S(2)}) collective-permute-start(f32[4224]{0:T(1024)S(1)} %add.223), channel_id=1, source_target_pairs={{0,2},{1,3},{2,0},{3,1},{4,6},{5,7},{6,4},{7,5},{8,10},{9,11},{10,... | collective-permute-start | bytes 50696 | tf_op jit(solution)/shard_map/ppermute | solution.py:553
  373.3 3.8 collective-permute-start.48
  377.2 3.8 collective-permute-start.49
  381.0 4.9 %collective-permute-start.50 = (f32[4224]{0:T(1024)S(1)}, f32[4224]{0:T(1024)S(1)}, u32[]{:S(2)}, u32[]{:S(2)}) collective-permute-start(f32[4224]{0:T(1024)S(1)} %add.226), channel_id=1, source_target_pairs={{0,16},{4,20},{8,24},{12,28},{16,0},{20,4},{24,8},{28,12},{1,17},{... | collective-permute-start | bytes 50696 | tf_op jit(solution)/shard_map/ppermute | solution.py:553
  (71 other events, 387.3 us)
Sparse Core Ops, SparseCore 0:
  171.4 195.1 all-reduce.2
